TPU v7x, 512 devices: a whole 4x8x8 slice. The times are simulated.
512 devices in a mesh: tile: 32 (over x, z), row: 16 (over y, core).
Axes of the slice: x: 4, y: 8, z: 8, core: 2. Of those that a mesh axis runs over, the one named last changes fastest.
Arguments:
- voltage: float32 [32, 16, 1, 64, 128], P('tile', 'row'), may hold values from -6 to 6
- history: bfloat16 [32, 16, 32, 64, 128], P('tile', 'row'), may hold values from -6 to 6
- far_blocks: bfloat16 [32, 16, 32, 128, 128], P('tile', 'row'), may hold values from -0.09375 to 0.09375
- far_target: int32 [32, 16, 32, 1], P('tile', 'row'), may hold values from 0 to 31; in each aligned block of 32 rows (0 to 31, 32 to 63, ..., all dimensions but the last counted through in order) at most 2 rows name the same one
- far_delay: int32 [32, 16, 32], P('tile', 'row'), may hold values from 1 to 32
- near_blocks: bfloat16 [32, 16, 3, 128, 128], P('tile', 'row'), may hold values from -0.15625 to 0.15625
- near_link: int32 [32, 16, 2], P('tile', 'row'), may hold values 0 or 1
- jacobi_blocks: bfloat16 [32, 16, 128, 128], P('tile', 'row'), may hold values from -0.21875 to 0.21875
Outputs:
- currents: float32 [32, 16, 1, 64, 128], P('tile', 'row')
Inputs may be any that keep to these rules, and one draw needn't show every extreme that they name: `far_target`: among the 32 entries of one tile at most 2 name the same target, and some tile has exactly 2 naming one target.
All inputs are finite; a program needn't handle non-finite values. No bound on the sum of `near_link` on one device may be relied on, other than what follows from the above.
Results may differ from a plain program's by a relative error of at most 0.0003.
Values sent between devices are 32-bit elements; how exact they have to be, the bound alone decides.
No kernel may reach another device: no remote copies, remote signals or barrier semaphores. Data moves between devices by JAX's collectives and lax.ppermute only.
A program may use at most 64 MiB of HBM per device.

v0:
```python
import jax
import jax.numpy as jnp
from jax import lax
from jax.sharding import PartitionSpec as P

ITERS = 5


PRECISE = lax.Precision.HIGHEST


def padded_2(array, sides, width):
    for axis, dim in sides:
        size, length = (lax.axis_size(axis), array.shape[dim])
        up = [(i, (i + 1) % size) for i in range(size - 1)]
        down = [(j, i) for i, j in up]
        last = lax.slice_in_dim(array, length - width, length, axis=dim)
        first = lax.slice_in_dim(array, 0, width, axis=dim)
        before = lax.ppermute(last, axis, up)
        after = lax.ppermute(first, axis, down)
        array = jnp.concatenate([before, array, after], axis=dim)
    return array


def near_apply(field, near_f32, link_gain):
    padded = padded_2(field[None], (("row", 0),), 1)
    result = field + jnp.dot(field, near_f32[1], precision=PRECISE)
    result = result + link_gain[0] * jnp.dot(padded[0], near_f32[0], precision=PRECISE)
    result = result + link_gain[1] * jnp.dot(padded[2], near_f32[2], precision=PRECISE)
    return result


def jacobi_apply(field, jacobi_f32):
    return field + jnp.dot(field, jacobi_f32, precision=PRECISE)


def givens_solve(hessen, start_norm, iterations):
    matrix = [[hessen[i][k] for k in range(iterations)] for i in range(iterations + 1)]
    target = [start_norm] + [jnp.zeros_like(start_norm) for k in range(iterations)]
    for j in range(iterations):
        diag_val = matrix[j][j]
        below_val = matrix[j + 1][j]
        radius = jnp.sqrt(diag_val * diag_val + below_val * below_val)
        cosine = diag_val / radius
        sine_val = below_val / radius
        for k in range(j, iterations):
            upper_val = matrix[j][k]
            lower_val = matrix[j + 1][k]
            matrix[j][k] = cosine * upper_val + sine_val * lower_val
            matrix[j + 1][k] = cosine * lower_val - sine_val * upper_val
        target[j + 1] = -sine_val * target[j]
        target[j] = cosine * target[j]
    coeffs = [None] * iterations
    for j in reversed(range(iterations)):
        partial_val = target[j]
        for k in range(j + 1, iterations):
            partial_val = partial_val - matrix[j][k] * coeffs[k]
        coeffs[j] = partial_val / matrix[j][j]
    return coeffs


def krylov_solve(right_side, near_f32, link_gain, jacobi_f32):
    initial = jacobi_apply(right_side, jacobi_f32)
    start_sq = lax.psum(jnp.sum(initial * initial, axis=1), ("tile", "row"))
    start_norm = jnp.sqrt(start_sq)
    basis = [initial / start_norm[:, None]]
    zero_row = jnp.zeros_like(start_norm)
    hessen = [[zero_row for k in range(ITERS)] for i in range(ITERS + 1)]
    for j in range(ITERS):
        candidate = jacobi_apply(near_apply(basis[j], near_f32, link_gain), jacobi_f32)
        local_dots = jnp.stack([jnp.sum(v * candidate, axis=1) for v in basis])
        projections = lax.psum(local_dots, ("tile", "row"))
        for i in range(j + 1):
            candidate = candidate - projections[i][:, None] * basis[i]
        new_sq = lax.psum(jnp.sum(candidate * candidate, axis=1), ("tile", "row"))
        new_norm = jnp.sqrt(new_sq)
        for i in range(j + 1):
            hessen[i][j] = projections[i]
        hessen[j + 1][j] = new_norm
        basis.append(candidate / new_norm[:, None])
    coeffs = givens_solve(hessen, start_norm, ITERS)
    result = coeffs[0][:, None] * basis[0]
    for j in range(1, ITERS):
        result = result + coeffs[j][:, None] * basis[j]
    return result


def per_device(
    voltage, history, far_blocks, far_target, far_delay, near_blocks, near_link, jacobi_blocks
):
    voltage = voltage[0, 0]
    history = history[0, 0]
    far_blocks = far_blocks[0, 0]
    targets = far_target[0, 0, :, 0]
    delays = far_delay[0, 0]
    near_f32 = near_blocks[0, 0].astype(jnp.float32)
    link_gain = near_link[0, 0].astype(jnp.float32)
    jacobi_f32 = jacobi_blocks[0, 0].astype(jnp.float32)
    tile_count = lax.axis_size("tile")
    entries = far_blocks.shape[0]
    capacity = max(2, entries // tile_count + 1)
    scenarios = voltage.shape[1]
    segments = voltage.shape[2]
    ordinal = jnp.arange(entries, dtype=jnp.int32)
    earlier = (ordinal[:, None] > ordinal[None, :]) & (targets[:, None] == targets[None, :])
    ranking = jnp.sum(earlier.astype(jnp.int32), axis=1)
    destination = targets * capacity + ranking
    placing = (
        jnp.arange(tile_count * capacity, dtype=jnp.int32)[:, None] == destination[None, :]
    ).astype(jnp.float32)
    currents = []
    pieces = [c.astype(jnp.bfloat16)[None] for c in reversed(currents)]
    stacked = jnp.concatenate(pieces + [history], axis=0)
    chosen = jnp.take(stacked, delays - 1, axis=0)
    products = jnp.einsum("lcs,lst->lct", chosen, far_blocks, preferred_element_type=jnp.float32)
    flattened = products.reshape(entries, scenarios * segments)
    bucket = jnp.dot(placing, flattened, precision=PRECISE).reshape(
        tile_count, capacity, scenarios, segments
    )
    received = lax.all_to_all(bucket, "tile", split_axis=0, concat_axis=0, tiled=True)
    far_field = jnp.sum(received, axis=(0, 1))
    right_side = voltage[0] - far_field
    currents.append(krylov_solve(right_side, near_f32, link_gain, jacobi_f32))
    return jnp.stack(currents)[None, None]


def solution(mesh):
    return jax.shard_map(
        per_device,
        mesh=mesh,
        in_specs=(
            P("tile", "row", None, None, None),
            P("tile", "row", None, None, None),
            P("tile", "row", None, None, None),
            P("tile", "row", None, None),
            P("tile", "row", None),
            P("tile", "row", None, None, None),
            P("tile", "row", None),
            P("tile", "row", None, None),
        ),
        out_specs=P("tile", "row", None, None, None),
        check_vma=False,
    )
```

profile of v0, /device:TPU:1, one launch (start us, length us, event | category | flops | bytes accessed | tf_op | source)
XLA Modules:
  0.0 1178.2 jit_solution(18012329410993611256)
XLA Ops:
  6.9 2.6 copy.13
  9.4 13.8 %all-to-all-start = ((f32[32,2,64,128]{3,2,1,0:T(8,128)}), f32[32,2,64,128]{3,2,1,0:T(8,128)S(1)}, u32[]{:S(2)}, u32[]{:S(2)}) async-start(f32[32,2,64,128]{3,2,1,0:T(8,128)} %copy.13), calls=%async_computation | async-start | bytes 4194304 | tf_op jit(solution)/shard_map/all_to_all | solution.py:120
  23.9 48.2 %all-to-all-done = f32[32,2,64,128]{3,2,1,0:T(8,128)S(1)} async-done(((f32[32,2,64,128]{3,2,1,0:T(8,128)}), f32[32,2,64,128]{3,2,1,0:T(8,128)S(1)}, u32[]{:S(2)}, u32[]{:S(2)}) %all-to-all-start) | async-done | bytes 2097184 | tf_op jit(solution)/shard_map/all_to_all | solution.py:120
  72.6 98.6 %psum.77 = f32[64]{0:T(128)S(1)} all-reduce(f32[64]{0:T(128)S(1)} %get-tuple-element.55), channel_id=1, replica_groups=mesh['tile'=32,'row'=16] {'tile','row'}, use_global_device_ids=true, to_apply=%region_3.4 | all-reduce | flops 64 | bytes 512 | tf_op jit(solution)/shard_map/psum | solution.py:64
  171.3 3.0 collective-permute-start
  177.2 2.3 collective-permute-done.1
  180.5 95.9 %psum.78 = f32[64]{0:T(128)S(1)} all-reduce(f32[64]{0:T(128)S(1)} %get-tuple-element.57), channel_id=1, replica_groups=mesh['tile'=32,'row'=16] {'tile','row'}, use_global_device_ids=true, to_apply=%region_5.6 | all-reduce | flops 64 | bytes 512 | tf_op jit(solution)/shard_map/psum | solution.py:72
  276.6 95.5 %psum.79 = f32[64]{0:T(128)S(1)} all-reduce(f32[64]{0:T(128)S(1)} %multiply_reduce_fusion.18), channel_id=1, replica_groups=mesh['tile'=32,'row'=16] {'tile','row'}, use_global_device_ids=true, to_apply=%region_7.8 | all-reduce | flops 64 | bytes 512 | tf_op jit(solution)/shard_map/psum | solution.py:75
  372.3 2.7 collective-permute-start.2
  377.9 2.5 collective-permute-done.3
  381.5 95.9 %psum.80 = f32[2,64]{1,0:T(2,128)S(1)} all-reduce(f32[2,64]{1,0:T(2,128)S(1)} %pad_maximum_fusion.2), channel_id=1, replica_groups=mesh['tile'=32,'row'=16] {'tile','row'}, use_global_device_ids=true, to_apply=%region_10.11 | all-reduce | flops 128 | bytes 1024 | tf_op jit(solution)/shard_map/psum | solution.py:72
  477.7 95.3 %psum.81 = f32[64]{0:T(128)S(1)} all-reduce(f32[64]{0:T(128)S(1)} %get-tuple-element.34), channel_id=1, replica_groups=mesh['tile'=32,'row'=16] {'tile','row'}, use_global_device_ids=true, to_apply=%region_12.13 | all-reduce | flops 64 | bytes 512 | tf_op jit(solution)/shard_map/psum | solution.py:75
  573.0 3.3 collective-permute-start.4
  579.3 2.5 collective-permute-done.5
  583.0 96.0 %psum.82 = f32[3,64]{1,0:T(4,128)S(1)} all-reduce(f32[3,64]{1,0:T(4,128)S(1)} %pad_maximum_fusion), channel_id=1, replica_groups=mesh['tile'=32,'row'=16] {'tile','row'}, use_global_device_ids=true, to_apply=%region_16.17 | all-reduce | flops 192 | bytes 1536 | tf_op jit(solution)/shard_map/psum | solution.py:72
  679.2 95.1 %psum.83 = f32[64]{0:T(128)S(1)} all-reduce(f32[64]{0:T(128)S(1)} %get-tuple-element.32), channel_id=1, replica_groups=mesh['tile'=32,'row'=16] {'tile','row'}, use_global_device_ids=true, to_apply=%region_18.19 | all-reduce | flops 64 | bytes 512 | tf_op jit(solution)/shard_map/psum | solution.py:75
  774.6 3.1 collective-permute-start.6
  780.7 2.3 collective-permute-done.7
  784.1 96.8 %psum.84 = f32[4,64]{1,0:T(4,128)S(1)} all-reduce(f32[4,64]{1,0:T(4,128)S(1)} %pad_maximum_fusion.1), channel_id=1, replica_groups=mesh['tile'=32,'row'=16] {'tile','row'}, use_global_device_ids=true, to_apply=%region_23.24 | all-reduce | flops 256 | bytes 2048 | tf_op jit(solution)/shard_map/psum | solution.py:72
  881.1 94.5 %psum.85 = f32[64]{0:T(128)S(1)} all-reduce(f32[64]{0:T(128)S(1)} %get-tuple-element.30), channel_id=1, replica_groups=mesh['tile'=32,'row'=16] {'tile','row'}, use_global_device_ids=true, to_apply=%region_25.26 | all-reduce | flops 64 | bytes 512 | tf_op jit(solution)/shard_map/psum | solution.py:75
  975.7 3.3 collective-permute-start.8
  981.9 2.5 collective-permute-done.9
  985.6 96.2 %psum.86 = f32[5,64]{1,0:T(8,128)S(1)} all-reduce(f32[5,64]{1,0:T(8,128)S(1)} %stack.75), channel_id=1, replica_groups=mesh['tile'=32,'row'=16] {'tile','row'}, use_global_device_ids=true, to_apply=%region_31.32 | all-reduce | flops 320 | bytes 2560 | tf_op jit(solution)/shard_map/psum | solution.py:72
  1082.1 95.2 %psum.87 = f32[64]{0:T(128)S(1)} all-reduce(f32[64]{0:T(128)S(1)} %multiply_reduce_fusion), channel_id=1, replica_groups=mesh['tile'=32,'row'=16] {'tile','row'}, use_global_device_ids=true, to_apply=%region_33.34 | all-reduce | flops 64 | bytes 512 | tf_op jit(solution)/shard_map/psum | solution.py:75
  (80 shorter events, 30.6 us)
Async XLA Ops:
  0.0 4.7 copy-start
  9.4 13.9 %copy-start.4 = (s32[1,1,2]{2,1,0:T(1,128)S(1)}, s32[1,1,2]{2,1,0:T(1,128)}, u32[]{:S(2)}) copy-start(s32[1,1,2]{2,1,0:T(1,128)} %param.14) | copy-start | bytes 28
  9.4 62.7 %all-to-all-start = ((f32[32,2,64,128]{3,2,1,0:T(8,128)}), f32[32,2,64,128]{3,2,1,0:T(8,128)S(1)}, u32[]{:S(2)}, u32[]{:S(2)}) async-start(f32[32,2,64,128]{3,2,1,0:T(8,128)} %copy.13), calls=%async_computation | async-start | bytes 4194304 | tf_op jit(solution)/shard_map/all_to_all | solution.py:120
  23.3 49.0 %copy-start.2 = (f32[1,1,1,64,128]{4,3,2,1,0:T(8,128)S(1)}, f32[1,1,1,64,128]{4,3,2,1,0:T(8,128)}, u32[]{:S(2)}) copy-start(f32[1,1,1,64,128]{4,3,2,1,0:T(8,128)} %param.8) | copy-start | bytes 98308
  23.3 49.0 %copy-start.3 = (bf16[1,1,128,128]{3,2,1,0:T(8,128)(2,1)S(1)}, bf16[1,1,128,128]{3,2,1,0:T(8,128)(2,1)}, u32[]{:S(2)}) copy-start(bf16[1,1,128,128]{3,2,1,0:T(8,128)(2,1)} %param.15) | copy-start | bytes 98308
  23.3 152.8 %copy-start.1 = (bf16[1,1,3,128,128]{4,3,2,1,0:T(8,128)(2,1)S(1)}, bf16[1,1,3,128,128]{4,3,2,1,0:T(8,128)(2,1)}, u32[]{:S(2)}) copy-start(bf16[1,1,3,128,128]{4,3,2,1,0:T(8,128)(2,1)} %param.13) | copy-start | bytes 294916
  171.3 5.1 collective-permute-start
  174.2 5.2 collective-permute-start.1
  372.3 4.8 collective-permute-start.2
  375.2 5.2 collective-permute-start.3
  573.0 5.5 collective-permute-start.4
  576.6 5.2 collective-permute-start.5
  774.6 5.2 collective-permute-start.6
  777.7 5.2 collective-permute-start.7
  975.7 5.4 collective-permute-start.8
  979.2 5.2 collective-permute-start.9
where the time goes:
time: 1180 us
  blocking collectives  1060 us (90%)
  waiting for transfers between devices  60.3 us (5%)
  starting transfers between devices  38.9 us (3%)
  matrix products  12.9 us (1%)
    psum x5, blocking collectives, krylov_solve(): projections = lax.psum(local_dots, ('tile', 'row'))  481 us
    psum x5, blocking collectives, krylov_solve(): new_sq = lax.psum(jnp.sum(candidate * candidate, axis=1), ('tile', 'row'))  476 us
    psum x1, blocking collectives, krylov_solve(): start_sq = lax.psum(jnp.sum(initial * initial, axis=1), ('tile', 'row'))  98.6 us
    all_to_all x1, waiting for transfers between devices, per_device(): lax.all_to_all(bucket, 'tile', split_axis=0, concat_axis=0, tiled=True)  48.2 us
  transfers between devices with their start and end apart: 11, of which 6 were waited for; matrix products, arithmetic and copies ran while one was open for 0% of the time, Pallas kernels for 0%

commit v1 on v0

v1 whole, which is shorter than its diff:
```python
import functools

import jax
import jax.numpy as jnp
from jax import lax
from jax.experimental import pallas as pl
from jax.experimental.pallas import tpu as pltpu
from jax.sharding import PartitionSpec as P

ITERS = 5
BASIS = ITERS + 1
PAIRS = [(i, j) for i in range(BASIS) for j in range(i, BASIS)]
PIVOT_SHARE = 0.02
VMEM_BYTES = 48 * 1024 * 1024
PRECISE = lax.Precision.HIGHEST


def call(kernel, out_shape, in_spaces, **kwargs):
    spaces = {"v": pltpu.VMEM, "s": pltpu.SMEM}
    return pl.pallas_call(
        kernel,
        out_shape=out_shape,
        in_specs=[pl.BlockSpec(memory_space=spaces[c]) for c in in_spaces],
        compiler_params=pltpu.CompilerParams(vmem_limit_bytes=VMEM_BYTES),
        **kwargs,
    )


def split_dot(field, block):
    rows = field.shape[0]
    high = field.astype(jnp.bfloat16)
    low = (field - high.astype(jnp.float32)).astype(jnp.bfloat16)
    both = jnp.dot(jnp.concatenate([high, low], axis=0), block, preferred_element_type=jnp.float32)
    return both[:rows] + both[rows:]


def far_kernel(target_ref, delay_ref, history_ref, blocks_ref, out_ref):
    out_ref[...] = jnp.zeros_like(out_ref)
    for entry in range(blocks_ref.shape[0]):
        target = target_ref[entry]
        product = jnp.dot(
            history_ref[delay_ref[entry] - 1],
            blocks_ref[entry],
            preferred_element_type=jnp.float32,
        )
        out_ref[target] = out_ref[target] + product


def start_kernel(received_ref, voltage_ref, jacobi_ref, out_ref):
    right_side = voltage_ref[...] - jnp.sum(received_ref[...], axis=0)
    out_ref[...] = right_side + split_dot(right_side, jacobi_ref[...])


def power_kernel(link_ref, field_ref, lower_ref, upper_ref, near_ref, jacobi_ref, out_ref):
    field = field_ref[...]
    lower = link_ref[0].astype(jnp.float32) * lower_ref[...]
    upper = link_ref[1].astype(jnp.float32) * upper_ref[...]
    depth = near_ref.shape[0] * near_ref.shape[1]
    near = split_dot(
        jnp.concatenate([lower, field, upper], axis=1), near_ref[...].reshape(depth, field.shape[1])
    )
    out_ref[...] = near + split_dot(field + near, jacobi_ref[...])


def gram_kernel(*refs):
    out_ref = refs[-1]
    fields = [ref[...] for ref in refs[:-1]]
    scenarios, segments = fields[0].shape
    ones = jnp.ones((8, segments), jnp.float32)
    stacked = jnp.concatenate([fields[i] * fields[j] for i, j in PAIRS], axis=0)
    sums = lax.dot_general(
        ones, stacked, (((1,), (1,)), ((), ())), precision=PRECISE, preferred_element_type=jnp.float32
    )
    sums = jnp.concatenate([sums[0:1], jnp.zeros((1, out_ref.shape[2] - sums.shape[1]), jnp.float32)], axis=1)
    out_ref[...] = jnp.broadcast_to(sums[None], out_ref.shape)


def add_kernel(received_ref, out_ref):
    total = jnp.sum(received_ref[...], axis=0)
    out_ref[...] = jnp.broadcast_to(total[None], out_ref.shape)


def solve_kernel(*refs):
    received_ref, field_refs, out_ref, safe_ref = refs[0], refs[1:-2], refs[-2], refs[-1]
    total = jnp.sum(received_ref[...], axis=0)
    scenarios = out_ref.shape[0]
    gram = {pair: total[:, p * scenarios : (p + 1) * scenarios] for p, pair in enumerate(PAIRS)}
    factor = {}
    safe = jnp.ones((1, scenarios), jnp.float32)
    for i in range(BASIS):
        pivot = gram[i, i]
        for k in range(i):
            pivot = pivot - factor[k, i] * factor[k, i]
        safe = jnp.where(pivot >= PIVOT_SHARE * gram[i, i], safe, 0.0)
        safe = jnp.where(pivot > 0.0, safe, 0.0)
        safe = jnp.where(gram[i, i] < jnp.inf, safe, 0.0)
        factor[i, i] = jnp.sqrt(pivot)
        for j in range(i + 1, BASIS):
            entry = gram[i, j]
            for k in range(i):
                entry = entry - factor[k, i] * factor[k, j]
            factor[i, j] = entry / factor[i, i]
    matrix = [[None] * ITERS for _ in range(BASIS)]
    for j in range(ITERS):
        for i in range(j + 1):
            matrix[i][j] = factor[i, j] + factor[i, j + 1]
        matrix[j + 1][j] = factor[j + 1, j + 1]
    target = [factor[0, 0]] + [None] * ITERS
    for j in range(ITERS):
        diagonal, below = matrix[j][j], matrix[j + 1][j]
        radius = jnp.sqrt(diagonal * diagonal + below * below)
        cosine, sine = diagonal / radius, below / radius
        matrix[j][j] = radius
        for k in range(j + 1, ITERS):
            upper, lower = matrix[j][k], matrix[j + 1][k]
            matrix[j][k] = cosine * upper + sine * lower
            matrix[j + 1][k] = cosine * lower - sine * upper
        target[j + 1] = -sine * target[j]
        target[j] = cosine * target[j]
    coeffs = [None] * ITERS
    for j in reversed(range(ITERS)):
        partial = target[j]
        for k in range(j + 1, ITERS):
            partial = partial - matrix[j][k] * coeffs[k]
        coeffs[j] = partial / matrix[j][j]
    padded = jnp.concatenate(coeffs + [jnp.zeros((8 - ITERS, scenarios), jnp.float32)], axis=0)
    padded = jnp.concatenate([padded, jnp.zeros((8, 128 - scenarios), jnp.float32)], axis=1)
    columns = jnp.transpose(padded)[:scenarios]
    result = columns[:, 0:1] * field_refs[0][...]
    for j in range(1, ITERS):
        result = result + columns[:, j : j + 1] * field_refs[j][...]
    out_ref[...] = result
    safe_ref[0] = jnp.min(safe)


def neighbours(field):
    size = lax.axis_size("row")
    up = [(i, i + 1) for i in range(size - 1)]
    down = [(j, i) for i, j in up]
    return lax.ppermute(field, "row", up), lax.ppermute(field, "row", down)


def near_apply(field, near_f32, link_gain):
    lower, upper = neighbours(field)
    result = field + jnp.dot(field, near_f32[1], precision=PRECISE)
    result = result + link_gain[0] * jnp.dot(lower, near_f32[0], precision=PRECISE)
    return result + link_gain[1] * jnp.dot(upper, near_f32[2], precision=PRECISE)


def jacobi_apply(field, jacobi_f32):
    return field + jnp.dot(field, jacobi_f32, precision=PRECISE)


def givens_solve(hessen, start_norm):
    matrix = [[hessen[i][k] for k in range(ITERS)] for i in range(ITERS + 1)]
    target = [start_norm] + [jnp.zeros_like(start_norm) for k in range(ITERS)]
    for j in range(ITERS):
        diag_val = matrix[j][j]
        below_val = matrix[j + 1][j]
        radius = jnp.sqrt(diag_val * diag_val + below_val * below_val)
        cosine = diag_val / radius
        sine_val = below_val / radius
        for k in range(j, ITERS):
            upper_val = matrix[j][k]
            lower_val = matrix[j + 1][k]
            matrix[j][k] = cosine * upper_val + sine_val * lower_val
            matrix[j + 1][k] = cosine * lower_val - sine_val * upper_val
        target[j + 1] = -sine_val * target[j]
        target[j] = cosine * target[j]
    coeffs = [None] * ITERS
    for j in reversed(range(ITERS)):
        partial_val = target[j]
        for k in range(j + 1, ITERS):
            partial_val = partial_val - matrix[j][k] * coeffs[k]
        coeffs[j] = partial_val / matrix[j][j]
    return coeffs


def stepwise_solve(initial, near, jacobi, link):
    near_f32 = near.astype(jnp.float32)
    jacobi_f32 = jacobi.astype(jnp.float32)
    link_gain = link.astype(jnp.float32)
    start_norm = jnp.sqrt(lax.psum(jnp.sum(initial * initial, axis=1), ("tile", "row")))
    basis = [initial / start_norm[:, None]]
    zero_row = jnp.zeros_like(start_norm)
    hessen = [[zero_row for k in range(ITERS)] for i in range(ITERS + 1)]
    for j in range(ITERS):
        candidate = jacobi_apply(near_apply(basis[j], near_f32, link_gain), jacobi_f32)
        local_dots = jnp.stack([jnp.sum(v * candidate, axis=1) for v in basis])
        projections = lax.psum(local_dots, ("tile", "row"))
        for i in range(j + 1):
            candidate = candidate - projections[i][:, None] * basis[i]
        new_norm = jnp.sqrt(lax.psum(jnp.sum(candidate * candidate, axis=1), ("tile", "row")))
        for i in range(j + 1):
            hessen[i][j] = projections[i]
        hessen[j + 1][j] = new_norm
        basis.append(candidate / new_norm[:, None])
    coeffs = givens_solve(hessen, start_norm)
    result = coeffs[0][:, None] * basis[0]
    for j in range(1, ITERS):
        result = result + coeffs[j][:, None] * basis[j]
    return result


def per_device(
    voltage, history, far_blocks, far_target, far_delay, near_blocks, near_link, jacobi_blocks
):
    voltage = voltage[0, 0, 0]
    history = history[0, 0]
    far_blocks = far_blocks[0, 0]
    targets = far_target[0, 0, :, 0]
    delays = far_delay[0, 0]
    near = near_blocks[0, 0]
    link = near_link[0, 0]
    jacobi = jacobi_blocks[0, 0]
    tiles, rows = lax.axis_size("tile"), lax.axis_size("row")
    scenarios, segments = voltage.shape
    f32 = jnp.float32
    field_shape = jax.ShapeDtypeStruct((scenarios, segments), f32)

    bucket = call(
        far_kernel, jax.ShapeDtypeStruct((tiles, scenarios, segments), f32), "ssvv"
    )(targets, delays, history, far_blocks)
    received = lax.all_to_all(bucket, "tile", split_axis=0, concat_axis=0, tiled=True)
    initial = call(start_kernel, field_shape, "vvv")(received, voltage, jacobi)

    power = call(power_kernel, field_shape, "svvvvv")
    fields = [initial]
    for _ in range(ITERS):
        lower, upper = neighbours(fields[-1])
        fields.append(power(link, fields[-1], lower, upper, near, jacobi))

    width = -(-len(PAIRS) * scenarios // 128) * 128
    local = call(gram_kernel, jax.ShapeDtypeStruct((rows, 1, width), f32), "v" * BASIS)(*fields)
    by_row = lax.all_to_all(local, "row", split_axis=0, concat_axis=0, tiled=True)
    group = call(add_kernel, jax.ShapeDtypeStruct((tiles, 1, width), f32), "v")(by_row)
    by_tile = lax.all_to_all(group, "tile", split_axis=0, concat_axis=0, tiled=True)
    result, safe = call(
        solve_kernel,
        (field_shape, jax.ShapeDtypeStruct((1,), f32)),
        "v" * (BASIS),
        out_specs=(pl.BlockSpec(memory_space=pltpu.VMEM), pl.BlockSpec(memory_space=pltpu.SMEM)),
    )(by_tile, *fields[:ITERS])
    result = lax.cond(
        safe[0] > 0.5,
        lambda: result,
        lambda: stepwise_solve(initial, near, jacobi, link),
    )
    return result[None, None, None]


def solution(mesh):
    return jax.shard_map(
        per_device,
        mesh=mesh,
        in_specs=(
            P("tile", "row", None, None, None),
            P("tile", "row", None, None, None),
            P("tile", "row", None, None, None),
            P("tile", "row", None, None),
            P("tile", "row", None),
            P("tile", "row", None, None, None),
            P("tile", "row", None),
            P("tile", "row", None, None),
        ),
        out_specs=P("tile", "row", None, None, None),
        check_vma=False,
    )
```

time: 1180 us -> 129 us (0.11)
  blocking collectives: 1060 us -> 60.6 us
  waiting for transfers between devices: 60.3 us -> 14.3 us
  matrix products: 12.9 us -> 0 us
    psum x11 -> x0, blocking collectives: 1060 us -> none  [the longest x5 481 us: krylov_solve(): projections = lax.psum(local_dots, ('tile', 'row'))]
    all_to_all x0 -> x2, blocking collectives: none -> 60.6 us  [the longest x1 38.1 us: per_device(): lax.all_to_all(bucket, 'tile', split_axis=0, concat_axis=0, tiled=True)]
    all_to_all x1, waiting for transfers between devices: 48.2 us -> 9.33 us  [per_device(): lax.all_to_all(group, 'tile', split_axis=0, concat_axis=0, tiled=True)]
    dot_general x23 -> x0, matrix products: 12.9 us -> none  [the longest x5 4.04 us: near_apply(): jnp.dot(padded[2], near_f32[2], precision=PRECISE)]
where the time goes in v1:
time: 129 us; the launch traced here: 128 us
  blocking collectives  60.6 us (47%)
  starting transfers between devices  39.4 us (31%)
  waiting for transfers between devices  14.3 us (11%)
  Pallas kernels  8.12 us (6%)
  local copies, waits for them, and re-layouts  4.21 us (3%)
    all_to_all x1, blocking collectives, per_device(): lax.all_to_all(bucket, 'tile', split_axis=0, concat_axis=0, tiled=True)  38.1 us
    ppermute x10, starting transfers between devices, neighbours(): return (lax.ppermute(field, 'row', up), lax.ppermute(field, 'row', down))  34.6 us
    all_to_all x1, blocking collectives, per_device(): lax.all_to_all(local, 'row', split_axis=0, concat_axis=0, tiled=True)  22.4 us
    all_to_all x1, waiting for transfers between devices, per_device(): lax.all_to_all(group, 'tile', split_axis=0, concat_axis=0, tiled=True)  9.33 us
    ppermute x10, waiting for transfers between devices, neighbours(): return (lax.ppermute(field, 'row', up), lax.ppermute(field, 'row', down))  4.97 us
    all_to_all x1, starting transfers between devices, per_device(): lax.all_to_all(group, 'tile', split_axis=0, concat_axis=0, tiled=True)  4.79 us
    unnamed x18, local copies, waits for them, and re-layouts  4.21 us
    pallas_call x5, Pallas kernels, per_device(): fields.append(power(link, fields[-1], lower, upper, near, jacobi))  4.15 us
  transfers between devices with their start and end apart: 11, of which 6 were waited for; matrix products, arithmetic and copies ran while one was open for 0% of the time, Pallas kernels for 0%

profile of v1, /device:TPU:1, one launch (start us, length us, event | category | flops | bytes accessed | tf_op | source)
XLA Modules:
  0.0 127.6 jit_solution(10172635542324843407)
XLA Ops:
  0.7 1.2 copy-done
  1.9 1.0 copy-done.1
  2.9 0.9 shard_map.84
  3.9 38.1 %all_to_all.15.received_ref = f32[32,64,128]{2,1,0:T(8,128)S(1)} all-to-all(f32[32,64,128]{2,1,0:T(8,128)S(1)} %shard_map.84), channel_id=1, replica_groups=mesh['tile'=32,'row'=16] {'tile'}, dimensions={0} | all-to-all | bytes 2097152 | tf_op jit(solution)/shard_map/all_to_all | solution.py:224
  42.3 6.9 %collective-permute-start.11 = (f32[64,128]{1,0:T(8,128)S(1)}, f32[64,128]{1,0:T(8,128)S(1)}, u32[]{:S(2)}, u32[]{:S(2)}) collective-permute-start(f32[64,128]{1,0:T(8,128)S(1)} %shard_map.85.field_ref.refs_0_.refs_1_), channel_id=1, source_target_pairs={{1,0},{2,1},{3,2},{4,3},{5,4},{6,5},{7,6},{8,7},{9,8},{10,9},{11,1... | collective-permute-start | bytes 98312 | tf_op jit(solution)/shard_map/ppermute | solution.py:140
  49.1 3.1 %collective-permute-start.10 = (f32[64,128]{1,0:T(8,128)S(1)}, f32[64,128]{1,0:T(8,128)S(1)}, u32[]{:S(2)}, u32[]{:S(2)}) collective-permute-start(f32[64,128]{1,0:T(8,128)S(1)} %shard_map.85.field_ref.refs_0_.refs_1_), channel_id=1, source_target_pairs={{0,1},{1,2},{2,3},{3,4},{4,5},{5,6},{6,7},{7,8},{8,9},{9,10},{10,1... | collective-permute-start | bytes 98312 | tf_op jit(solution)/shard_map/ppermute | solution.py:140
  52.3 1.0 collective-permute-done.10.lower_ref
  54.7 1.9 %collective-permute-start.13 = (f32[64,128]{1,0:T(8,128)S(1)}, f32[64,128]{1,0:T(8,128)S(1)}, u32[]{:S(2)}, u32[]{:S(2)}) collective-permute-start(f32[64,128]{1,0:T(8,128)S(1)} %shard_map.86.field_ref.refs_1_.refs_2_), channel_id=1, source_target_pairs={{1,0},{2,1},{3,2},{4,3},{5,4},{6,5},{7,6},{8,7},{9,8},{10,9},{11,1... | collective-permute-start | bytes 98312 | tf_op jit(solution)/shard_map/ppermute | solution.py:140
  56.7 4.2 %collective-permute-start.12 = (f32[64,128]{1,0:T(8,128)S(1)}, f32[64,128]{1,0:T(8,128)S(1)}, u32[]{:S(2)}, u32[]{:S(2)}) collective-permute-start(f32[64,128]{1,0:T(8,128)S(1)} %shard_map.86.field_ref.refs_1_.refs_2_), channel_id=1, source_target_pairs={{0,1},{1,2},{2,3},{3,4},{4,5},{5,6},{6,7},{7,8},{8,9},{9,10},{10,1... | collective-permute-start | bytes 98312 | tf_op jit(solution)/shard_map/ppermute | solution.py:140
  60.9 1.0 collective-permute-done.12.lower_ref
  62.7 1.9 %collective-permute-start.15 = (f32[64,128]{1,0:T(8,128)S(1)}, f32[64,128]{1,0:T(8,128)S(1)}, u32[]{:S(2)}, u32[]{:S(2)}) collective-permute-start(f32[64,128]{1,0:T(8,128)S(1)} %shard_map.87.field_ref.refs_2_.refs_3_), channel_id=1, source_target_pairs={{1,0},{2,1},{3,2},{4,3},{5,4},{6,5},{7,6},{8,7},{9,8},{10,9},{11,1... | collective-permute-start | bytes 98312 | tf_op jit(solution)/shard_map/ppermute | solution.py:140
  64.7 4.2 %collective-permute-start.14 = (f32[64,128]{1,0:T(8,128)S(1)}, f32[64,128]{1,0:T(8,128)S(1)}, u32[]{:S(2)}, u32[]{:S(2)}) collective-permute-start(f32[64,128]{1,0:T(8,128)S(1)} %shard_map.87.field_ref.refs_2_.refs_3_), channel_id=1, source_target_pairs={{0,1},{1,2},{2,3},{3,4},{4,5},{5,6},{6,7},{7,8},{8,9},{9,10},{10,1... | collective-permute-start | bytes 98312 | tf_op jit(solution)/shard_map/ppermute | solution.py:140
  68.9 1.0 collective-permute-done.14.lower_ref
  69.9 0.8 shard_map.88.field_ref.refs_3_.refs_4_
  70.7 1.9 %collective-permute-start.17 = (f32[64,128]{1,0:T(8,128)S(1)}, f32[64,128]{1,0:T(8,128)S(1)}, u32[]{:S(2)}, u32[]{:S(2)}) collective-permute-start(f32[64,128]{1,0:T(8,128)S(1)} %shard_map.88.field_ref.refs_3_.refs_4_), channel_id=1, source_target_pairs={{1,0},{2,1},{3,2},{4,3},{5,4},{6,5},{7,6},{8,7},{9,8},{10,9},{11,1... | collective-permute-start | bytes 98312 | tf_op jit(solution)/shard_map/ppermute | solution.py:140
  72.7 4.2 %collective-permute-start.16 = (f32[64,128]{1,0:T(8,128)S(1)}, f32[64,128]{1,0:T(8,128)S(1)}, u32[]{:S(2)}, u32[]{:S(2)}) collective-permute-start(f32[64,128]{1,0:T(8,128)S(1)} %shard_map.88.field_ref.refs_3_.refs_4_), channel_id=1, source_target_pairs={{0,1},{1,2},{2,3},{3,4},{4,5},{5,6},{6,7},{7,8},{8,9},{9,10},{10,1... | collective-permute-start | bytes 98312 | tf_op jit(solution)/shard_map/ppermute | solution.py:140
  76.9 1.0 collective-permute-done.16.lower_ref
  78.7 1.9 %collective-permute-start.19 = (f32[64,128]{1,0:T(8,128)S(1)}, f32[64,128]{1,0:T(8,128)S(1)}, u32[]{:S(2)}, u32[]{:S(2)}) collective-permute-start(f32[64,128]{1,0:T(8,128)S(1)} %shard_map.89.field_ref.refs_4_.refs_5_), channel_id=1, source_target_pairs={{1,0},{2,1},{3,2},{4,3},{5,4},{6,5},{7,6},{8,7},{9,8},{10,9},{11,1... | collective-permute-start | bytes 98312 | tf_op jit(solution)/shard_map/ppermute | solution.py:140
  80.7 4.2 %collective-permute-start.18 = (f32[64,128]{1,0:T(8,128)S(1)}, f32[64,128]{1,0:T(8,128)S(1)}, u32[]{:S(2)}, u32[]{:S(2)}) collective-permute-start(f32[64,128]{1,0:T(8,128)S(1)} %shard_map.89.field_ref.refs_4_.refs_5_), channel_id=1, source_target_pairs={{0,1},{1,2},{2,3},{3,4},{4,5},{5,6},{6,7},{7,8},{8,9},{9,10},{10,1... | collective-permute-start | bytes 98312 | tf_op jit(solution)/shard_map/ppermute | solution.py:140
  84.9 1.0 collective-permute-done.18.lower_ref
  87.4 22.4 %all_to_all.16.received_ref = f32[16,1,1408]{2,1,0:T(1,128)S(1)} all-to-all(f32[16,1,1408]{2,1,0:T(1,128)S(1)} %shard_map.91), channel_id=1, replica_groups=mesh['tile'=32,'row'=16] {'row'}, dimensions={0} | all-to-all | bytes 180224 | tf_op jit(solution)/shard_map/all_to_all | solution.py:235
  110.6 4.8 %all-to-all-start.2 = ((f32[32,1,1408]{2,1,0:T(1,128)}), f32[32,1,1408]{2,1,0:T(1,128)S(1)}, u32[]{:S(2)}, u32[]{:S(2)}) async-start(f32[32,1,1408]{2,1,0:T(1,128)} %shard_map.92), calls=%async_computation.2 | async-start | bytes 360448 | tf_op jit(solution)/shard_map/all_to_all | solution.py:237
  115.4 9.3 %all-to-all-done.2.refs_0_ = f32[32,1,1408]{2,1,0:T(1,128)S(1)} async-done(((f32[32,1,1408]{2,1,0:T(1,128)}), f32[32,1,1408]{2,1,0:T(1,128)S(1)}, u32[]{:S(2)}, u32[]{:S(2)}) %all-to-all-start.2) | async-done | bytes 180256 | tf_op jit(solution)/shard_map/all_to_all | solution.py:237
  124.7 1.4 %shard_map.93 = (f32[64,128]{1,0:T(8,128)S(1)}, f32[1]{0:T(128)}) custom-call(f32[32,1,1408]{2,1,0:T(1,128)S(1)} %all-to-all-done.2.refs_0_, f32[64,128]{1,0:T(8,128)S(1)} %shard_map.85.field_ref.refs_0_.refs_1_, f32[64,128]{1,0:T(8,128)S(1)} %shard_map.86.field_ref.refs_1_.refs_2_, f32[64,128]{1,0:T(8,128)S(1)} %shard_map.87.field_ref.refs_2_.refs_3_, ...), custom_call_target="tpu_custom_call" | custom-call | tf_op jit(solution)/shard_map/pallas_call | solution.py:238
  (29 shorter events, 7.1 us)
Async XLA Ops:
  0.0 0.7 copy-start.3
  0.0 0.7 copy-start.4
  0.7 1.2 copy-start
  1.9 1.0 copy-start.1
  3.9 38.2 %copy-start.2 = (f32[1,1,1,64,128]{4,3,2,1,0:T(8,128)S(1)}, f32[1,1,1,64,128]{4,3,2,1,0:T(8,128)}, u32[]{:S(2)}) copy-start(f32[1,1,1,64,128]{4,3,2,1,0:T(8,128)} %param.10) | copy-start | bytes 98308
  3.9 38.2 %copy-start.6 = (bf16[1,1,128,128]{3,2,1,0:T(8,128)(2,1)S(1)}, bf16[1,1,128,128]{3,2,1,0:T(8,128)(2,1)}, u32[]{:S(2)}) copy-start(bf16[1,1,128,128]{3,2,1,0:T(8,128)(2,1)} %param.17) | copy-start | bytes 98308
  42.1 11.2 %copy-start.5 = (bf16[1,1,3,128,128]{4,3,2,1,0:T(8,128)(2,1)S(1)}, bf16[1,1,3,128,128]{4,3,2,1,0:T(8,128)(2,1)}, u32[]{:S(2)}) copy-start(bf16[1,1,3,128,128]{4,3,2,1,0:T(8,128)(2,1)} %param.15) | copy-start | bytes 294916
  42.3 10.0 %collective-permute-start.11 = (f32[64,128]{1,0:T(8,128)S(1)}, f32[64,128]{1,0:T(8,128)S(1)}, u32[]{:S(2)}, u32[]{:S(2)}) collective-permute-start(f32[64,128]{1,0:T(8,128)S(1)} %shard_map.85.field_ref.refs_0_.refs_1_), channel_id=1, source_target_pairs={{1,0},{2,1},{3,2},{4,3},{5,4},{6,5},{7,6},{8,7},{9,8},{10,9},{11,1... | collective-permute-start | bytes 98312 | tf_op jit(solution)/shard_map/ppermute | solution.py:140
  49.1 4.1 %collective-permute-start.10 = (f32[64,128]{1,0:T(8,128)S(1)}, f32[64,128]{1,0:T(8,128)S(1)}, u32[]{:S(2)}, u32[]{:S(2)}) collective-permute-start(f32[64,128]{1,0:T(8,128)S(1)} %shard_map.85.field_ref.refs_0_.refs_1_), channel_id=1, source_target_pairs={{0,1},{1,2},{2,3},{3,4},{4,5},{5,6},{6,7},{7,8},{8,9},{9,10},{10,1... | collective-permute-start | bytes 98312 | tf_op jit(solution)/shard_map/ppermute | solution.py:140
  53.2 0.7 copy-start.7
  54.7 6.2 %collective-permute-start.13 = (f32[64,128]{1,0:T(8,128)S(1)}, f32[64,128]{1,0:T(8,128)S(1)}, u32[]{:S(2)}, u32[]{:S(2)}) collective-permute-start(f32[64,128]{1,0:T(8,128)S(1)} %shard_map.86.field_ref.refs_1_.refs_2_), channel_id=1, source_target_pairs={{1,0},{2,1},{3,2},{4,3},{5,4},{6,5},{7,6},{8,7},{9,8},{10,9},{11,1... | collective-permute-start | bytes 98312 | tf_op jit(solution)/shard_map/ppermute | solution.py:140
  56.7 5.2 %collective-permute-start.12 = (f32[64,128]{1,0:T(8,128)S(1)}, f32[64,128]{1,0:T(8,128)S(1)}, u32[]{:S(2)}, u32[]{:S(2)}) collective-permute-start(f32[64,128]{1,0:T(8,128)S(1)} %shard_map.86.field_ref.refs_1_.refs_2_), channel_id=1, source_target_pairs={{0,1},{1,2},{2,3},{3,4},{4,5},{5,6},{6,7},{7,8},{8,9},{9,10},{10,1... | collective-permute-start | bytes 98312 | tf_op jit(solution)/shard_map/ppermute | solution.py:140
  62.7 6.2 %collective-permute-start.15 = (f32[64,128]{1,0:T(8,128)S(1)}, f32[64,128]{1,0:T(8,128)S(1)}, u32[]{:S(2)}, u32[]{:S(2)}) collective-permute-start(f32[64,128]{1,0:T(8,128)S(1)} %shard_map.87.field_ref.refs_2_.refs_3_), channel_id=1, source_target_pairs={{1,0},{2,1},{3,2},{4,3},{5,4},{6,5},{7,6},{8,7},{9,8},{10,9},{11,1... | collective-permute-start | bytes 98312 | tf_op jit(solution)/shard_map/ppermute | solution.py:140
  64.7 5.2 %collective-permute-start.14 = (f32[64,128]{1,0:T(8,128)S(1)}, f32[64,128]{1,0:T(8,128)S(1)}, u32[]{:S(2)}, u32[]{:S(2)}) collective-permute-start(f32[64,128]{1,0:T(8,128)S(1)} %shard_map.87.field_ref.refs_2_.refs_3_), channel_id=1, source_target_pairs={{0,1},{1,2},{2,3},{3,4},{4,5},{5,6},{6,7},{7,8},{8,9},{9,10},{10,1... | collective-permute-start | bytes 98312 | tf_op jit(solution)/shard_map/ppermute | solution.py:140
  70.7 6.2 %collective-permute-start.17 = (f32[64,128]{1,0:T(8,128)S(1)}, f32[64,128]{1,0:T(8,128)S(1)}, u32[]{:S(2)}, u32[]{:S(2)}) collective-permute-start(f32[64,128]{1,0:T(8,128)S(1)} %shard_map.88.field_ref.refs_3_.refs_4_), channel_id=1, source_target_pairs={{1,0},{2,1},{3,2},{4,3},{5,4},{6,5},{7,6},{8,7},{9,8},{10,9},{11,1... | collective-permute-start | bytes 98312 | tf_op jit(solution)/shard_map/ppermute | solution.py:140
  72.7 5.2 %collective-permute-start.16 = (f32[64,128]{1,0:T(8,128)S(1)}, f32[64,128]{1,0:T(8,128)S(1)}, u32[]{:S(2)}, u32[]{:S(2)}) collective-permute-start(f32[64,128]{1,0:T(8,128)S(1)} %shard_map.88.field_ref.refs_3_.refs_4_), channel_id=1, source_target_pairs={{0,1},{1,2},{2,3},{3,4},{4,5},{5,6},{6,7},{7,8},{8,9},{9,10},{10,1... | collective-permute-start | bytes 98312 | tf_op jit(solution)/shard_map/ppermute | solution.py:140
  78.7 6.2 %collective-permute-start.19 = (f32[64,128]{1,0:T(8,128)S(1)}, f32[64,128]{1,0:T(8,128)S(1)}, u32[]{:S(2)}, u32[]{:S(2)}) collective-permute-start(f32[64,128]{1,0:T(8,128)S(1)} %shard_map.89.field_ref.refs_4_.refs_5_), channel_id=1, source_target_pairs={{1,0},{2,1},{3,2},{4,3},{5,4},{6,5},{7,6},{8,7},{9,8},{10,9},{11,1... | collective-permute-start | bytes 98312 | tf_op jit(solution)/shard_map/ppermute | solution.py:140
  80.7 5.2 %collective-permute-start.18 = (f32[64,128]{1,0:T(8,128)S(1)}, f32[64,128]{1,0:T(8,128)S(1)}, u32[]{:S(2)}, u32[]{:S(2)}) collective-permute-start(f32[64,128]{1,0:T(8,128)S(1)} %shard_map.89.field_ref.refs_4_.refs_5_), channel_id=1, source_target_pairs={{0,1},{1,2},{2,3},{3,4},{4,5},{5,6},{6,7},{7,8},{8,9},{9,10},{10,1... | collective-permute-start | bytes 98312 | tf_op jit(solution)/shard_map/ppermute | solution.py:140
  110.6 14.1 %all-to-all-start.2 = ((f32[32,1,1408]{2,1,0:T(1,128)}), f32[32,1,1408]{2,1,0:T(1,128)S(1)}, u32[]{:S(2)}, u32[]{:S(2)}) async-start(f32[32,1,1408]{2,1,0:T(1,128)} %shard_map.92), calls=%async_computation.2 | async-start | bytes 360448 | tf_op jit(solution)/shard_map/all_to_all | solution.py:237
  127.0 0.6 copy-start.8

commit v2 on v1

--- a/solution.py
+++ b/solution.py
@@ -1,5 +1,3 @@
-import functools
-
 import jax
 import jax.numpy as jnp
 from jax import lax
@@ -51,37 +49,70 @@
     out_ref[...] = right_side + split_dot(right_side, jacobi_ref[...])
 
 
-def power_kernel(link_ref, field_ref, lower_ref, upper_ref, near_ref, jacobi_ref, out_ref):
-    field = field_ref[...]
-    lower = link_ref[0].astype(jnp.float32) * lower_ref[...]
-    upper = link_ref[1].astype(jnp.float32) * upper_ref[...]
-    depth = near_ref.shape[0] * near_ref.shape[1]
-    near = split_dot(
-        jnp.concatenate([lower, field, upper], axis=1), near_ref[...].reshape(depth, field.shape[1])
-    )
-    out_ref[...] = near + split_dot(field + near, jacobi_ref[...])
-
-
-def gram_kernel(*refs):
-    out_ref = refs[-1]
-    fields = [ref[...] for ref in refs[:-1]]
-    scenarios, segments = fields[0].shape
-    ones = jnp.ones((8, segments), jnp.float32)
-    stacked = jnp.concatenate([fields[i] * fields[j] for i, j in PAIRS], axis=0)
-    sums = lax.dot_general(
-        ones, stacked, (((1,), (1,)), ((), ())), precision=PRECISE, preferred_element_type=jnp.float32
-    )
-    sums = jnp.concatenate([sums[0:1], jnp.zeros((1, out_ref.shape[2] - sums.shape[1]), jnp.float32)], axis=1)
-    out_ref[...] = jnp.broadcast_to(sums[None], out_ref.shape)
-
-
-def add_kernel(received_ref, out_ref):
-    total = jnp.sum(received_ref[...], axis=0)
-    out_ref[...] = jnp.broadcast_to(total[None], out_ref.shape)
-
-
-def solve_kernel(*refs):
-    received_ref, field_refs, out_ref, safe_ref = refs[0], refs[1:-2], refs[-2], refs[-1]
+def krylov_kernel(place_ref, start_ref, blocks_ref, gram_ref, own_ref, fields, parts, blocks, sums):
+    rows, scenarios, segments = start_ref.shape
+    depth = blocks.shape[1]
+    zero_part = jnp.zeros(parts.shape[2:], parts.dtype)
+    for side in range(2):
+        parts[side, 0] = zero_part
+        parts[side, rows + 1] = zero_part
+
+    def halves(value):
+        high = value.astype(jnp.bfloat16)
+        low = (value - high.astype(jnp.float32)).astype(jnp.bfloat16)
+        return jnp.concatenate([high, low], axis=0)
+
+    for b in range(rows):
+        blocks[b] = blocks_ref[b].reshape(depth, segments).astype(jnp.bfloat16)
+        fields[0, b] = start_ref[b]
+        parts[0, b + 1] = halves(start_ref[b])
+
+    def power(k, carry):
+        now, later = lax.rem(k, 2), lax.rem(k + 1, 2)
+        for b in range(rows):
+            around = jnp.concatenate([parts[now, b], parts[now, b + 1], parts[now, b + 2]], axis=1)
+            near = jnp.dot(
+                around, blocks[b, : depth - segments], preferred_element_type=jnp.float32
+            )
+            near = near[:scenarios] + near[scenarios:]
+            last = jnp.dot(
+                halves(fields[k, b] + near),
+                blocks[b, depth - segments :],
+                preferred_element_type=jnp.float32,
+            )
+            value = near + last[:scenarios] + last[scenarios:]
+            fields[k + 1, b] = value
+            parts[later, b + 1] = halves(value)
+        return carry
+
+    lax.fori_loop(0, ITERS, power, 0)
+
+    def gram(c, carry):
+        at = pl.ds(pl.multiple_of(c * 8, 8), 8)
+        totals = [jnp.zeros((8, segments), jnp.float32) for _ in PAIRS]
+        for b in range(rows):
+            values = [fields[i, b, at] for i in range(BASIS)]
+            totals = [t + values[i] * values[j] for t, (i, j) in zip(totals, PAIRS)]
+        for p, t in enumerate(totals):
+            sums[p, at] = t
+        return carry
+
+    lax.fori_loop(0, scenarios // 8, gram, 0)
+    for p in range(len(PAIRS), sums.shape[0]):
+        sums[p] = jnp.zeros((scenarios, segments), jnp.float32)
+    total = lax.dot_general(
+        jnp.ones((8, segments), jnp.float32),
+        sums[...].reshape(sums.shape[0] * scenarios, segments),
+        (((1,), (1,)), ((), ())),
+        precision=PRECISE,
+        preferred_element_type=jnp.float32,
+    )
+    gram_ref[...] = jnp.broadcast_to(total[0:1][None], gram_ref.shape)
+    for j in range(ITERS):
+        own_ref[j] = fields[j, place_ref[0]]
+
+
+def solve_kernel(received_ref, fields_ref, out_ref, safe_ref):
     total = jnp.sum(received_ref[...], axis=0)
     scenarios = out_ref.shape[0]
     gram = {pair: total[:, p * scenarios : (p + 1) * scenarios] for p, pair in enumerate(PAIRS)}
@@ -126,9 +157,9 @@
     padded = jnp.concatenate(coeffs + [jnp.zeros((8 - ITERS, scenarios), jnp.float32)], axis=0)
     padded = jnp.concatenate([padded, jnp.zeros((8, 128 - scenarios), jnp.float32)], axis=1)
     columns = jnp.transpose(padded)[:scenarios]
-    result = columns[:, 0:1] * field_refs[0][...]
+    result = columns[:, 0:1] * fields_ref[0]
     for j in range(1, ITERS):
-        result = result + columns[:, j : j + 1] * field_refs[j][...]
+        result = result + columns[:, j : j + 1] * fields_ref[j]
     out_ref[...] = result
     safe_ref[0] = jnp.min(safe)
 
@@ -218,29 +249,43 @@
     f32 = jnp.float32
     field_shape = jax.ShapeDtypeStruct((scenarios, segments), f32)
 
+    gate = jnp.stack([link[0], jnp.ones_like(link[0]), link[1]]).astype(f32)
+    own_blocks = jnp.concatenate(
+        [near.astype(f32) * gate[:, None, None], jacobi.astype(f32)[None]], axis=0
+    )
+    all_blocks = lax.all_gather(own_blocks, "row")
+
     bucket = call(
         far_kernel, jax.ShapeDtypeStruct((tiles, scenarios, segments), f32), "ssvv"
     )(targets, delays, history, far_blocks)
     received = lax.all_to_all(bucket, "tile", split_axis=0, concat_axis=0, tiled=True)
     initial = call(start_kernel, field_shape, "vvv")(received, voltage, jacobi)
 
-    power = call(power_kernel, field_shape, "svvvvv")
-    fields = [initial]
-    for _ in range(ITERS):
-        lower, upper = neighbours(fields[-1])
-        fields.append(power(link, fields[-1], lower, upper, near, jacobi))
-
-    width = -(-len(PAIRS) * scenarios // 128) * 128
-    local = call(gram_kernel, jax.ShapeDtypeStruct((rows, 1, width), f32), "v" * BASIS)(*fields)
-    by_row = lax.all_to_all(local, "row", split_axis=0, concat_axis=0, tiled=True)
-    group = call(add_kernel, jax.ShapeDtypeStruct((tiles, 1, width), f32), "v")(by_row)
-    by_tile = lax.all_to_all(group, "tile", split_axis=0, concat_axis=0, tiled=True)
+    starts = lax.all_gather(initial, "row")
+
+    padded_pairs = -(-len(PAIRS) * scenarios // 128) * 128 // scenarios
+    width = padded_pairs * scenarios
+    gram, own = call(
+        krylov_kernel,
+        (
+            jax.ShapeDtypeStruct((tiles, 1, width), f32),
+            jax.ShapeDtypeStruct((ITERS, scenarios, segments), f32),
+        ),
+        "svv",
+        scratch_shapes=[
+            pltpu.VMEM((BASIS, rows, scenarios, segments), f32),
+            pltpu.VMEM((2, rows + 2, 2 * scenarios, segments), jnp.bfloat16),
+            pltpu.VMEM((rows, 4 * segments, segments), jnp.bfloat16),
+            pltpu.VMEM((padded_pairs, scenarios, segments), f32),
+        ],
+    )(lax.axis_index("row").astype(jnp.int32)[None], starts, all_blocks)
+    by_tile = lax.all_to_all(gram, "tile", split_axis=0, concat_axis=0, tiled=True)
     result, safe = call(
         solve_kernel,
         (field_shape, jax.ShapeDtypeStruct((1,), f32)),
-        "v" * (BASIS),
+        "vv",
         out_specs=(pl.BlockSpec(memory_space=pltpu.VMEM), pl.BlockSpec(memory_space=pltpu.SMEM)),
-    )(by_tile, *fields[:ITERS])
+    )(by_tile, own)
     result = lax.cond(
         safe[0] > 0.5,
         lambda: result,

time: 129 us -> 1230 us (9.53)
  blocking collectives: 60.6 us -> 1080 us
  waiting for transfers between devices: 14.3 us -> 45.9 us
  Pallas kernels: 8.12 us -> 28.6 us
  between operations: 0.84 us -> 14.1 us
    psum x0 -> x11, blocking collectives: none -> 1050 us  [the longest x5 483 us: stepwise_solve(): projections = lax.psum(local_dots, ('tile', 'row'))]
    all_to_all x2 -> x0, blocking collectives: 60.6 us -> none  [the longest x1 38.1 us: per_device(): lax.all_to_all(bucket, 'tile', split_axis=0, concat_axis=0, tiled=True)]
    all_to_all x1 -> x2, waiting for transfers between devices: 9.33 us -> 33.9 us  [the longest x1 24.6 us: per_device(): lax.all_to_all(bucket, 'tile', split_axis=0, concat_axis=0, tiled=True)]
    all_gather x0 -> x1, blocking collectives: none -> 23.8 us  [per_device(): starts = lax.all_gather(initial, 'row')]
    pallas_call x8 -> x2, Pallas kernels: 6.99 us -> 26.5 us  [the longest x1 25.1 us: per_device(): call(krylov_kernel, (jax.ShapeDtypeStruct((tiles, 1, width), f32), jax.Sh...]
    all_to_all x1 -> x2, starting transfers between devices: 4.79 us -> 18.6 us  [the longest x1 13.8 us: per_device(): lax.all_to_all(bucket, 'tile', split_axis=0, concat_axis=0, tiled=True)]
  transfers between devices with their start and end apart: 11 -> 13, of which waited for: 6 -> 7; matrix products, arithmetic and copies ran while one was open for 0% -> 0% of each run, Pallas kernels for 0% -> 0%
where the time goes in v2:
time: 1230 us
  blocking collectives  1080 us (88%)
  waiting for transfers between devices  45.9 us (4%)
  starting transfers between devices  43.2 us (4%)
  Pallas kernels  28.6 us (2%)
  between operations  14.1 us (1%)
    psum x5, blocking collectives, stepwise_solve(): projections = lax.psum(local_dots, ('tile', 'row'))  483 us
    psum x5, blocking collectives, stepwise_solve(): lax.psum(jnp.sum(candidate * candidate, axis=1), ('tile', 'row'))  473 us
    psum x1, blocking collectives, stepwise_solve(): lax.psum(jnp.sum(initial * initial, axis=1), ('tile', 'row'))  95.2 us
    pallas_call x1, Pallas kernels, per_device(): call(krylov_kernel, (jax.ShapeDtypeStruct((tiles, 1, width), f32), jax.Sh...  25.1 us
    all_to_all x1, waiting for transfers between devices, per_device(): lax.all_to_all(bucket, 'tile', split_axis=0, concat_axis=0, tiled=True)  24.6 us
  transfers between devices with their start and end apart: 13, of which 7 were waited for; matrix products, arithmetic and copies ran while one was open for 0% of the time, Pallas kernels for 0%

profile of v2, /device:TPU:1, one launch (start us, length us, event | category | flops | bytes accessed | tf_op | source)
XLA Modules:
  0.0 1232.2 jit_solution(4173546751818635392)
XLA Ops:
  17.4 13.8 %all-to-all-start = ((f32[32,64,128]{2,1,0:T(8,128)}), f32[32,64,128]{2,1,0:T(8,128)S(1)}, u32[]{:S(2)}, u32[]{:S(2)}) async-start(f32[32,64,128]{2,1,0:T(8,128)} %shard_map.84), calls=%async_computation | async-start | bytes 2097152 | tf_op jit(solution)/shard_map/all_to_all | solution.py:261
  31.2 24.6 %all-to-all-done.received_ref = f32[32,64,128]{2,1,0:T(8,128)S(1)} async-done(((f32[32,64,128]{2,1,0:T(8,128)}), f32[32,64,128]{2,1,0:T(8,128)S(1)}, u32[]{:S(2)}, u32[]{:S(2)}) %all-to-all-start) | async-done | bytes 1048608 | tf_op jit(solution)/shard_map/all_to_all | solution.py:261
  56.0 23.8 %all-gather = f32[1024,128]{1,0:T(8,128)S(1)} all-gather(f32[64,128]{1,0:T(8,128)S(1)} %shard_map.85), channel_id=2, replica_groups=mesh['tile'=32,'row'=16] {'row'}, dimensions={0}, use_global_device_ids=true | all-gather | bytes 557056 | tf_op jit(solution)/shard_map/all_gather | solution.py:264
  82.0 25.1 %shard_map.86 = (f32[32,1,1408]{2,1,0:T(1,128)}, f32[5,64,128]{2,1,0:T(8,128)S(1)}) custom-call(s32[1]{0:T(128)} %bitcast.35.place_ref, f32[16,64,128]{2,1,0:T(8,128)S(1)} %bitcast.230, f32[16,4,128,128]{3,2,1,0:T(8,128)S(1)} %bitcast.229), custom_call_target="tpu_custom_call" | custom-call | tf_op jit(solution)/shard_map/pallas_call | solution.py:268
  107.2 4.8 all-to-all-start.1
  112.0 9.3 all-to-all-done.1.received_ref
  123.4 1101.3 %conditional.1 = (f32[1,1,1,64,128]{4,3,2,1,0:T(8,128)S(1)}) conditional(s32[]{:T(128)} %bitcast.48, (f32[64,128]{1,0:T(8,128)S(1)}, bf16[3,128,128]{2,1,0:T(8,128)(2,1)S(1)}, s32[1,1,2]{2,1,0:T(1,128)S(1)}, bf16[128,128]{1,0:T(8,128)(2,1)S(1)}) %tuple.63, f32[64,128]{1,0:T(8,128)S(1)} %get-tuple-element.31), branch_computations={%region_0.0_spmd, %region_33.0_spmd} | conditional | flops 252766784 | bytes 5663712 | solution.py:289
  123.5 95.2 %psum.66 = f32[64]{0:T(128)S(1)} all-reduce(f32[64]{0:T(128)S(1)} %multiply_reduce_fusion.20), channel_id=1, replica_groups=mesh['tile'=32,'row'=16] {'tile','row'}, use_global_device_ids=true, to_apply=%region_2.0 | all-reduce | flops 64 | bytes 512 | tf_op jit(solution)/shard_map/cond/branch_0_fun/psum | solution.py:214
  218.8 2.9 collective-permute-start
  228.1 96.3 %psum.67 = f32[64]{0:T(128)S(1)} all-reduce(f32[64]{0:T(128)S(1)} %get-tuple-element.83), channel_id=1, replica_groups=mesh['tile'=32,'row'=16] {'tile','row'}, use_global_device_ids=true, to_apply=%region_4.0 | all-reduce | flops 64 | bytes 512 | tf_op jit(solution)/shard_map/cond/branch_0_fun/psum | solution.py:221
  324.5 94.4 %psum.68 = f32[64]{0:T(128)S(1)} all-reduce(f32[64]{0:T(128)S(1)} %multiply_reduce_fusion.18), channel_id=1, replica_groups=mesh['tile'=32,'row'=16] {'tile','row'}, use_global_device_ids=true, to_apply=%region_6.0 | all-reduce | flops 64 | bytes 512 | tf_op jit(solution)/shard_map/cond/branch_0_fun/psum | solution.py:224
  419.0 3.3 collective-permute-start.2
  425.2 2.6 collective-permute-done.3
  428.9 96.8 %psum.69 = f32[2,64]{1,0:T(2,128)S(1)} all-reduce(f32[2,64]{1,0:T(2,128)S(1)} %pad_maximum_fusion.2), channel_id=1, replica_groups=mesh['tile'=32,'row'=16] {'tile','row'}, use_global_device_ids=true, to_apply=%region_9.0 | all-reduce | flops 128 | bytes 1024 | tf_op jit(solution)/shard_map/cond/branch_0_fun/psum | solution.py:221
  525.9 94.6 %psum.70 = f32[64]{0:T(128)S(1)} all-reduce(f32[64]{0:T(128)S(1)} %get-tuple-element.62), channel_id=1, replica_groups=mesh['tile'=32,'row'=16] {'tile','row'}, use_global_device_ids=true, to_apply=%region_11.0 | all-reduce | flops 64 | bytes 512 | tf_op jit(solution)/shard_map/cond/branch_0_fun/psum | solution.py:224
  620.7 2.7 collective-permute-start.4
  630.0 96.8 %psum.71 = f32[3,64]{1,0:T(4,128)S(1)} all-reduce(f32[3,64]{1,0:T(4,128)S(1)} %pad_maximum_fusion), channel_id=1, replica_groups=mesh['tile'=32,'row'=16] {'tile','row'}, use_global_device_ids=true, to_apply=%region_15.0 | all-reduce | flops 192 | bytes 1536 | tf_op jit(solution)/shard_map/cond/branch_0_fun/psum | solution.py:221
  727.0 94.6 %psum.72 = f32[64]{0:T(128)S(1)} all-reduce(f32[64]{0:T(128)S(1)} %get-tuple-element.60), channel_id=1, replica_groups=mesh['tile'=32,'row'=16] {'tile','row'}, use_global_device_ids=true, to_apply=%region_17.0 | all-reduce | flops 64 | bytes 512 | tf_op jit(solution)/shard_map/cond/branch_0_fun/psum | solution.py:224
  821.7 3.3 collective-permute-start.6
  831.6 96.8 %psum.73 = f32[4,64]{1,0:T(4,128)S(1)} all-reduce(f32[4,64]{1,0:T(4,128)S(1)} %pad_maximum_fusion.1), channel_id=1, replica_groups=mesh['tile'=32,'row'=16] {'tile','row'}, use_global_device_ids=true, to_apply=%region_22.0 | all-reduce | flops 256 | bytes 2048 | tf_op jit(solution)/shard_map/cond/branch_0_fun/psum | solution.py:221
  928.7 94.6 %psum.74 = f32[64]{0:T(128)S(1)} all-reduce(f32[64]{0:T(128)S(1)} %get-tuple-element.58), channel_id=1, replica_groups=mesh['tile'=32,'row'=16] {'tile','row'}, use_global_device_ids=true, to_apply=%region_24.0 | all-reduce | flops 64 | bytes 512 | tf_op jit(solution)/shard_map/cond/branch_0_fun/psum | solution.py:224
  1023.4 2.7 collective-permute-start.8
  1032.8 96.8 %psum.75 = f32[5,64]{1,0:T(8,128)S(1)} all-reduce(f32[5,64]{1,0:T(8,128)S(1)} %stack.60), channel_id=1, replica_groups=mesh['tile'=32,'row'=16] {'tile','row'}, use_global_device_ids=true, to_apply=%region_30.0 | all-reduce | flops 320 | bytes 2560 | tf_op jit(solution)/shard_map/cond/branch_0_fun/psum | solution.py:221
  1129.8 94.4 %psum.76 = f32[64]{0:T(128)S(1)} all-reduce(f32[64]{0:T(128)S(1)} %multiply_reduce_fusion), channel_id=1, replica_groups=mesh['tile'=32,'row'=16] {'tile','row'}, use_global_device_ids=true, to_apply=%region_32.0 | all-reduce | flops 64 | bytes 512 | tf_op jit(solution)/shard_map/cond/branch_0_fun/psum | solution.py:224
  (95 shorter events, 47.0 us)
Async XLA Ops:
  6.5 49.3 %copy-start.7 = (bf16[1,1,128,128]{3,2,1,0:T(8,128)(2,1)S(1)}, bf16[1,1,128,128]{3,2,1,0:T(8,128)(2,1)}, u32[]{:S(2)}) copy-start(bf16[1,1,128,128]{3,2,1,0:T(8,128)(2,1)} %param.17) | copy-start | bytes 98308
  6.5 49.3 %copy-start.3 = (f32[1,1,1,64,128]{4,3,2,1,0:T(8,128)S(1)}, f32[1,1,1,64,128]{4,3,2,1,0:T(8,128)}, u32[]{:S(2)}) copy-start(f32[1,1,1,64,128]{4,3,2,1,0:T(8,128)} %param.10) | copy-start | bytes 98308
  6.5 73.3 %all-gather.4.cloned.1.call-start = ((), (), s32[]{:S(2)}) async-start(), calls=%async_computation.2 | async-start | bytes 4456448 | tf_op jit(solution)/shard_map/all_gather | solution.py:256
  11.8 1.2 copy-start.1
  13.1 1.0 copy-start.2
  14.1 0.7 copy-start.4
  14.8 0.7 copy-start.5
  17.4 106.0 %copy-start.6 = (bf16[1,1,3,128,128]{4,3,2,1,0:T(8,128)(2,1)S(1)}, bf16[1,1,3,128,128]{4,3,2,1,0:T(8,128)(2,1)}, u32[]{:S(2)}) copy-start(bf16[1,1,3,128,128]{4,3,2,1,0:T(8,128)(2,1)} %param.15) | copy-start | bytes 294916
  17.4 106.0 %copy-start.8 = (s32[1,1,2]{2,1,0:T(1,128)S(1)}, s32[1,1,2]{2,1,0:T(1,128)}, u32[]{:S(2)}) copy-start(s32[1,1,2]{2,1,0:T(1,128)} %param.16) | copy-start | bytes 28
  17.4 38.5 %all-to-all-start = ((f32[32,64,128]{2,1,0:T(8,128)}), f32[32,64,128]{2,1,0:T(8,128)S(1)}, u32[]{:S(2)}, u32[]{:S(2)}) async-start(f32[32,64,128]{2,1,0:T(8,128)} %shard_map.84), calls=%async_computation | async-start | bytes 2097152 | tf_op jit(solution)/shard_map/all_to_all | solution.py:261
  79.9 2.2 copy-start
  107.2 14.1 %all-to-all-start.1 = ((f32[32,1,1408]{2,1,0:T(1,128)}), f32[32,1,1408]{2,1,0:T(1,128)S(1)}, u32[]{:S(2)}, u32[]{:S(2)}) async-start(f32[32,1,1408]{2,1,0:T(1,128)} %get-tuple-element.28), calls=%async_computation.1 | async-start | bytes 360448 | tf_op jit(solution)/shard_map/all_to_all | solution.py:282
  218.8 5.7 collective-permute-start
  221.7 5.2 collective-permute-start.1
  419.0 5.5 collective-permute-start.2
  422.6 5.2 collective-permute-start.3
  620.7 4.8 collective-permute-start.4
  623.6 5.2 collective-permute-start.5
  821.7 5.5 collective-permute-start.6
  825.2 5.2 collective-permute-start.7
  1023.4 4.8 collective-permute-start.8
  1026.3 5.2 collective-permute-start.9
  1224.7 0.6 copy-start.9
Sparse Core Ops, SparseCore 0:
  12.0 50.6 all-gather.3

commit v3 on v2

--- a/solution.py
+++ b/solution.py
@@ -14,8 +14,8 @@
 
 
 def call(kernel, out_shape, in_spaces, **kwargs):
-    spaces = {"v": pltpu.VMEM, "s": pltpu.SMEM}
-    return pl.pallas_call(
+    spaces = {"v": pltpu.VMEM, "s": pltpu.SMEM, "h": pltpu.HBM}
+    run = pl.pallas_call(
         kernel,
         out_shape=out_shape,
         in_specs=[pl.BlockSpec(memory_space=spaces[c]) for c in in_spaces],
@@ -23,6 +23,16 @@
         **kwargs,
     )
 
+    def placed(*operands):
+        return run(
+            *(
+                pltpu.with_memory_space_constraint(x, pltpu.HBM) if c == "h" else x
+                for c, x in zip(in_spaces, operands)
+            )
+        )
+
+    return placed
+
 
 def split_dot(field, block):
     rows = field.shape[0]
@@ -32,16 +42,41 @@
     return both[:rows] + both[rows:]
 
 
-def far_kernel(target_ref, delay_ref, history_ref, blocks_ref, out_ref):
-    out_ref[...] = jnp.zeros_like(out_ref)
-    for entry in range(blocks_ref.shape[0]):
-        target = target_ref[entry]
-        product = jnp.dot(
-            history_ref[delay_ref[entry] - 1],
-            blocks_ref[entry],
-            preferred_element_type=jnp.float32,
+def front_kernel(
+    target_hbm, delay_hbm, link_hbm, near_hbm, jacobi_hbm, history_hbm, blocks_hbm, bucket_ref, own_ref,
+    target_ref, delay_ref, link_ref, near_ref, jacobi_ref, history_ref, blocks_ref, sems, block_sems,
+):
+    entries, chunks = blocks_ref.shape[0], block_sems.shape[0]
+    step = entries // chunks
+    pairs = [
+        (target_hbm, target_ref), (delay_hbm, delay_ref), (link_hbm, link_ref),
+        (near_hbm, near_ref), (jacobi_hbm, jacobi_ref), (history_hbm, history_ref),
+    ]
+    copies = [pltpu.make_async_copy(a, b, sems.at[i]) for i, (a, b) in enumerate(pairs)]
+    slabs = [
+        pltpu.make_async_copy(
+            blocks_hbm.at[pl.ds(c * step, step)], blocks_ref.at[pl.ds(c * step, step)], block_sems.at[c]
         )
-        out_ref[target] = out_ref[target] + product
+        for c in range(chunks)
+    ]
+    for copy in copies + slabs:
+        copy.start()
+    bucket_ref[...] = jnp.zeros_like(bucket_ref)
+    for copy in copies:
+        copy.wait()
+    for side, gate in enumerate((link_ref[0], 1, link_ref[1])):
+        own_ref[side] = near_ref[side].astype(jnp.float32) * jnp.float32(gate)
+    own_ref[near_ref.shape[0]] = jacobi_ref[...].astype(jnp.float32)
+    for c in range(chunks):
+        slabs[c].wait()
+        for entry in range(c * step, (c + 1) * step):
+            target = target_ref[entry]
+            product = jnp.dot(
+                history_ref[delay_ref[entry] - 1],
+                blocks_ref[entry],
+                preferred_element_type=jnp.float32,
+            )
+            bucket_ref[target] = bucket_ref[target] + product
 
 
 def start_kernel(received_ref, voltage_ref, jacobi_ref, out_ref):
@@ -49,9 +84,14 @@
     out_ref[...] = right_side + split_dot(right_side, jacobi_ref[...])
 
 
-def krylov_kernel(place_ref, start_ref, blocks_ref, gram_ref, own_ref, fields, parts, blocks, sums):
+def krylov_kernel(
+    place_ref, start_ref, blocks_hbm, gram_ref, own_ref, fields, nears, parts, blocks, sums, staged, sems
+):
     rows, scenarios, segments = start_ref.shape
-    depth = blocks.shape[1]
+    depth, group = blocks.shape[1], rows // 4
+    copies = [pltpu.make_async_copy(blocks_hbm.at[b], staged.at[b], sems.at[b]) for b in range(rows)]
+    for copy in copies:
+        copy.start()
     zero_part = jnp.zeros(parts.shape[2:], parts.dtype)
     for side in range(2):
         parts[side, 0] = zero_part
@@ -63,29 +103,32 @@
         return jnp.concatenate([high, low], axis=0)
 
     for b in range(rows):
-        blocks[b] = blocks_ref[b].reshape(depth, segments).astype(jnp.bfloat16)
         fields[0, b] = start_ref[b]
         parts[0, b + 1] = halves(start_ref[b])
 
-    def power(k, carry):
-        now, later = lax.rem(k, 2), lax.rem(k + 1, 2)
+    for k in range(ITERS):
+        now, later = k % 2, (k + 1) % 2
         for b in range(rows):
+            if k == 0 and b % group == 0:
+                for c in range(b, b + group):
+                    copies[c].wait()
+                for c in range(b, b + group):
+                    blocks[c] = staged[c].reshape(depth, segments).astype(jnp.bfloat16)
             around = jnp.concatenate([parts[now, b], parts[now, b + 1], parts[now, b + 2]], axis=1)
             near = jnp.dot(
                 around, blocks[b, : depth - segments], preferred_element_type=jnp.float32
             )
-            near = near[:scenarios] + near[scenarios:]
+            nears[b] = near[:scenarios] + near[scenarios:]
+        for b in range(rows):
             last = jnp.dot(
-                halves(fields[k, b] + near),
+                halves(fields[k, b] + nears[b]),
                 blocks[b, depth - segments :],
                 preferred_element_type=jnp.float32,
             )
-            value = near + last[:scenarios] + last[scenarios:]
+            value = nears[b] + (last[:scenarios] + last[scenarios:])
             fields[k + 1, b] = value
-            parts[later, b + 1] = halves(value)
-        return carry
-
-    lax.fori_loop(0, ITERS, power, 0)
+            if k + 1 < ITERS:
+                parts[later, b + 1] = halves(value)
 
     def gram(c, carry):
         at = pl.ds(pl.multiple_of(c * 8, 8), 8)
@@ -110,6 +153,29 @@
     gram_ref[...] = jnp.broadcast_to(total[0:1][None], gram_ref.shape)
     for j in range(ITERS):
         own_ref[j] = fields[j, place_ref[0]]
+
+
+def krylov_call(place, starts, blocks, tiles=32):
+    rows, scenarios, segments = starts.shape
+    f32 = jnp.float32
+    padded_pairs = -(-len(PAIRS) * scenarios // 128) * 128 // scenarios
+    return call(
+        krylov_kernel,
+        (
+            jax.ShapeDtypeStruct((tiles, 1, padded_pairs * scenarios), f32),
+            jax.ShapeDtypeStruct((ITERS, scenarios, segments), f32),
+        ),
+        "svh",
+        scratch_shapes=[
+            pltpu.VMEM((BASIS, rows, scenarios, segments), f32),
+            pltpu.VMEM((rows, scenarios, segments), f32),
+            pltpu.VMEM((2, rows + 2, 2 * scenarios, segments), jnp.bfloat16),
+            pltpu.VMEM((rows, 4 * segments, segments), jnp.bfloat16),
+            pltpu.VMEM((padded_pairs, scenarios, segments), f32),
+            pltpu.VMEM(blocks.shape, f32),
+            pltpu.SemaphoreType.DMA((rows,)),
+        ],
+    )(place, starts, blocks)
 
 
 def solve_kernel(received_ref, fields_ref, out_ref, safe_ref):
@@ -249,36 +315,26 @@
     f32 = jnp.float32
     field_shape = jax.ShapeDtypeStruct((scenarios, segments), f32)
 
-    gate = jnp.stack([link[0], jnp.ones_like(link[0]), link[1]]).astype(f32)
-    own_blocks = jnp.concatenate(
-        [near.astype(f32) * gate[:, None, None], jacobi.astype(f32)[None]], axis=0
-    )
+    inputs = (targets, delays, link, near, jacobi, history, far_blocks)
+    spaces = [pltpu.SMEM] * 3 + [pltpu.VMEM] * 4
+    bucket, own_blocks = call(
+        front_kernel,
+        (
+            jax.ShapeDtypeStruct((tiles, scenarios, segments), f32),
+            jax.ShapeDtypeStruct((near.shape[0] + 1, segments, segments), f32),
+        ),
+        "h" * len(inputs),
+        scratch_shapes=[space(x.shape, x.dtype) for space, x in zip(spaces, inputs)]
+        + [pltpu.SemaphoreType.DMA((len(inputs) - 1,)), pltpu.SemaphoreType.DMA((4,))],
+    )(*inputs)
     all_blocks = lax.all_gather(own_blocks, "row")
-
-    bucket = call(
-        far_kernel, jax.ShapeDtypeStruct((tiles, scenarios, segments), f32), "ssvv"
-    )(targets, delays, history, far_blocks)
     received = lax.all_to_all(bucket, "tile", split_axis=0, concat_axis=0, tiled=True)
     initial = call(start_kernel, field_shape, "vvv")(received, voltage, jacobi)
 
     starts = lax.all_gather(initial, "row")
 
-    padded_pairs = -(-len(PAIRS) * scenarios // 128) * 128 // scenarios
-    width = padded_pairs * scenarios
-    gram, own = call(
-        krylov_kernel,
-        (
-            jax.ShapeDtypeStruct((tiles, 1, width), f32),
-            jax.ShapeDtypeStruct((ITERS, scenarios, segments), f32),
-        ),
-        "svv",
-        scratch_shapes=[
-            pltpu.VMEM((BASIS, rows, scenarios, segments), f32),
-            pltpu.VMEM((2, rows + 2, 2 * scenarios, segments), jnp.bfloat16),
-            pltpu.VMEM((rows, 4 * segments, segments), jnp.bfloat16),
-            pltpu.VMEM((padded_pairs, scenarios, segments), f32),
-        ],
-    )(lax.axis_index("row").astype(jnp.int32)[None], starts, all_blocks)
+    place = lax.axis_index("row").astype(jnp.int32)[None]
+    gram, own = krylov_call(place, starts, all_blocks, tiles)
     by_tile = lax.all_to_all(gram, "tile", split_axis=0, concat_axis=0, tiled=True)
     result, safe = call(
         solve_kernel,

time: 1230 us -> 106 us (0.09)
  blocking collectives: 1080 us -> 23.8 us
  starting transfers between devices: 43.2 us -> 18.8 us
  Pallas kernels: 28.6 us -> 12.9 us
    psum x11 -> x0, blocking collectives: 1050 us -> none  [the longest x5 483 us: stepwise_solve(): projections = lax.psum(local_dots, ('tile', 'row'))]
    ppermute x10 -> x0, starting transfers between devices: 24.6 us -> none  [neighbours(): return (lax.ppermute(field, 'row', up), lax.ppermute(field, 'row', down))]
    pallas_call x4, Pallas kernels: 28.6 us -> 12.9 us  [placed(): run(*(pltpu.with_memory_space_constraint(x, pltpu.HBM) if c == 'h' else x...]
  transfers between devices with their start and end apart: 13 -> 3, of which waited for: 7 -> 2; matrix products, arithmetic and copies ran while one was open for 0% -> 0% of each run, Pallas kernels for 0% -> 1%
where the time goes in v3:
time: 106 us; the launch traced here: 105 us
  waiting for transfers between devices  34 us (32%)
  blocking collectives  23.8 us (22%)
  starting transfers between devices  18.8 us (18%)
  between operations  14.1 us (13%)
  Pallas kernels  12.9 us (12%)
  local copies, waits for them, and re-layouts  1.39 us (1%)
    all_to_all x1, waiting for transfers between devices, per_device(): lax.all_to_all(bucket, 'tile', split_axis=0, concat_axis=0, tiled=True)  24.6 us
    all_gather x1, blocking collectives, per_device(): starts = lax.all_gather(initial, 'row')  23.8 us
    all_to_all x1, starting transfers between devices, per_device(): lax.all_to_all(bucket, 'tile', split_axis=0, concat_axis=0, tiled=True)  13.9 us
    pallas_call x4, Pallas kernels, placed(): run(*(pltpu.with_memory_space_constraint(x, pltpu.HBM) if c == 'h' else x...  12.9 us
    all_to_all x1, waiting for transfers between devices, per_device(): lax.all_to_all(gram, 'tile', split_axis=0, concat_axis=0, tiled=True)  9.33 us
    all_to_all x1, starting transfers between devices, per_device(): lax.all_to_all(gram, 'tile', split_axis=0, concat_axis=0, tiled=True)  4.9 us
  transfers between devices with their start and end apart: 3, of which 2 were waited for; matrix products, arithmetic and copies ran while one was open for 0% of the time, Pallas kernels for 1%

profile of v3, /device:TPU:1, one launch (start us, length us, event | category | flops | bytes accessed | tf_op | source)
XLA Modules:
  0.0 105.2 jit_solution(1487829255172353246)
XLA Ops:
  6.5 0.0 all-gather.4.cloned.1.call-start
  6.5 3.3 %shard_map.84 = (f32[32,64,128]{2,1,0:T(8,128)}, f32[4,128,128]{2,1,0:T(8,128)}) custom-call(s32[32]{0:T(128)} %bitcast.248, s32[32]{0:T(128)} %bitcast.249, s32[2]{0:T(128)} %bitcast.250, bf16[3,128,128]{2,1,0:T(8,128)(2,1)} %bitcast.227, bf16[128,128]{1,0:T(8,128)(2,1)} %bitcast.229, bf16[32,64,128]{2,1,0:T(8,128)(2,1)} %bitcast.233, ...), custom_call_target="tpu_custom_call" | custom-call | tf_op jit(solution)/shard_map/pallas_call | solution.py:27
  9.8 0.0 all-gather.4.cloned.1.call-update
  9.8 0.0 copy-start.1
  9.9 0.0 copy-start.2
  9.9 0.0 copy-start.3
  9.9 13.9 %all-to-all-start = ((f32[32,64,128]{2,1,0:T(8,128)}), f32[32,64,128]{2,1,0:T(8,128)S(1)}, u32[]{:S(2)}, u32[]{:S(2)}) async-start(f32[32,64,128]{2,1,0:T(8,128)} %get-tuple-element.29), calls=%async_computation | async-start | bytes 2097152 | tf_op jit(solution)/shard_map/all_to_all | solution.py:331
  23.7 24.6 %all-to-all-done.received_ref = f32[32,64,128]{2,1,0:T(8,128)S(1)} async-done(((f32[32,64,128]{2,1,0:T(8,128)}), f32[32,64,128]{2,1,0:T(8,128)S(1)}, u32[]{:S(2)}, u32[]{:S(2)}) %all-to-all-start) | async-done | bytes 1048608 | tf_op jit(solution)/shard_map/all_to_all | solution.py:331
  48.4 0.0 copy-start
  48.4 0.8 copy-done
  49.1 0.9 shard_map.85
  50.1 23.8 %all-gather = f32[1024,128]{1,0:T(8,128)S(1)} all-gather(f32[64,128]{1,0:T(8,128)S(1)} %shard_map.85), channel_id=2, replica_groups=mesh['tile'=32,'row'=16] {'row'}, dimensions={0}, use_global_device_ids=true | all-gather | bytes 557056 | tf_op jit(solution)/shard_map/all_gather | solution.py:334
  73.9 0.0 all-gather.4.cloned.1.call-done
  73.9 7.3 %shard_map.86 = (f32[32,1,1408]{2,1,0:T(1,128)}, f32[5,64,128]{2,1,0:T(8,128)S(1)}) custom-call(s32[1]{0:T(128)} %bitcast.35.place_ref, f32[16,64,128]{2,1,0:T(8,128)S(1)} %bitcast.224, f32[16,4,128,128]{3,2,1,0:T(8,128)} %bitcast.226), custom_call_target="tpu_custom_call" | custom-call | tf_op jit(solution)/shard_map/pallas_call | solution.py:27
  81.2 4.9 %all-to-all-start.1 = ((f32[32,1,1408]{2,1,0:T(1,128)}), f32[32,1,1408]{2,1,0:T(1,128)S(1)}, u32[]{:S(2)}, u32[]{:S(2)}) async-start(f32[32,1,1408]{2,1,0:T(1,128)} %get-tuple-element.31), calls=%async_computation.1 | async-start | bytes 360448 | tf_op jit(solution)/shard_map/all_to_all | solution.py:338
  86.1 9.3 %all-to-all-done.1.received_ref = f32[32,1,1408]{2,1,0:T(1,128)S(1)} async-done(((f32[32,1,1408]{2,1,0:T(1,128)}), f32[32,1,1408]{2,1,0:T(1,128)S(1)}, u32[]{:S(2)}, u32[]{:S(2)}) %all-to-all-start.1) | async-done | bytes 180256 | tf_op jit(solution)/shard_map/all_to_all | solution.py:338
  95.4 1.4 %shard_map.87 = (f32[64,128]{1,0:T(8,128)S(1)}, f32[1]{0:T(128)}) custom-call(f32[32,1,1408]{2,1,0:T(1,128)S(1)} %all-to-all-done.1.received_ref, f32[5,64,128]{2,1,0:T(8,128)S(1)} %get-tuple-element.32.fields_ref), custom_call_target="tpu_custom_call" | custom-call | tf_op jit(solution)/shard_map/pallas_call | solution.py:27
  97.5 0.0 copy-done.1
  97.5 0.0 copy-done.2
  97.5 0.0 copy-done.3
  97.5 0.2 conditional.1
  97.8 0.0 copy-start.4
  97.8 0.6 copy-done.4
Async XLA Ops:
  6.5 67.4 %all-gather.4.cloned.1.call-start = ((), (), s32[]{:S(2)}) async-start(), calls=%async_computation.2 | async-start | bytes 4456448 | tf_op jit(solution)/shard_map/all_gather | solution.py:330
  9.8 87.7 %copy-start.1 = (bf16[1,1,3,128,128]{4,3,2,1,0:T(8,128)(2,1)S(1)}, bf16[1,1,3,128,128]{4,3,2,1,0:T(8,128)(2,1)}, u32[]{:S(2)}) copy-start(bf16[1,1,3,128,128]{4,3,2,1,0:T(8,128)(2,1)} %param.15) | copy-start | bytes 294916
  9.9 87.7 %copy-start.2 = (bf16[1,1,128,128]{3,2,1,0:T(8,128)(2,1)S(1)}, bf16[1,1,128,128]{3,2,1,0:T(8,128)(2,1)}, u32[]{:S(2)}) copy-start(bf16[1,1,128,128]{3,2,1,0:T(8,128)(2,1)} %param.17) | copy-start | bytes 98308
  9.9 87.7 %copy-start.3 = (s32[1,1,2]{2,1,0:T(1,128)S(1)}, s32[1,1,2]{2,1,0:T(1,128)}, u32[]{:S(2)}) copy-start(s32[1,1,2]{2,1,0:T(1,128)} %param.16) | copy-start | bytes 28
  9.9 38.5 %all-to-all-start = ((f32[32,64,128]{2,1,0:T(8,128)}), f32[32,64,128]{2,1,0:T(8,128)S(1)}, u32[]{:S(2)}, u32[]{:S(2)}) async-start(f32[32,64,128]{2,1,0:T(8,128)} %get-tuple-element.29), calls=%async_computation | async-start | bytes 2097152 | tf_op jit(solution)/shard_map/all_to_all | solution.py:331
  48.4 0.8 copy-start
  81.2 14.2 %all-to-all-start.1 = ((f32[32,1,1408]{2,1,0:T(1,128)}), f32[32,1,1408]{2,1,0:T(1,128)S(1)}, u32[]{:S(2)}, u32[]{:S(2)}) async-start(f32[32,1,1408]{2,1,0:T(1,128)} %get-tuple-element.31), calls=%async_computation.1 | async-start | bytes 360448 | tf_op jit(solution)/shard_map/all_to_all | solution.py:338
  97.8 0.6 copy-start.4
Sparse Core Ops, SparseCore 0:
  10.0 50.6 all-gather.3

commit v4 on v3

--- a/solution.py
+++ b/solution.py
@@ -9,8 +9,10 @@
 BASIS = ITERS + 1
 PAIRS = [(i, j) for i in range(BASIS) for j in range(i, BASIS)]
 PIVOT_SHARE = 0.02
-VMEM_BYTES = 48 * 1024 * 1024
+VMEM_BYTES = 20 * 1024 * 1024
 PRECISE = lax.Precision.HIGHEST
+CORES = 2
+CHIPS = 8
 
 
 def call(kernel, out_shape, in_spaces, **kwargs):
@@ -42,15 +44,24 @@
     return both[:rows] + both[rows:]
 
 
+def ring_steps():
+    steps = [0]
+    for distance in range(1, CHIPS // 2 + 1):
+        steps += [distance] if distance == CHIPS // 2 else [distance, -distance]
+    return steps
+
+
 def front_kernel(
-    target_hbm, delay_hbm, link_hbm, near_hbm, jacobi_hbm, history_hbm, blocks_hbm, bucket_ref, own_ref,
-    target_ref, delay_ref, link_ref, near_ref, jacobi_ref, history_ref, blocks_ref, sems, block_sems,
+    tile_ref, target_hbm, delay_hbm, link_hbm, near_hbm, jacobi_hbm, voltage_hbm, history_hbm, blocks_hbm,
+    bucket_ref, own_ref, kept_ref,
+    target_ref, delay_ref, link_ref, near_ref, jacobi_ref, voltage_ref, history_ref, blocks_ref, sems, block_sems,
 ):
     entries, chunks = blocks_ref.shape[0], block_sems.shape[0]
     step = entries // chunks
     pairs = [
         (target_hbm, target_ref), (delay_hbm, delay_ref), (link_hbm, link_ref),
-        (near_hbm, near_ref), (jacobi_hbm, jacobi_ref), (history_hbm, history_ref),
+        (near_hbm, near_ref), (jacobi_hbm, jacobi_ref), (voltage_hbm, voltage_ref),
+        (history_hbm, history_ref),
     ]
     copies = [pltpu.make_async_copy(a, b, sems.at[i]) for i, (a, b) in enumerate(pairs)]
     slabs = [
@@ -64,9 +75,14 @@
     bucket_ref[...] = jnp.zeros_like(bucket_ref)
     for copy in copies:
         copy.wait()
+    jacobi = jacobi_ref[...]
+    kept_ref[...] = jacobi
     for side, gate in enumerate((link_ref[0], 1, link_ref[1])):
-        own_ref[side] = near_ref[side].astype(jnp.float32) * jnp.float32(gate)
-    own_ref[near_ref.shape[0]] = jacobi_ref[...].astype(jnp.float32)
+        near = near_ref[side]
+        product = jnp.dot(near, jacobi, preferred_element_type=jnp.float32)
+        merged = near.astype(jnp.float32) + product
+        own_ref[side] = merged + jacobi.astype(jnp.float32) if side == 1 else merged * gate.astype(jnp.float32)
+    bucket_ref[tile_ref[0]] = -voltage_ref[...]
     for c in range(chunks):
         slabs[c].wait()
         for entry in range(c * step, (c + 1) * step):
@@ -79,19 +95,17 @@
             bucket_ref[target] = bucket_ref[target] + product
 
 
-def start_kernel(received_ref, voltage_ref, jacobi_ref, out_ref):
-    right_side = voltage_ref[...] - jnp.sum(received_ref[...], axis=0)
+def start_kernel(received_ref, jacobi_ref, out_ref):
+    right_side = -jnp.sum(received_ref[...], axis=0)
     out_ref[...] = right_side + split_dot(right_side, jacobi_ref[...])
 
 
-def krylov_kernel(
-    place_ref, start_ref, blocks_hbm, gram_ref, own_ref, fields, nears, parts, blocks, sums, staged, sems
-):
+def krylov_kernel(place_ref, start_ref, *refs):
+    chips = CHIPS
+    piece_refs = refs[:chips]
+    gram_ref, own_ref, fields, parts, highs, lows, sums = refs[chips:]
     rows, scenarios, segments = start_ref.shape
-    depth, group = blocks.shape[1], rows // 4
-    copies = [pltpu.make_async_copy(blocks_hbm.at[b], staged.at[b], sems.at[b]) for b in range(rows)]
-    for copy in copies:
-        copy.start()
+    cores = rows // chips
     zero_part = jnp.zeros(parts.shape[2:], parts.dtype)
     for side in range(2):
         parts[side, 0] = zero_part
@@ -100,35 +114,28 @@
     def halves(value):
         high = value.astype(jnp.bfloat16)
         low = (value - high.astype(jnp.float32)).astype(jnp.bfloat16)
-        return jnp.concatenate([high, low], axis=0)
-
+        return high, low
+
+    chip, core = lax.div(place_ref[0], cores), lax.rem(place_ref[0], cores)
+    for piece_ref, steps in zip(piece_refs, ring_steps()):
+        source = lax.rem(chip + (2 * core - 1) * steps + chips, chips)
+        for core_there in range(cores):
+            b = source * cores + core_there
+            highs[b], lows[b] = halves(piece_ref[core_there].reshape(highs.shape[1:]))
     for b in range(rows):
         fields[0, b] = start_ref[b]
-        parts[0, b + 1] = halves(start_ref[b])
+        parts[0, b + 1] = jnp.concatenate(halves(start_ref[b]), axis=0)
 
     for k in range(ITERS):
         now, later = k % 2, (k + 1) % 2
         for b in range(rows):
-            if k == 0 and b % group == 0:
-                for c in range(b, b + group):
-                    copies[c].wait()
-                for c in range(b, b + group):
-                    blocks[c] = staged[c].reshape(depth, segments).astype(jnp.bfloat16)
             around = jnp.concatenate([parts[now, b], parts[now, b + 1], parts[now, b + 2]], axis=1)
-            near = jnp.dot(
-                around, blocks[b, : depth - segments], preferred_element_type=jnp.float32
-            )
-            nears[b] = near[:scenarios] + near[scenarios:]
-        for b in range(rows):
-            last = jnp.dot(
-                halves(fields[k, b] + nears[b]),
-                blocks[b, depth - segments :],
-                preferred_element_type=jnp.float32,
-            )
-            value = nears[b] + (last[:scenarios] + last[scenarios:])
+            main = jnp.dot(around, highs[b], preferred_element_type=jnp.float32)
+            rest = jnp.dot(around[:scenarios], lows[b], preferred_element_type=jnp.float32)
+            value = main[:scenarios] + (main[scenarios:] + rest)
             fields[k + 1, b] = value
             if k + 1 < ITERS:
-                parts[later, b + 1] = halves(value)
+                parts[later, b + 1] = jnp.concatenate(halves(value), axis=0)
 
     def gram(c, carry):
         at = pl.ds(pl.multiple_of(c * 8, 8), 8)
@@ -155,7 +162,7 @@
         own_ref[j] = fields[j, place_ref[0]]
 
 
-def krylov_call(place, starts, blocks, tiles=32):
+def krylov_call(place, starts, pieces, tiles=32):
     rows, scenarios, segments = starts.shape
     f32 = jnp.float32
     padded_pairs = -(-len(PAIRS) * scenarios // 128) * 128 // scenarios
@@ -165,17 +172,15 @@
             jax.ShapeDtypeStruct((tiles, 1, padded_pairs * scenarios), f32),
             jax.ShapeDtypeStruct((ITERS, scenarios, segments), f32),
         ),
-        "svh",
+        "sv" + "v" * len(pieces),
         scratch_shapes=[
             pltpu.VMEM((BASIS, rows, scenarios, segments), f32),
-            pltpu.VMEM((rows, scenarios, segments), f32),
             pltpu.VMEM((2, rows + 2, 2 * scenarios, segments), jnp.bfloat16),
-            pltpu.VMEM((rows, 4 * segments, segments), jnp.bfloat16),
+            pltpu.VMEM((rows, 3 * segments, segments), jnp.bfloat16),
+            pltpu.VMEM((rows, 3 * segments, segments), jnp.bfloat16),
             pltpu.VMEM((padded_pairs, scenarios, segments), f32),
-            pltpu.VMEM(blocks.shape, f32),
-            pltpu.SemaphoreType.DMA((rows,)),
         ],
-    )(place, starts, blocks)
+    )(place, starts, *pieces)
 
 
 def solve_kernel(received_ref, fields_ref, out_ref, safe_ref):
@@ -230,6 +235,21 @@
     safe_ref[0] = jnp.min(safe)
 
 
+def gather_blocks(own):
+    size = CHIPS * CORES
+    pairs = [[CORES * chip + core for core in range(CORES)] for chip in range(CHIPS)]
+    ring = [(i, (i + (CORES if i % CORES == 0 else -CORES)) % size) for i in range(size)]
+    swap = [(i, i ^ 1) for i in range(size)]
+    piece = lax.all_gather(own, "row", axis_index_groups=pairs)
+    pieces = [piece]
+    for distance in range(1, CHIPS // 2 + 1):
+        piece = lax.ppermute(piece, "row", ring)
+        pieces.append(piece)
+        if distance < CHIPS // 2:
+            pieces.append(lax.ppermute(piece, "row", swap))
+    return pieces
+
+
 def neighbours(field):
     size = lax.axis_size("row")
     up = [(i, i + 1) for i in range(size - 1)]
@@ -315,26 +335,25 @@
     f32 = jnp.float32
     field_shape = jax.ShapeDtypeStruct((scenarios, segments), f32)
 
-    inputs = (targets, delays, link, near, jacobi, history, far_blocks)
-    spaces = [pltpu.SMEM] * 3 + [pltpu.VMEM] * 4
-    bucket, own_blocks = call(
+    inputs = (targets, delays, link, near, jacobi, voltage, history, far_blocks)
+    spaces = [pltpu.SMEM] * 3 + [pltpu.VMEM] * 5
+    bucket, own_blocks, jacobi_kept = call(
         front_kernel,
         (
             jax.ShapeDtypeStruct((tiles, scenarios, segments), f32),
-            jax.ShapeDtypeStruct((near.shape[0] + 1, segments, segments), f32),
+            jax.ShapeDtypeStruct(near.shape, f32),
+            jax.ShapeDtypeStruct(jacobi.shape, jacobi.dtype),
         ),
-        "h" * len(inputs),
+        "s" + "h" * len(inputs),
         scratch_shapes=[space(x.shape, x.dtype) for space, x in zip(spaces, inputs)]
         + [pltpu.SemaphoreType.DMA((len(inputs) - 1,)), pltpu.SemaphoreType.DMA((4,))],
-    )(*inputs)
-    all_blocks = lax.all_gather(own_blocks, "row")
+    )(lax.axis_index("tile").astype(jnp.int32)[None], *inputs)
     received = lax.all_to_all(bucket, "tile", split_axis=0, concat_axis=0, tiled=True)
-    initial = call(start_kernel, field_shape, "vvv")(received, voltage, jacobi)
-
+    pieces = gather_blocks(own_blocks)
+    initial = call(start_kernel, field_shape, "vv")(received, jacobi_kept)
     starts = lax.all_gather(initial, "row")
-
     place = lax.axis_index("row").astype(jnp.int32)[None]
-    gram, own = krylov_call(place, starts, all_blocks, tiles)
+    gram, own = krylov_call(place, starts, pieces, tiles)
     by_tile = lax.all_to_all(gram, "tile", split_axis=0, concat_axis=0, tiled=True)
     result, safe = call(
         solve_kernel,

time: 106 us -> 109 us (1.028)
  the two profiles are of different devices: /device:TPU:1 before, /device:TPU:24 now
where the time goes in v4:
time: 109 us
  starting transfers between devices  50.7 us (47%)
  waiting for transfers between devices  23.2 us (21%)
  blocking collectives  20.1 us (18%)
  Pallas kernels  12.8 us (12%)
  local copies, waits for them, and re-layouts  1.25 us (1%)
    ppermute x4, starting transfers between devices, gather_blocks(): piece = lax.ppermute(piece, 'row', ring)  21.5 us
    all_gather x1, blocking collectives, per_device(): starts = lax.all_gather(initial, 'row')  18 us
    all_to_all x1, starting transfers between devices, per_device(): lax.all_to_all(bucket, 'tile', split_axis=0, concat_axis=0, tiled=True)  13.2 us
    pallas_call x4, Pallas kernels, placed(): run(*(pltpu.with_memory_space_constraint(x, pltpu.HBM) if c == 'h' else x...  12.8 us
    all_to_all x1, waiting for transfers between devices, per_device(): lax.all_to_all(gram, 'tile', split_axis=0, concat_axis=0, tiled=True)  11.7 us
    ppermute x4, waiting for transfers between devices, gather_blocks(): piece = lax.ppermute(piece, 'row', ring)  11.5 us
    all_to_all x1, starting transfers between devices, per_device(): lax.all_to_all(gram, 'tile', split_axis=0, concat_axis=0, tiled=True)  9.79 us
    ppermute x3, starting transfers between devices, gather_blocks(): pieces.append(lax.ppermute(piece, 'row', swap))  6.24 us
  transfers between devices with their start and end apart: 9, of which 4 were waited for; matrix products, arithmetic and copies ran while one was open for 0% of the time, Pallas kernels for 0%

profile of v4, /device:TPU:24, one launch (start us, length us, event | category | flops | bytes accessed | tf_op | source)
XLA Modules:
  0.0 108.8 jit_solution(9784375365660825975)
XLA Ops:
  0.0 3.5 %shard_map.84 = (f32[32,64,128]{2,1,0:T(8,128)}, f32[3,128,128]{2,1,0:T(8,128)S(1)}, bf16[128,128]{1,0:T(8,128)(2,1)S(1)}) custom-call(s32[1]{0:T(128)} %bitcast.36.tile_ref, s32[32]{0:T(128)} %bitcast.249, s32[32]{0:T(128)} %bitcast.250, s32[2]{0:T(128)} %bitcast.251, bf16[3,128,128]{2,1,0:T(8,128)(2,1)} %bitcast.228, bf16[128,128]{1,0:T(8,128)(2,1)} %bitcast.230, ...), custom_call_target="tpu_custom_call" | custom-call | tf_op jit(solution)/shard_map/pallas_call | solution.py:29
  3.5 13.2 %all-to-all-start = ((f32[32,64,128]{2,1,0:T(8,128)}), f32[32,64,128]{2,1,0:T(8,128)S(1)}, u32[]{:S(2)}, u32[]{:S(2)}) async-start(f32[32,64,128]{2,1,0:T(8,128)} %get-tuple-element.30), calls=%async_computation | async-start | bytes 2097152 | tf_op jit(solution)/shard_map/all_to_all | solution.py:351
  16.7 2.1 %all-gather.1 = f32[6,128,128]{2,1,0:T(8,128)S(1)} all-gather(f32[3,128,128]{2,1,0:T(8,128)S(1)} %get-tuple-element.32), channel_id=3, replica_groups={{0,1},{2,3},{4,5},{6,7},{8,9},{10,11},{12,13},{14,15},{16,17},{18,19},{..., dimensions={0}, use_global_device_ids=true | all-gather | bytes 589824 | tf_op jit(solution)/shard_map/all_gather | solution.py:243
  18.8 4.7 %collective-permute-start.10 = (f32[2,3,128,128]{3,2,1,0:T(8,128)S(1)}, f32[2,3,128,128]{3,2,1,0:T(8,128)S(1)}, u32[]{:S(2)}, u32[]{:S(2)}) collective-permute-start(f32[2,3,128,128]{3,2,1,0:T(8,128)S(1)} %bitcast.226), channel_id=1, source_target_pairs={{0,2},{1,15},{2,4},{3,1},{4,6},{5,3},{6,8},{7,5},{8,10},{9,7},{10,... | collective-permute-start | bytes 1179656 | tf_op jit(solution)/shard_map/ppermute | solution.py:246
  23.5 5.3 %collective-permute-done.10.refs_1_ = f32[2,3,128,128]{3,2,1,0:T(8,128)S(1)} collective-permute-done((f32[2,3,128,128]{3,2,1,0:T(8,128)S(1)}, f32[2,3,128,128]{3,2,1,0:T(8,128)S(1)}, u32[]{:S(2)}, u32[]{:S(2)}) %collective-permute-start.10) | collective-permute-done | bytes 393248 | tf_op jit(solution)/shard_map/ppermute | solution.py:246
  28.7 5.6 %collective-permute-start.12 = (f32[2,3,128,128]{3,2,1,0:T(8,128)S(1)}, f32[2,3,128,128]{3,2,1,0:T(8,128)S(1)}, u32[]{:S(2)}, u32[]{:S(2)}) collective-permute-start(f32[2,3,128,128]{3,2,1,0:T(8,128)S(1)} %collective-permute-done.10.refs_1_), channel_id=1, source_target_pairs={{0,2},{1,15},{2,4},{3,1},{4,6},{5,3},{6,8},{7,5},{8,10},{9,7},{10,... | collective-permute-start | bytes 1179656 | tf_op jit(solution)/shard_map/ppermute | solution.py:246
  34.3 5.3 %collective-permute-done.12.refs_3_ = f32[2,3,128,128]{3,2,1,0:T(8,128)S(1)} collective-permute-done((f32[2,3,128,128]{3,2,1,0:T(8,128)S(1)}, f32[2,3,128,128]{3,2,1,0:T(8,128)S(1)}, u32[]{:S(2)}, u32[]{:S(2)}) %collective-permute-start.12) | collective-permute-done | bytes 393248 | tf_op jit(solution)/shard_map/ppermute | solution.py:246
  39.6 5.6 %collective-permute-start.14 = (f32[2,3,128,128]{3,2,1,0:T(8,128)S(1)}, f32[2,3,128,128]{3,2,1,0:T(8,128)S(1)}, u32[]{:S(2)}, u32[]{:S(2)}) collective-permute-start(f32[2,3,128,128]{3,2,1,0:T(8,128)S(1)} %collective-permute-done.12.refs_3_), channel_id=1, source_target_pairs={{0,2},{1,15},{2,4},{3,1},{4,6},{5,3},{6,8},{7,5},{8,10},{9,7},{10,... | collective-permute-start | bytes 1179656 | tf_op jit(solution)/shard_map/ppermute | solution.py:246
  45.2 1.9 %collective-permute-start.11 = (f32[2,3,128,128]{3,2,1,0:T(8,128)S(1)}, f32[2,3,128,128]{3,2,1,0:T(8,128)S(1)}, u32[]{:S(2)}, u32[]{:S(2)}) collective-permute-start(f32[2,3,128,128]{3,2,1,0:T(8,128)S(1)} %collective-permute-done.10.refs_1_), channel_id=1, source_target_pairs={{0,1},{1,0},{2,3},{3,2},{4,5},{5,4},{6,7},{7,6},{8,9},{9,8},{10,11... | collective-permute-start | bytes 1179656 | tf_op jit(solution)/shard_map/ppermute | solution.py:249
  47.1 2.4 %collective-permute-start.13 = (f32[2,3,128,128]{3,2,1,0:T(8,128)S(1)}, f32[2,3,128,128]{3,2,1,0:T(8,128)S(1)}, u32[]{:S(2)}, u32[]{:S(2)}) collective-permute-start(f32[2,3,128,128]{3,2,1,0:T(8,128)S(1)} %collective-permute-done.12.refs_3_), channel_id=1, source_target_pairs={{0,1},{1,0},{2,3},{3,2},{4,5},{5,4},{6,7},{7,6},{8,9},{9,8},{10,11... | collective-permute-start | bytes 1179656 | tf_op jit(solution)/shard_map/ppermute | solution.py:249
  49.5 0.9 collective-permute-done.14.refs_5_
  50.5 1.9 %collective-permute-start.15 = (f32[2,3,128,128]{3,2,1,0:T(8,128)S(1)}, f32[2,3,128,128]{3,2,1,0:T(8,128)}, u32[]{:S(2)}, u32[]{:S(2)}) collective-permute-start(f32[2,3,128,128]{3,2,1,0:T(8,128)S(1)} %collective-permute-done.14.refs_5_), channel_id=1, source_target_pairs={{0,1},{1,0},{2,3},{3,2},{4,5},{5,4},{6,7},{7,6},{8,9},{9,8},{10,11... | collective-permute-start | bytes 1179656 | tf_op jit(solution)/shard_map/ppermute | solution.py:249
  52.4 5.6 %collective-permute-start.16 = (f32[2,3,128,128]{3,2,1,0:T(8,128)S(1)}, f32[2,3,128,128]{3,2,1,0:T(8,128)}, u32[]{:S(2)}, u32[]{:S(2)}) collective-permute-start(f32[2,3,128,128]{3,2,1,0:T(8,128)S(1)} %collective-permute-done.14.refs_5_), channel_id=1, source_target_pairs={{0,2},{1,15},{2,4},{3,1},{4,6},{5,3},{6,8},{7,5},{8,10},{9,7},{10,... | collective-permute-start | bytes 1179656 | tf_op jit(solution)/shard_map/ppermute | solution.py:246
  58.0 0.0 all-to-all-done.received_ref
  58.0 0.2 shard_map.85
  58.2 18.0 %all-gather = f32[1024,128]{1,0:T(8,128)S(1)} all-gather(f32[64,128]{1,0:T(8,128)S(1)} %shard_map.85), channel_id=2, replica_groups=mesh['tile'=32,'row'=16] {'row'}, dimensions={0}, use_global_device_ids=true | all-gather | bytes 557056 | tf_op jit(solution)/shard_map/all_gather | solution.py:354
  76.2 0.0 collective-permute-done.11.refs_2_
  76.3 7.7 %shard_map.86 = (f32[32,1,1408]{2,1,0:T(1,128)}, f32[5,64,128]{2,1,0:T(8,128)S(1)}) custom-call(s32[1]{0:T(128)} %bitcast.35.place_ref, f32[16,64,128]{2,1,0:T(8,128)S(1)} %bitcast.225, f32[2,3,128,128]{3,2,1,0:T(8,128)S(1)} %bitcast.227, f32[2,3,128,128]{3,2,1,0:T(8,128)S(1)} %collective-permute-done.10.refs_1_, ...), custom_call_target="tpu_custom_call" | custom-call | tf_op jit(solution)/shard_map/pallas_call | solution.py:29
  84.0 9.8 %all-to-all-start.1 = ((f32[32,1,1408]{2,1,0:T(1,128)}), f32[32,1,1408]{2,1,0:T(1,128)S(1)}, u32[]{:S(2)}, u32[]{:S(2)}) async-start(f32[32,1,1408]{2,1,0:T(1,128)} %get-tuple-element.33), calls=%async_computation.1 | async-start | bytes 360448 | tf_op jit(solution)/shard_map/all_to_all | solution.py:357
  93.8 11.7 %all-to-all-done.1.received_ref = f32[32,1,1408]{2,1,0:T(1,128)S(1)} async-done(((f32[32,1,1408]{2,1,0:T(1,128)}), f32[32,1,1408]{2,1,0:T(1,128)S(1)}, u32[]{:S(2)}, u32[]{:S(2)}) %all-to-all-start.1) | async-done | bytes 180256 | tf_op jit(solution)/shard_map/all_to_all | solution.py:357
  105.4 1.4 %shard_map.87 = (f32[64,128]{1,0:T(8,128)S(1)}, f32[1]{0:T(128)}) custom-call(f32[32,1,1408]{2,1,0:T(1,128)S(1)} %all-to-all-done.1.received_ref, f32[5,64,128]{2,1,0:T(8,128)S(1)} %get-tuple-element.34.fields_ref), custom_call_target="tpu_custom_call" | custom-call | tf_op jit(solution)/shard_map/pallas_call | solution.py:29
  107.5 0.0 copy-start.2
  107.5 0.6 copy-done.2
  108.2 0.6 copy-done.3
  (9 shorter events, 0.0 us)
Async XLA Ops:
  3.5 54.5 %all-to-all-start = ((f32[32,64,128]{2,1,0:T(8,128)}), f32[32,64,128]{2,1,0:T(8,128)S(1)}, u32[]{:S(2)}, u32[]{:S(2)}) async-start(f32[32,64,128]{2,1,0:T(8,128)} %get-tuple-element.30), calls=%async_computation | async-start | bytes 2097152 | tf_op jit(solution)/shard_map/all_to_all | solution.py:351
  18.8 10.0 %collective-permute-start.10 = (f32[2,3,128,128]{3,2,1,0:T(8,128)S(1)}, f32[2,3,128,128]{3,2,1,0:T(8,128)S(1)}, u32[]{:S(2)}, u32[]{:S(2)}) collective-permute-start(f32[2,3,128,128]{3,2,1,0:T(8,128)S(1)} %bitcast.226), channel_id=1, source_target_pairs={{0,2},{1,15},{2,4},{3,1},{4,6},{5,3},{6,8},{7,5},{8,10},{9,7},{10,... | collective-permute-start | bytes 1179656 | tf_op jit(solution)/shard_map/ppermute | solution.py:246
  28.7 10.9 %collective-permute-start.12 = (f32[2,3,128,128]{3,2,1,0:T(8,128)S(1)}, f32[2,3,128,128]{3,2,1,0:T(8,128)S(1)}, u32[]{:S(2)}, u32[]{:S(2)}) collective-permute-start(f32[2,3,128,128]{3,2,1,0:T(8,128)S(1)} %collective-permute-done.10.refs_1_), channel_id=1, source_target_pairs={{0,2},{1,15},{2,4},{3,1},{4,6},{5,3},{6,8},{7,5},{8,10},{9,7},{10,... | collective-permute-start | bytes 1179656 | tf_op jit(solution)/shard_map/ppermute | solution.py:246
  39.6 10.9 %collective-permute-start.14 = (f32[2,3,128,128]{3,2,1,0:T(8,128)S(1)}, f32[2,3,128,128]{3,2,1,0:T(8,128)S(1)}, u32[]{:S(2)}, u32[]{:S(2)}) collective-permute-start(f32[2,3,128,128]{3,2,1,0:T(8,128)S(1)} %collective-permute-done.12.refs_3_), channel_id=1, source_target_pairs={{0,2},{1,15},{2,4},{3,1},{4,6},{5,3},{6,8},{7,5},{8,10},{9,7},{10,... | collective-permute-start | bytes 1179656 | tf_op jit(solution)/shard_map/ppermute | solution.py:246
  45.2 31.0 %collective-permute-start.11 = (f32[2,3,128,128]{3,2,1,0:T(8,128)S(1)}, f32[2,3,128,128]{3,2,1,0:T(8,128)S(1)}, u32[]{:S(2)}, u32[]{:S(2)}) collective-permute-start(f32[2,3,128,128]{3,2,1,0:T(8,128)S(1)} %collective-permute-done.10.refs_1_), channel_id=1, source_target_pairs={{0,1},{1,0},{2,3},{3,2},{4,5},{5,4},{6,7},{7,6},{8,9},{9,8},{10,11... | collective-permute-start | bytes 1179656 | tf_op jit(solution)/shard_map/ppermute | solution.py:249
  47.1 29.1 %collective-permute-start.13 = (f32[2,3,128,128]{3,2,1,0:T(8,128)S(1)}, f32[2,3,128,128]{3,2,1,0:T(8,128)S(1)}, u32[]{:S(2)}, u32[]{:S(2)}) collective-permute-start(f32[2,3,128,128]{3,2,1,0:T(8,128)S(1)} %collective-permute-done.12.refs_3_), channel_id=1, source_target_pairs={{0,1},{1,0},{2,3},{3,2},{4,5},{5,4},{6,7},{7,6},{8,9},{9,8},{10,11... | collective-permute-start | bytes 1179656 | tf_op jit(solution)/shard_map/ppermute | solution.py:249
  50.5 25.8 %collective-permute-start.15 = (f32[2,3,128,128]{3,2,1,0:T(8,128)S(1)}, f32[2,3,128,128]{3,2,1,0:T(8,128)}, u32[]{:S(2)}, u32[]{:S(2)}) collective-permute-start(f32[2,3,128,128]{3,2,1,0:T(8,128)S(1)} %collective-permute-done.14.refs_5_), channel_id=1, source_target_pairs={{0,1},{1,0},{2,3},{3,2},{4,5},{5,4},{6,7},{7,6},{8,9},{9,8},{10,11... | collective-permute-start | bytes 1179656 | tf_op jit(solution)/shard_map/ppermute | solution.py:249
  52.4 23.9 %collective-permute-start.16 = (f32[2,3,128,128]{3,2,1,0:T(8,128)S(1)}, f32[2,3,128,128]{3,2,1,0:T(8,128)}, u32[]{:S(2)}, u32[]{:S(2)}) collective-permute-start(f32[2,3,128,128]{3,2,1,0:T(8,128)S(1)} %collective-permute-done.14.refs_5_), channel_id=1, source_target_pairs={{0,2},{1,15},{2,4},{3,1},{4,6},{5,3},{6,8},{7,5},{8,10},{9,7},{10,... | collective-permute-start | bytes 1179656 | tf_op jit(solution)/shard_map/ppermute | solution.py:246
  84.0 21.5 %all-to-all-start.1 = ((f32[32,1,1408]{2,1,0:T(1,128)}), f32[32,1,1408]{2,1,0:T(1,128)S(1)}, u32[]{:S(2)}, u32[]{:S(2)}) async-start(f32[32,1,1408]{2,1,0:T(1,128)} %get-tuple-element.33), calls=%async_computation.1 | async-start | bytes 360448 | tf_op jit(solution)/shard_map/all_to_all | solution.py:357
  105.4 2.1 %copy-start = (bf16[1,1,3,128,128]{4,3,2,1,0:T(8,128)(2,1)S(1)}, bf16[1,1,3,128,128]{4,3,2,1,0:T(8,128)(2,1)}, u32[]{:S(2)}) copy-start(bf16[1,1,3,128,128]{4,3,2,1,0:T(8,128)(2,1)} %param.15) | copy-start | bytes 294916
  105.4 2.1 %copy-start.1 = (bf16[1,1,128,128]{3,2,1,0:T(8,128)(2,1)S(1)}, bf16[1,1,128,128]{3,2,1,0:T(8,128)(2,1)}, u32[]{:S(2)}) copy-start(bf16[1,1,128,128]{3,2,1,0:T(8,128)(2,1)} %param.17) | copy-start | bytes 98308
  107.5 0.7 copy-start.2
  108.2 0.6 copy-start.3

commit v5 on v4

--- a/solution.py
+++ b/solution.py
@@ -51,29 +51,15 @@
     return steps
 
 
-def front_kernel(
-    tile_ref, target_hbm, delay_hbm, link_hbm, near_hbm, jacobi_hbm, voltage_hbm, history_hbm, blocks_hbm,
-    bucket_ref, own_ref, kept_ref,
-    target_ref, delay_ref, link_ref, near_ref, jacobi_ref, voltage_ref, history_ref, blocks_ref, sems, block_sems,
-):
-    entries, chunks = blocks_ref.shape[0], block_sems.shape[0]
-    step = entries // chunks
-    pairs = [
-        (target_hbm, target_ref), (delay_hbm, delay_ref), (link_hbm, link_ref),
-        (near_hbm, near_ref), (jacobi_hbm, jacobi_ref), (voltage_hbm, voltage_ref),
-        (history_hbm, history_ref),
-    ]
-    copies = [pltpu.make_async_copy(a, b, sems.at[i]) for i, (a, b) in enumerate(pairs)]
-    slabs = [
-        pltpu.make_async_copy(
-            blocks_hbm.at[pl.ds(c * step, step)], blocks_ref.at[pl.ds(c * step, step)], block_sems.at[c]
-        )
-        for c in range(chunks)
-    ]
-    for copy in copies + slabs:
+def copy_in(sources, targets, sems):
+    copies = [pltpu.make_async_copy(a, b, sems.at[i]) for i, (a, b) in enumerate(zip(sources, targets))]
+    for copy in copies:
         copy.start()
-    bucket_ref[...] = jnp.zeros_like(bucket_ref)
-    for copy in copies:
+    return copies
+
+
+def blocks_kernel(link_hbm, near_hbm, jacobi_hbm, own_ref, kept_ref, link_ref, near_ref, jacobi_ref, sems):
+    for copy in copy_in((link_hbm, near_hbm, jacobi_hbm), (link_ref, near_ref, jacobi_ref), sems):
         copy.wait()
     jacobi = jacobi_ref[...]
     kept_ref[...] = jacobi
@@ -82,6 +68,24 @@
         product = jnp.dot(near, jacobi, preferred_element_type=jnp.float32)
         merged = near.astype(jnp.float32) + product
         own_ref[side] = merged + jacobi.astype(jnp.float32) if side == 1 else merged * gate.astype(jnp.float32)
+
+
+def far_kernel(
+    tile_ref, target_hbm, delay_hbm, voltage_hbm, history_hbm, blocks_hbm, bucket_ref,
+    target_ref, delay_ref, voltage_ref, history_ref, blocks_ref, sems, block_sems,
+):
+    entries, chunks = blocks_ref.shape[0], block_sems.shape[0]
+    step = entries // chunks
+    copies = copy_in(
+        (target_hbm, delay_hbm, voltage_hbm, history_hbm),
+        (target_ref, delay_ref, voltage_ref, history_ref),
+        sems,
+    )
+    slices = [pl.ds(c * step, step) for c in range(chunks)]
+    slabs = copy_in([blocks_hbm.at[s] for s in slices], [blocks_ref.at[s] for s in slices], block_sems)
+    bucket_ref[...] = jnp.zeros_like(bucket_ref)
+    for copy in copies:
+        copy.wait()
     bucket_ref[tile_ref[0]] = -voltage_ref[...]
     for c in range(chunks):
         slabs[c].wait()
@@ -235,12 +239,10 @@
     safe_ref[0] = jnp.min(safe)
 
 
-def gather_blocks(own):
+def gather_blocks(piece):
     size = CHIPS * CORES
-    pairs = [[CORES * chip + core for core in range(CORES)] for chip in range(CHIPS)]
     ring = [(i, (i + (CORES if i % CORES == 0 else -CORES)) % size) for i in range(size)]
     swap = [(i, i ^ 1) for i in range(size)]
-    piece = lax.all_gather(own, "row", axis_index_groups=pairs)
     pieces = [piece]
     for distance in range(1, CHIPS // 2 + 1):
         piece = lax.ppermute(piece, "row", ring)
@@ -335,21 +337,31 @@
     f32 = jnp.float32
     field_shape = jax.ShapeDtypeStruct((scenarios, segments), f32)
 
-    inputs = (targets, delays, link, near, jacobi, voltage, history, far_blocks)
-    spaces = [pltpu.SMEM] * 3 + [pltpu.VMEM] * 5
-    bucket, own_blocks, jacobi_kept = call(
-        front_kernel,
-        (
-            jax.ShapeDtypeStruct((tiles, scenarios, segments), f32),
-            jax.ShapeDtypeStruct(near.shape, f32),
-            jax.ShapeDtypeStruct(jacobi.shape, jacobi.dtype),
-        ),
+    block_inputs = (link, near, jacobi)
+    own_blocks, jacobi_kept = call(
+        blocks_kernel,
+        (jax.ShapeDtypeStruct(near.shape, f32), jax.ShapeDtypeStruct(jacobi.shape, jacobi.dtype)),
+        "hhh",
+        scratch_shapes=[
+            space(x.shape, x.dtype) for space, x in zip((pltpu.SMEM, pltpu.VMEM, pltpu.VMEM), block_inputs)
+        ]
+        + [pltpu.SemaphoreType.DMA((len(block_inputs),))],
+    )(*block_inputs)
+    pairs = [[CORES * chip + core for core in range(CORES)] for chip in range(CHIPS)]
+    piece = lax.all_gather(own_blocks, "row", axis_index_groups=pairs)
+    pieces = gather_blocks(piece)
+    targets, _ = lax.optimization_barrier((targets, piece))
+    inputs = (targets, delays, voltage, history, far_blocks)
+    spaces = [pltpu.SMEM] * 2 + [pltpu.VMEM] * 3
+    bucket = call(
+        far_kernel,
+        jax.ShapeDtypeStruct((tiles, scenarios, segments), f32),
         "s" + "h" * len(inputs),
         scratch_shapes=[space(x.shape, x.dtype) for space, x in zip(spaces, inputs)]
         + [pltpu.SemaphoreType.DMA((len(inputs) - 1,)), pltpu.SemaphoreType.DMA((4,))],
     )(lax.axis_index("tile").astype(jnp.int32)[None], *inputs)
+    bucket, _ = lax.optimization_barrier((bucket, pieces[1]))
     received = lax.all_to_all(bucket, "tile", split_axis=0, concat_axis=0, tiled=True)
-    pieces = gather_blocks(own_blocks)
     initial = call(start_kernel, field_shape, "vv")(received, jacobi_kept)
     starts = lax.all_gather(initial, "row")
     place = lax.axis_index("row").astype(jnp.int32)[None]
@@ -361,10 +373,10 @@
         "vv",
         out_specs=(pl.BlockSpec(memory_space=pltpu.VMEM), pl.BlockSpec(memory_space=pltpu.SMEM)),
     )(by_tile, own)
-    result = lax.cond(
-        safe[0] > 0.5,
-        lambda: result,
-        lambda: stepwise_solve(initial, near, jacobi, link),
+    safe, result = lax.while_loop(
+        lambda state: state[0][0] < 0.5,
+        lambda state: (jnp.ones_like(state[0]), stepwise_solve(initial, near, jacobi, link)),
+        (safe, result),
     )
     return result[None, None, None]
 

time: 109 us -> 106 us (0.972)
  blocking collectives: 20.1 us -> 41.4 us
  waiting for transfers between devices: 23.2 us -> 8.27 us
  starting transfers between devices: 50.7 us -> 40.9 us
    all_to_all x0 -> x1, blocking collectives: none -> 21.3 us  [per_device(): lax.all_to_all(gram, 'tile', split_axis=0, concat_axis=0, tiled=True)]
    all_to_all x1 -> x0, waiting for transfers between devices: 11.7 us -> none  [per_device(): lax.all_to_all(gram, 'tile', split_axis=0, concat_axis=0, tiled=True)]
    all_to_all x1 -> x0, starting transfers between devices: 9.79 us -> none  [per_device(): lax.all_to_all(gram, 'tile', split_axis=0, concat_axis=0, tiled=True)]
    ppermute x4, waiting for transfers between devices: 11.5 us -> 8.26 us  [gather_blocks(): piece = lax.ppermute(piece, 'row', ring)]
    pallas_call x4 -> x5, Pallas kernels: 12.8 us -> 13.2 us  [placed(): run(*(pltpu.with_memory_space_constraint(x, pltpu.HBM) if c == 'h' else x...]
  transfers between devices with their start and end apart: 9 -> 8, of which waited for: 4 -> 3; matrix products, arithmetic and copies ran while one was open for 0% -> 0% of each run, Pallas kernels for 0% -> 3%
where the time goes in v5:
time: 106 us; the launch traced here: 105 us
  blocking collectives  41.4 us (39%)
  starting transfers between devices  40.9 us (39%)
  Pallas kernels  13.2 us (12%)
  waiting for transfers between devices  8.27 us (8%)
    ppermute x4, starting transfers between devices, gather_blocks(): piece = lax.ppermute(piece, 'row', ring)  21.5 us
    all_to_all x1, blocking collectives, per_device(): lax.all_to_all(gram, 'tile', split_axis=0, concat_axis=0, tiled=True)  21.3 us
    all_gather x1, blocking collectives, per_device(): starts = lax.all_gather(initial, 'row')  18 us
    all_to_all x1, starting transfers between devices, per_device(): lax.all_to_all(bucket, 'tile', split_axis=0, concat_axis=0, tiled=True)  13.2 us
    pallas_call x5, Pallas kernels, placed(): run(*(pltpu.with_memory_space_constraint(x, pltpu.HBM) if c == 'h' else x...  13.2 us
    ppermute x4, waiting for transfers between devices, gather_blocks(): piece = lax.ppermute(piece, 'row', ring)  8.26 us
    ppermute x3, starting transfers between devices, gather_blocks(): pieces.append(lax.ppermute(piece, 'row', swap))  6.24 us
  transfers between devices with their start and end apart: 8, of which 3 were waited for; matrix products, arithmetic and copies ran while one was open for 0% of the time, Pallas kernels for 3%

profile of v5, /device:TPU:24, one launch (start us, length us, event | category | flops | bytes accessed | tf_op | source)
XLA Modules:
  0.0 105.4 jit_solution(13026526354077710504)
XLA Ops:
  0.0 1.1 %shard_map.82 = (f32[3,128,128]{2,1,0:T(8,128)S(1)}, bf16[128,128]{1,0:T(8,128)(2,1)S(1)}) custom-call(s32[2]{0:T(128)} %bitcast.247, bf16[3,128,128]{2,1,0:T(8,128)(2,1)} %bitcast.226, bf16[128,128]{1,0:T(8,128)(2,1)} %bitcast.228), custom_call_target="tpu_custom_call" | custom-call | tf_op jit(solution)/shard_map/pallas_call | solution.py:29
  1.1 2.1 %all-gather = f32[6,128,128]{2,1,0:T(8,128)S(1)} all-gather(f32[3,128,128]{2,1,0:T(8,128)S(1)} %get-tuple-element.43), channel_id=2, replica_groups={{0,1},{2,3},{4,5},{6,7},{8,9},{10,11},{12,13},{14,15},{16,17},{18,19},{..., dimensions={0}, use_global_device_ids=true | all-gather | bytes 589824 | tf_op jit(solution)/shard_map/all_gather | solution.py:351
  3.2 4.7 %collective-permute-start.10 = (f32[2,3,128,128]{3,2,1,0:T(8,128)S(1)}, f32[2,3,128,128]{3,2,1,0:T(8,128)S(1)}, u32[]{:S(2)}, u32[]{:S(2)}) collective-permute-start(f32[2,3,128,128]{3,2,1,0:T(8,128)S(1)} %bitcast.224), channel_id=1, source_target_pairs={{0,2},{1,15},{2,4},{3,1},{4,6},{5,3},{6,8},{7,5},{8,10},{9,7},{10,... | collective-permute-start | bytes 1179656 | tf_op jit(solution)/shard_map/ppermute | solution.py:248
  7.9 3.2 %shard_map.83 = f32[32,64,128]{2,1,0:T(8,128)} custom-call(s32[1]{0:T(128)} %bitcast.35.tile_ref, s32[32]{0:T(128)} %bitcast.249, s32[32]{0:T(128)} %bitcast.250, f32[64,128]{1,0:T(8,128)} %bitcast.246, bf16[32,64,128]{2,1,0:T(8,128)(2,1)} %bitcast.231, bf16[32,128,128]{2,1,0:T(8,128)(2,1)} %bitcast.230), custom_call_target="tpu_custom_call" | custom-call | tf_op jit(solution)/shard_map/pallas_call | solution.py:29
  11.1 2.1 %collective-permute-done.10.refs_1_ = f32[2,3,128,128]{3,2,1,0:T(8,128)S(1)} collective-permute-done((f32[2,3,128,128]{3,2,1,0:T(8,128)S(1)}, f32[2,3,128,128]{3,2,1,0:T(8,128)S(1)}, u32[]{:S(2)}, u32[]{:S(2)}) %collective-permute-start.10) | collective-permute-done | bytes 393248 | tf_op jit(solution)/shard_map/ppermute | solution.py:248
  13.2 13.2 %all-to-all-start = ((f32[32,64,128]{2,1,0:T(8,128)}), f32[32,64,128]{2,1,0:T(8,128)S(1)}, u32[]{:S(2)}, u32[]{:S(2)}) async-start(f32[32,64,128]{2,1,0:T(8,128)} %shard_map.83), calls=%async_computation | async-start | bytes 2097152 | tf_op jit(solution)/shard_map/all_to_all | solution.py:364
  26.3 5.6 %collective-permute-start.12 = (f32[2,3,128,128]{3,2,1,0:T(8,128)S(1)}, f32[2,3,128,128]{3,2,1,0:T(8,128)S(1)}, u32[]{:S(2)}, u32[]{:S(2)}) collective-permute-start(f32[2,3,128,128]{3,2,1,0:T(8,128)S(1)} %collective-permute-done.10.refs_1_), channel_id=1, source_target_pairs={{0,2},{1,15},{2,4},{3,1},{4,6},{5,3},{6,8},{7,5},{8,10},{9,7},{10,... | collective-permute-start | bytes 1179656 | tf_op jit(solution)/shard_map/ppermute | solution.py:248
  31.9 5.3 %collective-permute-done.12.refs_3_ = f32[2,3,128,128]{3,2,1,0:T(8,128)S(1)} collective-permute-done((f32[2,3,128,128]{3,2,1,0:T(8,128)S(1)}, f32[2,3,128,128]{3,2,1,0:T(8,128)S(1)}, u32[]{:S(2)}, u32[]{:S(2)}) %collective-permute-start.12) | collective-permute-done | bytes 393248 | tf_op jit(solution)/shard_map/ppermute | solution.py:248
  37.2 5.6 %collective-permute-start.14 = (f32[2,3,128,128]{3,2,1,0:T(8,128)S(1)}, f32[2,3,128,128]{3,2,1,0:T(8,128)S(1)}, u32[]{:S(2)}, u32[]{:S(2)}) collective-permute-start(f32[2,3,128,128]{3,2,1,0:T(8,128)S(1)} %collective-permute-done.12.refs_3_), channel_id=1, source_target_pairs={{0,2},{1,15},{2,4},{3,1},{4,6},{5,3},{6,8},{7,5},{8,10},{9,7},{10,... | collective-permute-start | bytes 1179656 | tf_op jit(solution)/shard_map/ppermute | solution.py:248
  42.8 1.9 %collective-permute-start.11 = (f32[2,3,128,128]{3,2,1,0:T(8,128)S(1)}, f32[2,3,128,128]{3,2,1,0:T(8,128)S(1)}, u32[]{:S(2)}, u32[]{:S(2)}) collective-permute-start(f32[2,3,128,128]{3,2,1,0:T(8,128)S(1)} %collective-permute-done.10.refs_1_), channel_id=1, source_target_pairs={{0,1},{1,0},{2,3},{3,2},{4,5},{5,4},{6,7},{7,6},{8,9},{9,8},{10,11... | collective-permute-start | bytes 1179656 | tf_op jit(solution)/shard_map/ppermute | solution.py:251
  44.7 2.4 %collective-permute-start.13 = (f32[2,3,128,128]{3,2,1,0:T(8,128)S(1)}, f32[2,3,128,128]{3,2,1,0:T(8,128)S(1)}, u32[]{:S(2)}, u32[]{:S(2)}) collective-permute-start(f32[2,3,128,128]{3,2,1,0:T(8,128)S(1)} %collective-permute-done.12.refs_3_), channel_id=1, source_target_pairs={{0,1},{1,0},{2,3},{3,2},{4,5},{5,4},{6,7},{7,6},{8,9},{9,8},{10,11... | collective-permute-start | bytes 1179656 | tf_op jit(solution)/shard_map/ppermute | solution.py:251
  47.1 0.9 collective-permute-done.14.refs_5_
  48.1 1.9 %collective-permute-start.15 = (f32[2,3,128,128]{3,2,1,0:T(8,128)S(1)}, f32[2,3,128,128]{3,2,1,0:T(8,128)}, u32[]{:S(2)}, u32[]{:S(2)}) collective-permute-start(f32[2,3,128,128]{3,2,1,0:T(8,128)S(1)} %collective-permute-done.14.refs_5_), channel_id=1, source_target_pairs={{0,1},{1,0},{2,3},{3,2},{4,5},{5,4},{6,7},{7,6},{8,9},{9,8},{10,11... | collective-permute-start | bytes 1179656 | tf_op jit(solution)/shard_map/ppermute | solution.py:251
  50.0 5.6 %collective-permute-start.16 = (f32[2,3,128,128]{3,2,1,0:T(8,128)S(1)}, f32[2,3,128,128]{3,2,1,0:T(8,128)}, u32[]{:S(2)}, u32[]{:S(2)}) collective-permute-start(f32[2,3,128,128]{3,2,1,0:T(8,128)S(1)} %collective-permute-done.14.refs_5_), channel_id=1, source_target_pairs={{0,2},{1,15},{2,4},{3,1},{4,6},{5,3},{6,8},{7,5},{8,10},{9,7},{10,... | collective-permute-start | bytes 1179656 | tf_op jit(solution)/shard_map/ppermute | solution.py:248
  55.6 0.0 all-to-all-done.received_ref
  55.6 0.2 shard_map.84
  55.8 18.0 %all-gather.1 = f32[1024,128]{1,0:T(8,128)S(1)} all-gather(f32[64,128]{1,0:T(8,128)S(1)} %shard_map.84), channel_id=3, replica_groups=mesh['tile'=32,'row'=16] {'row'}, dimensions={0}, use_global_device_ids=true | all-gather | bytes 557056 | tf_op jit(solution)/shard_map/all_gather | solution.py:366
  73.8 0.0 collective-permute-done.11.refs_2_
  73.9 7.0 %shard_map.85 = (f32[32,1,1408]{2,1,0:T(1,128)S(1)}, f32[5,64,128]{2,1,0:T(8,128)S(1)}) custom-call(s32[1]{0:T(128)} %bitcast.34.place_ref, f32[16,64,128]{2,1,0:T(8,128)S(1)} %bitcast.223, f32[2,3,128,128]{3,2,1,0:T(8,128)S(1)} %bitcast.225, f32[2,3,128,128]{3,2,1,0:T(8,128)S(1)} %collective-permute-done.10.refs_1_, ...), custom_call_target="tpu_custom_call" | custom-call | tf_op jit(solution)/shard_map/pallas_call | solution.py:29
  80.9 21.3 %all_to_all.10.received_ref = f32[32,1,1408]{2,1,0:T(1,128)S(1)} all-to-all(f32[32,1,1408]{2,1,0:T(1,128)S(1)} %get-tuple-element.47), channel_id=1, replica_groups=mesh['tile'=32,'row'=16] {'tile'}, dimensions={0} | all-to-all | bytes 360448 | tf_op jit(solution)/shard_map/all_to_all | solution.py:369
  102.2 1.6 %shard_map.86 = (f32[64,128]{1,0:T(8,128)}, f32[1]{0:T(128)}) custom-call(f32[32,1,1408]{2,1,0:T(1,128)S(1)} %all_to_all.10.received_ref, f32[5,64,128]{2,1,0:T(8,128)S(1)} %get-tuple-element.48.fields_ref), custom_call_target="tpu_custom_call" | custom-call | tf_op jit(solution)/shard_map/pallas_call | solution.py:29
  103.8 0.0 copy-start.2
  103.9 0.6 copy-done.2
  104.5 0.7 while.9
  (7 shorter events, 0.0 us)
Async XLA Ops:
  3.2 10.0 %collective-permute-start.10 = (f32[2,3,128,128]{3,2,1,0:T(8,128)S(1)}, f32[2,3,128,128]{3,2,1,0:T(8,128)S(1)}, u32[]{:S(2)}, u32[]{:S(2)}) collective-permute-start(f32[2,3,128,128]{3,2,1,0:T(8,128)S(1)} %bitcast.224), channel_id=1, source_target_pairs={{0,2},{1,15},{2,4},{3,1},{4,6},{5,3},{6,8},{7,5},{8,10},{9,7},{10,... | collective-permute-start | bytes 1179656 | tf_op jit(solution)/shard_map/ppermute | solution.py:248
  13.2 42.5 %all-to-all-start = ((f32[32,64,128]{2,1,0:T(8,128)}), f32[32,64,128]{2,1,0:T(8,128)S(1)}, u32[]{:S(2)}, u32[]{:S(2)}) async-start(f32[32,64,128]{2,1,0:T(8,128)} %shard_map.83), calls=%async_computation | async-start | bytes 2097152 | tf_op jit(solution)/shard_map/all_to_all | solution.py:364
  26.3 10.9 %collective-permute-start.12 = (f32[2,3,128,128]{3,2,1,0:T(8,128)S(1)}, f32[2,3,128,128]{3,2,1,0:T(8,128)S(1)}, u32[]{:S(2)}, u32[]{:S(2)}) collective-permute-start(f32[2,3,128,128]{3,2,1,0:T(8,128)S(1)} %collective-permute-done.10.refs_1_), channel_id=1, source_target_pairs={{0,2},{1,15},{2,4},{3,1},{4,6},{5,3},{6,8},{7,5},{8,10},{9,7},{10,... | collective-permute-start | bytes 1179656 | tf_op jit(solution)/shard_map/ppermute | solution.py:248
  37.2 10.9 %collective-permute-start.14 = (f32[2,3,128,128]{3,2,1,0:T(8,128)S(1)}, f32[2,3,128,128]{3,2,1,0:T(8,128)S(1)}, u32[]{:S(2)}, u32[]{:S(2)}) collective-permute-start(f32[2,3,128,128]{3,2,1,0:T(8,128)S(1)} %collective-permute-done.12.refs_3_), channel_id=1, source_target_pairs={{0,2},{1,15},{2,4},{3,1},{4,6},{5,3},{6,8},{7,5},{8,10},{9,7},{10,... | collective-permute-start | bytes 1179656 | tf_op jit(solution)/shard_map/ppermute | solution.py:248
  42.8 31.0 %collective-permute-start.11 = (f32[2,3,128,128]{3,2,1,0:T(8,128)S(1)}, f32[2,3,128,128]{3,2,1,0:T(8,128)S(1)}, u32[]{:S(2)}, u32[]{:S(2)}) collective-permute-start(f32[2,3,128,128]{3,2,1,0:T(8,128)S(1)} %collective-permute-done.10.refs_1_), channel_id=1, source_target_pairs={{0,1},{1,0},{2,3},{3,2},{4,5},{5,4},{6,7},{7,6},{8,9},{9,8},{10,11... | collective-permute-start | bytes 1179656 | tf_op jit(solution)/shard_map/ppermute | solution.py:251
  44.7 29.1 %collective-permute-start.13 = (f32[2,3,128,128]{3,2,1,0:T(8,128)S(1)}, f32[2,3,128,128]{3,2,1,0:T(8,128)S(1)}, u32[]{:S(2)}, u32[]{:S(2)}) collective-permute-start(f32[2,3,128,128]{3,2,1,0:T(8,128)S(1)} %collective-permute-done.12.refs_3_), channel_id=1, source_target_pairs={{0,1},{1,0},{2,3},{3,2},{4,5},{5,4},{6,7},{7,6},{8,9},{9,8},{10,11... | collective-permute-start | bytes 1179656 | tf_op jit(solution)/shard_map/ppermute | solution.py:251
  48.1 25.8 %collective-permute-start.15 = (f32[2,3,128,128]{3,2,1,0:T(8,128)S(1)}, f32[2,3,128,128]{3,2,1,0:T(8,128)}, u32[]{:S(2)}, u32[]{:S(2)}) collective-permute-start(f32[2,3,128,128]{3,2,1,0:T(8,128)S(1)} %collective-permute-done.14.refs_5_), channel_id=1, source_target_pairs={{0,1},{1,0},{2,3},{3,2},{4,5},{5,4},{6,7},{7,6},{8,9},{9,8},{10,11... | collective-permute-start | bytes 1179656 | tf_op jit(solution)/shard_map/ppermute | solution.py:251
  50.0 23.9 %collective-permute-start.16 = (f32[2,3,128,128]{3,2,1,0:T(8,128)S(1)}, f32[2,3,128,128]{3,2,1,0:T(8,128)}, u32[]{:S(2)}, u32[]{:S(2)}) collective-permute-start(f32[2,3,128,128]{3,2,1,0:T(8,128)S(1)} %collective-permute-done.14.refs_5_), channel_id=1, source_target_pairs={{0,2},{1,15},{2,4},{3,1},{4,6},{5,3},{6,8},{7,5},{8,10},{9,7},{10,... | collective-permute-start | bytes 1179656 | tf_op jit(solution)/shard_map/ppermute | solution.py:248
  102.2 1.7 %copy-start = (bf16[1,1,3,128,128]{4,3,2,1,0:T(8,128)(2,1)S(1)}, bf16[1,1,3,128,128]{4,3,2,1,0:T(8,128)(2,1)}, u32[]{:S(2)}) copy-start(bf16[1,1,3,128,128]{4,3,2,1,0:T(8,128)(2,1)} %param.15) | copy-start | bytes 294916
  102.2 1.7 %copy-start.1 = (bf16[1,1,128,128]{3,2,1,0:T(8,128)(2,1)S(1)}, bf16[1,1,128,128]{3,2,1,0:T(8,128)(2,1)}, u32[]{:S(2)}) copy-start(bf16[1,1,128,128]{3,2,1,0:T(8,128)(2,1)} %param.17) | copy-start | bytes 98308
  103.8 0.7 copy-start.2

commit v6 on v4

--- a/solution.py
+++ b/solution.py
@@ -13,6 +13,7 @@
 PRECISE = lax.Precision.HIGHEST
 CORES = 2
 CHIPS = 8
+REACH = -(-(ITERS - 1) // CORES)
 
 
 def call(kernel, out_shape, in_spaces, **kwargs):
@@ -46,8 +47,8 @@
 
 def ring_steps():
     steps = [0]
-    for distance in range(1, CHIPS // 2 + 1):
-        steps += [distance] if distance == CHIPS // 2 else [distance, -distance]
+    for distance in range(1, REACH + 1):
+        steps += [distance, -distance]
     return steps
 
 
@@ -101,53 +102,49 @@
 
 
 def krylov_kernel(place_ref, start_ref, *refs):
-    chips = CHIPS
-    piece_refs = refs[:chips]
-    gram_ref, own_ref, fields, parts, highs, lows, sums = refs[chips:]
+    steps = ring_steps()
+    piece_refs = refs[: len(steps)]
+    gram_ref, own_ref, fields, parts, highs, lows, sums = refs[len(steps) :]
     rows, scenarios, segments = start_ref.shape
-    cores = rows // chips
-    zero_part = jnp.zeros(parts.shape[2:], parts.dtype)
-    for side in range(2):
-        parts[side, 0] = zero_part
-        parts[side, rows + 1] = zero_part
+    place = place_ref[0]
+    core = lax.rem(place, CORES)
+    middle = ITERS
 
     def halves(value):
         high = value.astype(jnp.bfloat16)
         low = (value - high.astype(jnp.float32)).astype(jnp.bfloat16)
         return high, low
 
-    chip, core = lax.div(place_ref[0], cores), lax.rem(place_ref[0], cores)
-    for piece_ref, steps in zip(piece_refs, ring_steps()):
-        source = lax.rem(chip + (2 * core - 1) * steps + chips, chips)
-        for core_there in range(cores):
-            b = source * cores + core_there
-            highs[b], lows[b] = halves(piece_ref[core_there].reshape(highs.shape[1:]))
-    for b in range(rows):
-        fields[0, b] = start_ref[b]
-        parts[0, b + 1] = jnp.concatenate(halves(start_ref[b]), axis=0)
+    def inside(tile):
+        return jnp.where((tile >= 0) & (tile < rows), 1.0, 0.0)
+
+    for piece_ref, step in zip(piece_refs, steps):
+        for there in range(CORES):
+            away = (2 * core - 1) * (step * CORES) + there - core
+            block = piece_ref[there].reshape(highs.shape[1:]) * inside(place + away)
+            highs[away + middle], lows[away + middle] = halves(block)
+    for away in range(-middle, middle + 1):
+        tile = place + away
+        field = start_ref[jnp.clip(tile, 0, rows - 1)] * inside(tile)
+        parts[0, away + middle] = jnp.concatenate(halves(field), axis=0)
+        if away == 0:
+            fields[0] = field
 
     for k in range(ITERS):
-        now, later = k % 2, (k + 1) % 2
-        for b in range(rows):
-            around = jnp.concatenate([parts[now, b], parts[now, b + 1], parts[now, b + 2]], axis=1)
-            main = jnp.dot(around, highs[b], preferred_element_type=jnp.float32)
-            rest = jnp.dot(around[:scenarios], lows[b], preferred_element_type=jnp.float32)
+        reach = ITERS - 1 - k
+        for t in range(middle - reach, middle + reach + 1):
+            around = jnp.concatenate([parts[k, t - 1], parts[k, t], parts[k, t + 1]], axis=1)
+            main = jnp.dot(around, highs[t], preferred_element_type=jnp.float32)
+            rest = jnp.dot(around[:scenarios], lows[t], preferred_element_type=jnp.float32)
             value = main[:scenarios] + (main[scenarios:] + rest)
-            fields[k + 1, b] = value
+            if t == middle:
+                fields[k + 1] = value
             if k + 1 < ITERS:
-                parts[later, b + 1] = jnp.concatenate(halves(value), axis=0)
-
-    def gram(c, carry):
-        at = pl.ds(pl.multiple_of(c * 8, 8), 8)
-        totals = [jnp.zeros((8, segments), jnp.float32) for _ in PAIRS]
-        for b in range(rows):
-            values = [fields[i, b, at] for i in range(BASIS)]
-            totals = [t + values[i] * values[j] for t, (i, j) in zip(totals, PAIRS)]
-        for p, t in enumerate(totals):
-            sums[p, at] = t
-        return carry
-
-    lax.fori_loop(0, scenarios // 8, gram, 0)
+                parts[k + 1, t] = jnp.concatenate(halves(value), axis=0)
+
+    values = [fields[i] for i in range(BASIS)]
+    for p, (i, j) in enumerate(PAIRS):
+        sums[p] = values[i] * values[j]
     for p in range(len(PAIRS), sums.shape[0]):
         sums[p] = jnp.zeros((scenarios, segments), jnp.float32)
     total = lax.dot_general(
@@ -159,28 +156,34 @@
     )
     gram_ref[...] = jnp.broadcast_to(total[0:1][None], gram_ref.shape)
     for j in range(ITERS):
-        own_ref[j] = fields[j, place_ref[0]]
-
-
-def krylov_call(place, starts, pieces, tiles=32):
+        own_ref[j] = fields[j]
+
+
+def krylov_call(place, starts, pieces):
     rows, scenarios, segments = starts.shape
-    f32 = jnp.float32
+    f32, bf16 = jnp.float32, jnp.bfloat16
     padded_pairs = -(-len(PAIRS) * scenarios // 128) * 128 // scenarios
+    span = 2 * ITERS + 1
     return call(
         krylov_kernel,
         (
-            jax.ShapeDtypeStruct((tiles, 1, padded_pairs * scenarios), f32),
+            jax.ShapeDtypeStruct((rows, 1, padded_pairs * scenarios), f32),
             jax.ShapeDtypeStruct((ITERS, scenarios, segments), f32),
         ),
         "sv" + "v" * len(pieces),
         scratch_shapes=[
-            pltpu.VMEM((BASIS, rows, scenarios, segments), f32),
-            pltpu.VMEM((2, rows + 2, 2 * scenarios, segments), jnp.bfloat16),
-            pltpu.VMEM((rows, 3 * segments, segments), jnp.bfloat16),
-            pltpu.VMEM((rows, 3 * segments, segments), jnp.bfloat16),
+            pltpu.VMEM((BASIS, scenarios, segments), f32),
+            pltpu.VMEM((ITERS, span, 2 * scenarios, segments), bf16),
+            pltpu.VMEM((span, 3 * segments, segments), bf16),
+            pltpu.VMEM((span, 3 * segments, segments), bf16),
             pltpu.VMEM((padded_pairs, scenarios, segments), f32),
         ],
     )(place, starts, *pieces)
+
+
+def add_kernel(received_ref, out_ref):
+    total = jnp.sum(received_ref[...], axis=0)
+    out_ref[...] = jnp.broadcast_to(total[None], out_ref.shape)
 
 
 def solve_kernel(received_ref, fields_ref, out_ref, safe_ref):
@@ -242,11 +245,10 @@
     swap = [(i, i ^ 1) for i in range(size)]
     piece = lax.all_gather(own, "row", axis_index_groups=pairs)
     pieces = [piece]
-    for distance in range(1, CHIPS // 2 + 1):
+    for _ in range(REACH):
         piece = lax.ppermute(piece, "row", ring)
-        pieces.append(piece)
-        if distance < CHIPS // 2:
-            pieces.append(lax.ppermute(piece, "row", swap))
+        given, _ = lax.optimization_barrier((piece, pieces[-1]))
+        pieces += [piece, lax.ppermute(given, "row", swap)]
     return pieces
 
 
@@ -353,18 +355,20 @@
     initial = call(start_kernel, field_shape, "vv")(received, jacobi_kept)
     starts = lax.all_gather(initial, "row")
     place = lax.axis_index("row").astype(jnp.int32)[None]
-    gram, own = krylov_call(place, starts, pieces, tiles)
-    by_tile = lax.all_to_all(gram, "tile", split_axis=0, concat_axis=0, tiled=True)
+    gram, own = krylov_call(place, starts, pieces)
+    by_row = lax.all_to_all(gram, "row", split_axis=0, concat_axis=0, tiled=True)
+    group = call(add_kernel, jax.ShapeDtypeStruct((tiles,) + gram.shape[1:], f32), "v")(by_row)
+    by_tile = lax.all_to_all(group, "tile", split_axis=0, concat_axis=0, tiled=True)
     result, safe = call(
         solve_kernel,
         (field_shape, jax.ShapeDtypeStruct((1,), f32)),
         "vv",
         out_specs=(pl.BlockSpec(memory_space=pltpu.VMEM), pl.BlockSpec(memory_space=pltpu.SMEM)),
     )(by_tile, own)
-    result = lax.cond(
-        safe[0] > 0.5,
-        lambda: result,
-        lambda: stepwise_solve(initial, near, jacobi, link),
+    safe, result = lax.while_loop(
+        lambda state: state[0][0] < 0.5,
+        lambda state: (jnp.ones_like(state[0]), stepwise_solve(initial, near, jacobi, link)),
+        (safe, result),
     )
     return result[None, None, None]
 

time: 109 us -> 103 us (0.945)
  the two profiles are of different devices: /device:TPU:24 before, /device:TPU:1 now
where the time goes in v6:
time: 103 us; the launch traced here: 102 us
  blocking collectives  52.4 us (51%)
  starting transfers between devices  30 us (29%)
  waiting for transfers between devices  9.86 us (10%)
  Pallas kernels  7.76 us (8%)
    all_gather x1, blocking collectives, per_device(): starts = lax.all_gather(initial, 'row')  19.6 us
    all_to_all x1, blocking collectives, per_device(): lax.all_to_all(group, 'tile', split_axis=0, concat_axis=0, tiled=True)  17.6 us
    all_to_all x1, starting transfers between devices, per_device(): lax.all_to_all(bucket, 'tile', split_axis=0, concat_axis=0, tiled=True)  13.7 us
    all_to_all x1, blocking collectives, per_device(): lax.all_to_all(gram, 'row', split_axis=0, concat_axis=0, tiled=True)  12.6 us
    ppermute x2, waiting for transfers between devices, gather_blocks(): piece = lax.ppermute(piece, 'row', ring)  9.85 us
    ppermute x2, starting transfers between devices, gather_blocks(): piece = lax.ppermute(piece, 'row', ring)  8.73 us
    pallas_call x5, Pallas kernels, placed(): run(*(pltpu.with_memory_space_constraint(x, pltpu.HBM) if c == 'h' else x...  7.76 us
    ppermute x2, starting transfers between devices, gather_blocks(): pieces += [piece, lax.ppermute(given, 'row', swap)]  7.56 us
  transfers between devices with their start and end apart: 5, of which 2 were waited for; matrix products, arithmetic and copies ran while one was open for 0% of the time, Pallas kernels for 0%

profile of v6, /device:TPU:1, one launch (start us, length us, event | category | flops | bytes accessed | tf_op | source)
XLA Modules:
  0.0 101.7 jit_solution(3062736501833852698)
XLA Ops:
  0.0 3.5 %shard_map.82 = (f32[32,64,128]{2,1,0:T(8,128)}, f32[3,128,128]{2,1,0:T(8,128)S(1)}, bf16[128,128]{1,0:T(8,128)(2,1)S(1)}) custom-call(s32[1]{0:T(128)} %bitcast.35.tile_ref, s32[32]{0:T(128)} %bitcast.247, s32[32]{0:T(128)} %bitcast.248, s32[2]{0:T(128)} %bitcast.249, bf16[3,128,128]{2,1,0:T(8,128)(2,1)} %bitcast.226, bf16[128,128]{1,0:T(8,128)(2,1)} %bitcast.228, ...), custom_call_target="tpu_custom_call" | custom-call | tf_op jit(solution)/shard_map/pallas_call | solution.py:30
  3.5 13.7 %all-to-all-start = ((f32[32,64,128]{2,1,0:T(8,128)}), f32[32,64,128]{2,1,0:T(8,128)S(1)}, u32[]{:S(2)}, u32[]{:S(2)}) async-start(f32[32,64,128]{2,1,0:T(8,128)} %get-tuple-element.44), calls=%async_computation | async-start | bytes 2097152 | tf_op jit(solution)/shard_map/all_to_all | solution.py:353
  17.2 2.7 %all-gather.1 = f32[6,128,128]{2,1,0:T(8,128)S(1)} all-gather(f32[3,128,128]{2,1,0:T(8,128)S(1)} %get-tuple-element.46), channel_id=3, replica_groups={{0,1},{2,3},{4,5},{6,7},{8,9},{10,11},{12,13},{14,15},{16,17},{18,19},{..., dimensions={0}, use_global_device_ids=true | all-gather | bytes 589824 | tf_op jit(solution)/shard_map/all_gather | solution.py:246
  19.9 5.1 %collective-permute-start.10 = (f32[2,3,128,128]{3,2,1,0:T(8,128)S(1)}, f32[2,3,128,128]{3,2,1,0:T(8,128)S(1)}, u32[]{:S(2)}, u32[]{:S(2)}) collective-permute-start(f32[2,3,128,128]{3,2,1,0:T(8,128)S(1)} %bitcast.224), channel_id=1, source_target_pairs={{0,2},{1,15},{2,4},{3,1},{4,6},{5,3},{6,8},{7,5},{8,10},{9,7},{10,... | collective-permute-start | bytes 1179656 | tf_op jit(solution)/shard_map/ppermute | solution.py:249
  25.0 4.7 %collective-permute-done.10.refs_1_ = f32[2,3,128,128]{3,2,1,0:T(8,128)S(1)} collective-permute-done((f32[2,3,128,128]{3,2,1,0:T(8,128)S(1)}, f32[2,3,128,128]{3,2,1,0:T(8,128)S(1)}, u32[]{:S(2)}, u32[]{:S(2)}) %collective-permute-start.10) | collective-permute-done | bytes 393248 | tf_op jit(solution)/shard_map/ppermute | solution.py:249
  29.7 3.6 %collective-permute-start.11 = (f32[2,3,128,128]{3,2,1,0:T(8,128)S(1)}, f32[2,3,128,128]{3,2,1,0:T(8,128)S(1)}, u32[]{:S(2)}, u32[]{:S(2)}) collective-permute-start(f32[2,3,128,128]{3,2,1,0:T(8,128)S(1)} %collective-permute-done.10.refs_1_), channel_id=1, source_target_pairs={{0,1},{1,0},{2,3},{3,2},{4,5},{5,4},{6,7},{7,6},{8,9},{9,8},{10,11... | collective-permute-start | bytes 1179656 | tf_op jit(solution)/shard_map/ppermute | solution.py:251
  33.3 3.6 %collective-permute-start.12 = (f32[2,3,128,128]{3,2,1,0:T(8,128)S(1)}, f32[2,3,128,128]{3,2,1,0:T(8,128)S(1)}, u32[]{:S(2)}, u32[]{:S(2)}) collective-permute-start(f32[2,3,128,128]{3,2,1,0:T(8,128)S(1)} %collective-permute-done.10.refs_1_), channel_id=1, source_target_pairs={{0,2},{1,15},{2,4},{3,1},{4,6},{5,3},{6,8},{7,5},{8,10},{9,7},{10,... | collective-permute-start | bytes 1179656 | tf_op jit(solution)/shard_map/ppermute | solution.py:249
  36.9 0.0 collective-permute-done.11.refs_2_
  37.0 5.2 %collective-permute-done.12.refs_3_ = f32[2,3,128,128]{3,2,1,0:T(8,128)S(1)} collective-permute-done((f32[2,3,128,128]{3,2,1,0:T(8,128)S(1)}, f32[2,3,128,128]{3,2,1,0:T(8,128)S(1)}, u32[]{:S(2)}, u32[]{:S(2)}) %collective-permute-start.12) | collective-permute-done | bytes 393248 | tf_op jit(solution)/shard_map/ppermute | solution.py:249
  42.1 4.0 %collective-permute-start.13 = (f32[2,3,128,128]{3,2,1,0:T(8,128)S(1)}, f32[2,3,128,128]{3,2,1,0:T(8,128)S(1)}, u32[]{:S(2)}, u32[]{:S(2)}) collective-permute-start(f32[2,3,128,128]{3,2,1,0:T(8,128)S(1)} %collective-permute-done.12.refs_3_), channel_id=1, source_target_pairs={{0,1},{1,0},{2,3},{3,2},{4,5},{5,4},{6,7},{7,6},{8,9},{9,8},{10,11... | collective-permute-start | bytes 1179656 | tf_op jit(solution)/shard_map/ppermute | solution.py:251
  46.1 0.0 all-to-all-done.received_ref
  46.1 0.2 shard_map.83
  46.3 19.6 %all-gather = f32[1024,128]{1,0:T(8,128)S(1)} all-gather(f32[64,128]{1,0:T(8,128)S(1)} %shard_map.83), channel_id=2, replica_groups=mesh['tile'=32,'row'=16] {'row'}, dimensions={0}, use_global_device_ids=true | all-gather | bytes 557056 | tf_op jit(solution)/shard_map/all_gather | solution.py:356
  65.9 0.0 collective-permute-done.13.refs_4_
  65.9 2.4 %shard_map.84 = (f32[16,1,1408]{2,1,0:T(1,128)S(1)}, f32[5,64,128]{2,1,0:T(8,128)S(1)}) custom-call(s32[1]{0:T(128)} %bitcast.34.place_ref, f32[16,64,128]{2,1,0:T(8,128)S(1)} %bitcast.223, f32[2,3,128,128]{3,2,1,0:T(8,128)S(1)} %bitcast.225, f32[2,3,128,128]{3,2,1,0:T(8,128)S(1)} %collective-permute-done.10.refs_1_, ...), custom_call_target="tpu_custom_call" | custom-call | tf_op jit(solution)/shard_map/pallas_call | solution.py:30
  68.3 12.6 %all_to_all.15.received_ref = f32[16,1,1408]{2,1,0:T(1,128)S(1)} all-to-all(f32[16,1,1408]{2,1,0:T(1,128)S(1)} %get-tuple-element.49), channel_id=1, replica_groups=mesh['tile'=32,'row'=16] {'row'}, dimensions={0} | all-to-all | bytes 180224 | tf_op jit(solution)/shard_map/all_to_all | solution.py:359
  80.9 0.1 shard_map.85
  80.9 17.6 %all_to_all.16.received_ref = f32[32,1,1408]{2,1,0:T(1,128)S(1)} all-to-all(f32[32,1,1408]{2,1,0:T(1,128)S(1)} %shard_map.85), channel_id=1, replica_groups=mesh['tile'=32,'row'=16] {'tile'}, dimensions={0} | all-to-all | bytes 360448 | tf_op jit(solution)/shard_map/all_to_all | solution.py:361
  98.5 1.6 %shard_map.86 = (f32[64,128]{1,0:T(8,128)}, f32[1]{0:T(128)}) custom-call(f32[32,1,1408]{2,1,0:T(1,128)S(1)} %all_to_all.16.received_ref, f32[5,64,128]{2,1,0:T(8,128)S(1)} %get-tuple-element.50.fields_ref), custom_call_target="tpu_custom_call" | custom-call | tf_op jit(solution)/shard_map/pallas_call | solution.py:30
  100.1 0.0 copy-start.2
  100.2 0.0 copy-done
  100.2 0.0 copy-done.1
  100.2 0.6 copy-done.2
  100.8 0.7 while.9
  (2 shorter events, 0.0 us)
Async XLA Ops:
  3.5 42.6 %all-to-all-start = ((f32[32,64,128]{2,1,0:T(8,128)}), f32[32,64,128]{2,1,0:T(8,128)S(1)}, u32[]{:S(2)}, u32[]{:S(2)}) async-start(f32[32,64,128]{2,1,0:T(8,128)} %get-tuple-element.44), calls=%async_computation | async-start | bytes 2097152 | tf_op jit(solution)/shard_map/all_to_all | solution.py:353
  19.9 9.8 %collective-permute-start.10 = (f32[2,3,128,128]{3,2,1,0:T(8,128)S(1)}, f32[2,3,128,128]{3,2,1,0:T(8,128)S(1)}, u32[]{:S(2)}, u32[]{:S(2)}) collective-permute-start(f32[2,3,128,128]{3,2,1,0:T(8,128)S(1)} %bitcast.224), channel_id=1, source_target_pairs={{0,2},{1,15},{2,4},{3,1},{4,6},{5,3},{6,8},{7,5},{8,10},{9,7},{10,... | collective-permute-start | bytes 1179656 | tf_op jit(solution)/shard_map/ppermute | solution.py:249
  29.7 7.2 %collective-permute-start.11 = (f32[2,3,128,128]{3,2,1,0:T(8,128)S(1)}, f32[2,3,128,128]{3,2,1,0:T(8,128)S(1)}, u32[]{:S(2)}, u32[]{:S(2)}) collective-permute-start(f32[2,3,128,128]{3,2,1,0:T(8,128)S(1)} %collective-permute-done.10.refs_1_), channel_id=1, source_target_pairs={{0,1},{1,0},{2,3},{3,2},{4,5},{5,4},{6,7},{7,6},{8,9},{9,8},{10,11... | collective-permute-start | bytes 1179656 | tf_op jit(solution)/shard_map/ppermute | solution.py:251
  33.3 8.8 %collective-permute-start.12 = (f32[2,3,128,128]{3,2,1,0:T(8,128)S(1)}, f32[2,3,128,128]{3,2,1,0:T(8,128)S(1)}, u32[]{:S(2)}, u32[]{:S(2)}) collective-permute-start(f32[2,3,128,128]{3,2,1,0:T(8,128)S(1)} %collective-permute-done.10.refs_1_), channel_id=1, source_target_pairs={{0,2},{1,15},{2,4},{3,1},{4,6},{5,3},{6,8},{7,5},{8,10},{9,7},{10,... | collective-permute-start | bytes 1179656 | tf_op jit(solution)/shard_map/ppermute | solution.py:249
  42.1 23.8 %collective-permute-start.13 = (f32[2,3,128,128]{3,2,1,0:T(8,128)S(1)}, f32[2,3,128,128]{3,2,1,0:T(8,128)S(1)}, u32[]{:S(2)}, u32[]{:S(2)}) collective-permute-start(f32[2,3,128,128]{3,2,1,0:T(8,128)S(1)} %collective-permute-done.12.refs_3_), channel_id=1, source_target_pairs={{0,1},{1,0},{2,3},{3,2},{4,5},{5,4},{6,7},{7,6},{8,9},{9,8},{10,11... | collective-permute-start | bytes 1179656 | tf_op jit(solution)/shard_map/ppermute | solution.py:251
  98.5 1.7 %copy-start = (bf16[1,1,3,128,128]{4,3,2,1,0:T(8,128)(2,1)S(1)}, bf16[1,1,3,128,128]{4,3,2,1,0:T(8,128)(2,1)}, u32[]{:S(2)}) copy-start(bf16[1,1,3,128,128]{4,3,2,1,0:T(8,128)(2,1)} %param.15) | copy-start | bytes 294916
  98.5 1.7 %copy-start.1 = (bf16[1,1,128,128]{3,2,1,0:T(8,128)(2,1)S(1)}, bf16[1,1,128,128]{3,2,1,0:T(8,128)(2,1)}, u32[]{:S(2)}) copy-start(bf16[1,1,128,128]{3,2,1,0:T(8,128)(2,1)} %param.17) | copy-start | bytes 98308
  100.1 0.7 copy-start.2

commit v7 on v6

--- a/solution.py
+++ b/solution.py
@@ -46,15 +46,12 @@
 
 
 def ring_steps():
-    steps = [0]
-    for distance in range(1, REACH + 1):
-        steps += [distance, -distance]
-    return steps
+    return list(range(REACH + 1)) + [-distance for distance in range(1, REACH + 1)]
 
 
 def front_kernel(
     tile_ref, target_hbm, delay_hbm, link_hbm, near_hbm, jacobi_hbm, voltage_hbm, history_hbm, blocks_hbm,
-    bucket_ref, own_ref, kept_ref,
+    bucket_ref, own_ref, kept_ref, gates_ref,
     target_ref, delay_ref, link_ref, near_ref, jacobi_ref, voltage_ref, history_ref, blocks_ref, sems, block_sems,
 ):
     entries, chunks = blocks_ref.shape[0], block_sems.shape[0]
@@ -78,6 +75,8 @@
         copy.wait()
     jacobi = jacobi_ref[...]
     kept_ref[...] = jacobi
+    for side in range(2):
+        gates_ref[side : side + 1] = jnp.full((1, gates_ref.shape[1]), link_ref[side].astype(jnp.float32))
     for side, gate in enumerate((link_ref[0], 1, link_ref[1])):
         near = near_ref[side]
         product = jnp.dot(near, jacobi, preferred_element_type=jnp.float32)
@@ -96,6 +95,24 @@
             bucket_ref[target] = bucket_ref[target] + product
 
 
+def front_call(tile, inputs, tiles):
+    near, jacobi, voltage = inputs[3:6]
+    f32 = jnp.float32
+    spaces = [pltpu.SMEM] * 3 + [pltpu.VMEM] * 5
+    return call(
+        front_kernel,
+        (
+            jax.ShapeDtypeStruct((tiles,) + voltage.shape, f32),
+            jax.ShapeDtypeStruct(near.shape, f32),
+            jax.ShapeDtypeStruct(jacobi.shape, jacobi.dtype),
+            jax.ShapeDtypeStruct((2, jacobi.shape[0]), f32),
+        ),
+        "s" + "h" * len(inputs),
+        scratch_shapes=[space(x.shape, x.dtype) for space, x in zip(spaces, inputs)]
+        + [pltpu.SemaphoreType.DMA((len(inputs) - 1,)), pltpu.SemaphoreType.DMA((4,))],
+    )(tile, *inputs)
+
+
 def start_kernel(received_ref, jacobi_ref, out_ref):
     right_side = -jnp.sum(received_ref[...], axis=0)
     out_ref[...] = right_side + split_dot(right_side, jacobi_ref[...])
@@ -103,8 +120,9 @@
 
 def krylov_kernel(place_ref, start_ref, *refs):
     steps = ring_steps()
-    piece_refs = refs[: len(steps)]
-    gram_ref, own_ref, fields, parts, highs, lows, sums = refs[len(steps) :]
+    given_ref = refs[REACH + 1]
+    piece_refs = list(refs[: REACH + 1]) + [given_ref.at[i] for i in range(REACH)]
+    gram_ref, own_ref, fields, parts, highs, lows, sums = refs[REACH + 2 :]
     rows, scenarios, segments = start_ref.shape
     place = place_ref[0]
     core = lax.rem(place, CORES)
@@ -247,9 +265,8 @@
     pieces = [piece]
     for _ in range(REACH):
         piece = lax.ppermute(piece, "row", ring)
-        given, _ = lax.optimization_barrier((piece, pieces[-1]))
-        pieces += [piece, lax.ppermute(given, "row", swap)]
-    return pieces
+        pieces.append(piece)
+    return pieces + [lax.ppermute(jnp.stack(pieces[1:]), "row", swap)]
 
 
 def neighbours(field):
@@ -295,10 +312,9 @@
     return coeffs
 
 
-def stepwise_solve(initial, near, jacobi, link):
+def stepwise_solve(initial, near, jacobi, link_gain):
     near_f32 = near.astype(jnp.float32)
     jacobi_f32 = jacobi.astype(jnp.float32)
-    link_gain = link.astype(jnp.float32)
     start_norm = jnp.sqrt(lax.psum(jnp.sum(initial * initial, axis=1), ("tile", "row")))
     basis = [initial / start_norm[:, None]]
     zero_row = jnp.zeros_like(start_norm)
@@ -337,19 +353,10 @@
     f32 = jnp.float32
     field_shape = jax.ShapeDtypeStruct((scenarios, segments), f32)
 
-    inputs = (targets, delays, link, near, jacobi, voltage, history, far_blocks)
-    spaces = [pltpu.SMEM] * 3 + [pltpu.VMEM] * 5
-    bucket, own_blocks, jacobi_kept = call(
-        front_kernel,
-        (
-            jax.ShapeDtypeStruct((tiles, scenarios, segments), f32),
-            jax.ShapeDtypeStruct(near.shape, f32),
-            jax.ShapeDtypeStruct(jacobi.shape, jacobi.dtype),
-        ),
-        "s" + "h" * len(inputs),
-        scratch_shapes=[space(x.shape, x.dtype) for space, x in zip(spaces, inputs)]
-        + [pltpu.SemaphoreType.DMA((len(inputs) - 1,)), pltpu.SemaphoreType.DMA((4,))],
-    )(lax.axis_index("tile").astype(jnp.int32)[None], *inputs)
+    tile = lax.axis_index("tile").astype(jnp.int32)[None]
+    bucket, own_blocks, jacobi_kept, gates = front_call(
+        tile, (targets, delays, link, near, jacobi, voltage, history, far_blocks), tiles
+    )
     received = lax.all_to_all(bucket, "tile", split_axis=0, concat_axis=0, tiled=True)
     pieces = gather_blocks(own_blocks)
     initial = call(start_kernel, field_shape, "vv")(received, jacobi_kept)
@@ -367,7 +374,7 @@
     )(by_tile, own)
     safe, result = lax.while_loop(
         lambda state: state[0][0] < 0.5,
-        lambda state: (jnp.ones_like(state[0]), stepwise_solve(initial, near, jacobi, link)),
+        lambda state: (jnp.ones_like(state[0]), stepwise_solve(initial, near, jacobi_kept, gates)),
         (safe, result),
     )
     return result[None, None, None]

time: 103 us -> 101 us (0.981)
  starting transfers between devices: 30 us -> 28.6 us
    ppermute x2 -> x1, starting transfers between devices: 7.56 us -> 4.44 us  [gather_blocks(): return pieces + [lax.ppermute(jnp.stack(pieces[1:]), 'row', swap)]]
    ppermute x2, starting transfers between devices: 8.73 us -> 10.4 us  [gather_blocks(): piece = lax.ppermute(piece, 'row', ring)]
  transfers between devices with their start and end apart: 5 -> 4, of which waited for: 2 -> 2; matrix products, arithmetic and copies ran while one was open for 0% -> 1% of each run, Pallas kernels for 0% -> 0%
where the time goes in v7:
time: 101 us; the launch traced here: 100 us
  blocking collectives  52.4 us (52%)
  starting transfers between devices  28.6 us (28%)
  waiting for transfers between devices  9.4 us (9%)
  Pallas kernels  7.76 us (8%)
    all_gather x1, blocking collectives, per_device(): starts = lax.all_gather(initial, 'row')  20.5 us
    all_to_all x1, blocking collectives, per_device(): lax.all_to_all(group, 'tile', split_axis=0, concat_axis=0, tiled=True)  16.6 us
    all_to_all x1, starting transfers between devices, per_device(): lax.all_to_all(bucket, 'tile', split_axis=0, concat_axis=0, tiled=True)  13.7 us
    all_to_all x1, blocking collectives, per_device(): lax.all_to_all(gram, 'row', split_axis=0, concat_axis=0, tiled=True)  12.6 us
    ppermute x2, starting transfers between devices, gather_blocks(): piece = lax.ppermute(piece, 'row', ring)  10.4 us
    ppermute x2, waiting for transfers between devices, gather_blocks(): piece = lax.ppermute(piece, 'row', ring)  9.4 us
    pallas_call x5, Pallas kernels, placed(): run(*(pltpu.with_memory_space_constraint(x, pltpu.HBM) if c == 'h' else x...  7.76 us
    ppermute x1, starting transfers between devices, gather_blocks(): return pieces + [lax.ppermute(jnp.stack(pieces[1:]), 'row', swap)]  4.44 us
  transfers between devices with their start and end apart: 4, of which 2 were waited for; matrix products, arithmetic and copies ran while one was open for 1% of the time, Pallas kernels for 0%

profile of v7, /device:TPU:1, one launch (start us, length us, event | category | flops | bytes accessed | tf_op | source)
XLA Modules:
  0.0 100.1 jit_solution(3372937368522247280)
XLA Ops:
  0.0 3.5 %shard_map.82 = (f32[32,64,128]{2,1,0:T(8,128)}, f32[3,128,128]{2,1,0:T(8,128)S(1)}, bf16[128,128]{1,0:T(8,128)(2,1)S(1)}, f32[2,128]{1,0:T(2,128)S(1)}) custom-call(s32[1]{0:T(128)} %bitcast.35.tile_ref, s32[32]{0:T(128)} %bitcast.252, s32[32]{0:T(128)} %bitcast.253, s32[2]{0:T(128)} %bitcast.254, bf16[3,128,128]{2,1,0:T(8,128)(2,1)} %bitcast.232, ...), custom_call_target="tpu_custom_call" | custom-call | tf_op jit(solution)/shard_map/pallas_call | solution.py:30
  3.5 13.7 %all-to-all-start = ((f32[32,64,128]{2,1,0:T(8,128)}), f32[32,64,128]{2,1,0:T(8,128)S(1)}, u32[]{:S(2)}, u32[]{:S(2)}) async-start(f32[32,64,128]{2,1,0:T(8,128)} %get-tuple-element.43), calls=%async_computation | async-start | bytes 2097152 | tf_op jit(solution)/shard_map/all_to_all | solution.py:360
  17.2 2.7 %all-gather.1 = f32[6,128,128]{2,1,0:T(8,128)S(1)} all-gather(f32[3,128,128]{2,1,0:T(8,128)S(1)} %get-tuple-element.45), channel_id=3, replica_groups={{0,1},{2,3},{4,5},{6,7},{8,9},{10,11},{12,13},{14,15},{16,17},{18,19},{..., dimensions={0}, use_global_device_ids=true | all-gather | bytes 589824 | tf_op jit(solution)/shard_map/all_gather | solution.py:264
  19.9 5.1 %collective-permute-start.10 = (f32[2,3,128,128]{3,2,1,0:T(8,128)S(1)}, f32[2,3,128,128]{3,2,1,0:T(8,128)S(1)}, u32[]{:S(2)}, u32[]{:S(2)}) collective-permute-start(f32[2,3,128,128]{3,2,1,0:T(8,128)S(1)} %bitcast.228), channel_id=1, source_target_pairs={{0,2},{1,15},{2,4},{3,1},{4,6},{5,3},{6,8},{7,5},{8,10},{9,7},{10,... | collective-permute-start | bytes 1179656 | tf_op jit(solution)/shard_map/ppermute | solution.py:267
  25.0 4.7 %collective-permute-done.10.refs_1_ = f32[2,3,128,128]{3,2,1,0:T(8,128)S(1)} collective-permute-done((f32[2,3,128,128]{3,2,1,0:T(8,128)S(1)}, f32[2,3,128,128]{3,2,1,0:T(8,128)S(1)}, u32[]{:S(2)}, u32[]{:S(2)}) %collective-permute-start.10) | collective-permute-done | bytes 393248 | tf_op jit(solution)/shard_map/ppermute | solution.py:267
  29.7 5.3 %collective-permute-start.11 = (f32[2,3,128,128]{3,2,1,0:T(8,128)S(1)}, f32[2,3,128,128]{3,2,1,0:T(8,128)S(1)}, u32[]{:S(2)}, u32[]{:S(2)}) collective-permute-start(f32[2,3,128,128]{3,2,1,0:T(8,128)S(1)} %collective-permute-done.10.refs_1_), channel_id=1, source_target_pairs={{0,2},{1,15},{2,4},{3,1},{4,6},{5,3},{6,8},{7,5},{8,10},{9,7},{10,... | collective-permute-start | bytes 1179656 | tf_op jit(solution)/shard_map/ppermute | solution.py:267
  35.0 4.7 %collective-permute-done.11.refs_2_ = f32[2,3,128,128]{3,2,1,0:T(8,128)S(1)} collective-permute-done((f32[2,3,128,128]{3,2,1,0:T(8,128)S(1)}, f32[2,3,128,128]{3,2,1,0:T(8,128)S(1)}, u32[]{:S(2)}, u32[]{:S(2)}) %collective-permute-start.11) | collective-permute-done | bytes 393248 | tf_op jit(solution)/shard_map/ppermute | solution.py:267
  39.7 1.0 pad_maximum_fusion.3
  40.7 4.4 %collective-permute-start.12 = (f32[2,2,3,128,128]{4,3,2,1,0:T(8,128)}, f32[2,2,3,128,128]{4,3,2,1,0:T(8,128)S(1)}, u32[]{:S(2)}, u32[]{:S(2)}) collective-permute-start(f32[2,2,3,128,128]{4,3,2,1,0:T(8,128)} %pad_maximum_fusion.3), channel_id=1, source_target_pairs={{0,1},{1,0},{2,3},{3,2},{4,5},{5,4},{6,7},{7,6},{8,9},{9,8},{10,11... | collective-permute-start | bytes 2359304 | tf_op jit(solution)/shard_map/ppermute | solution.py:269
  45.1 0.0 all-to-all-done.received_ref
  45.1 0.2 shard_map.83
  45.3 20.5 %all-gather = f32[1024,128]{1,0:T(8,128)S(1)} all-gather(f32[64,128]{1,0:T(8,128)S(1)} %shard_map.83), channel_id=2, replica_groups=mesh['tile'=32,'row'=16] {'row'}, dimensions={0}, use_global_device_ids=true | all-gather | bytes 557056 | tf_op jit(solution)/shard_map/all_gather | solution.py:363
  65.9 0.0 collective-permute-done.12.refs_3_
  65.9 2.4 %shard_map.84 = (f32[16,1,1408]{2,1,0:T(1,128)S(1)}, f32[5,64,128]{2,1,0:T(8,128)S(1)}) custom-call(s32[1]{0:T(128)} %bitcast.34.place_ref, f32[16,64,128]{2,1,0:T(8,128)S(1)} %bitcast.227, f32[2,3,128,128]{3,2,1,0:T(8,128)S(1)} %bitcast.229, f32[2,3,128,128]{3,2,1,0:T(8,128)S(1)} %collective-permute-done.10.refs_1_, ...), custom_call_target="tpu_custom_call" | custom-call | tf_op jit(solution)/shard_map/pallas_call | solution.py:30
  68.3 12.6 %all_to_all.15.received_ref = f32[16,1,1408]{2,1,0:T(1,128)S(1)} all-to-all(f32[16,1,1408]{2,1,0:T(1,128)S(1)} %get-tuple-element.46), channel_id=1, replica_groups=mesh['tile'=32,'row'=16] {'row'}, dimensions={0} | all-to-all | bytes 180224 | tf_op jit(solution)/shard_map/all_to_all | solution.py:366
  80.9 0.1 shard_map.85
  80.9 16.6 %all_to_all.16.received_ref = f32[32,1,1408]{2,1,0:T(1,128)S(1)} all-to-all(f32[32,1,1408]{2,1,0:T(1,128)S(1)} %shard_map.85), channel_id=1, replica_groups=mesh['tile'=32,'row'=16] {'tile'}, dimensions={0} | all-to-all | bytes 360448 | tf_op jit(solution)/shard_map/all_to_all | solution.py:368
  97.6 0.0 copy-start
  97.6 1.6 %shard_map.86 = (f32[64,128]{1,0:T(8,128)}, f32[1]{0:T(128)}) custom-call(f32[32,1,1408]{2,1,0:T(1,128)S(1)} %all_to_all.16.received_ref, f32[5,64,128]{2,1,0:T(8,128)S(1)} %get-tuple-element.47.fields_ref), custom_call_target="tpu_custom_call" | custom-call | tf_op jit(solution)/shard_map/pallas_call | solution.py:30
  99.2 0.0 copy-done
  99.2 0.7 while.9
Async XLA Ops:
  3.5 41.6 %all-to-all-start = ((f32[32,64,128]{2,1,0:T(8,128)}), f32[32,64,128]{2,1,0:T(8,128)S(1)}, u32[]{:S(2)}, u32[]{:S(2)}) async-start(f32[32,64,128]{2,1,0:T(8,128)} %get-tuple-element.43), calls=%async_computation | async-start | bytes 2097152 | tf_op jit(solution)/shard_map/all_to_all | solution.py:360
  19.9 9.8 %collective-permute-start.10 = (f32[2,3,128,128]{3,2,1,0:T(8,128)S(1)}, f32[2,3,128,128]{3,2,1,0:T(8,128)S(1)}, u32[]{:S(2)}, u32[]{:S(2)}) collective-permute-start(f32[2,3,128,128]{3,2,1,0:T(8,128)S(1)} %bitcast.228), channel_id=1, source_target_pairs={{0,2},{1,15},{2,4},{3,1},{4,6},{5,3},{6,8},{7,5},{8,10},{9,7},{10,... | collective-permute-start | bytes 1179656 | tf_op jit(solution)/shard_map/ppermute | solution.py:267
  29.7 10.0 %collective-permute-start.11 = (f32[2,3,128,128]{3,2,1,0:T(8,128)S(1)}, f32[2,3,128,128]{3,2,1,0:T(8,128)S(1)}, u32[]{:S(2)}, u32[]{:S(2)}) collective-permute-start(f32[2,3,128,128]{3,2,1,0:T(8,128)S(1)} %collective-permute-done.10.refs_1_), channel_id=1, source_target_pairs={{0,2},{1,15},{2,4},{3,1},{4,6},{5,3},{6,8},{7,5},{8,10},{9,7},{10,... | collective-permute-start | bytes 1179656 | tf_op jit(solution)/shard_map/ppermute | solution.py:267
  40.7 25.2 %collective-permute-start.12 = (f32[2,2,3,128,128]{4,3,2,1,0:T(8,128)}, f32[2,2,3,128,128]{4,3,2,1,0:T(8,128)S(1)}, u32[]{:S(2)}, u32[]{:S(2)}) collective-permute-start(f32[2,2,3,128,128]{4,3,2,1,0:T(8,128)} %pad_maximum_fusion.3), channel_id=1, source_target_pairs={{0,1},{1,0},{2,3},{3,2},{4,5},{5,4},{6,7},{7,6},{8,9},{9,8},{10,11... | collective-permute-start | bytes 2359304 | tf_op jit(solution)/shard_map/ppermute | solution.py:269
  97.6 1.6 %copy-start = (bf16[1,1,3,128,128]{4,3,2,1,0:T(8,128)(2,1)S(1)}, bf16[1,1,3,128,128]{4,3,2,1,0:T(8,128)(2,1)}, u32[]{:S(2)}) copy-start(bf16[1,1,3,128,128]{4,3,2,1,0:T(8,128)(2,1)} %param.15) | copy-start | bytes 294916

commit v8 on v7

--- a/solution.py
+++ b/solution.py
@@ -199,6 +199,10 @@
     )(place, starts, *pieces)
 
 
+def hand_on_kernel(fields_ref, out_ref):
+    out_ref[...] = fields_ref[...]
+
+
 def add_kernel(received_ref, out_ref):
     total = jnp.sum(received_ref[...], axis=0)
     out_ref[...] = jnp.broadcast_to(total[None], out_ref.shape)
@@ -218,22 +222,24 @@
         safe = jnp.where(pivot > 0.0, safe, 0.0)
         safe = jnp.where(gram[i, i] < jnp.inf, safe, 0.0)
         factor[i, i] = jnp.sqrt(pivot)
+        inverse = 1.0 / factor[i, i]
         for j in range(i + 1, BASIS):
             entry = gram[i, j]
             for k in range(i):
                 entry = entry - factor[k, i] * factor[k, j]
-            factor[i, j] = entry / factor[i, i]
+            factor[i, j] = entry * inverse
     matrix = [[None] * ITERS for _ in range(BASIS)]
     for j in range(ITERS):
         for i in range(j + 1):
             matrix[i][j] = factor[i, j] + factor[i, j + 1]
         matrix[j + 1][j] = factor[j + 1, j + 1]
     target = [factor[0, 0]] + [None] * ITERS
+    inverses = [None] * ITERS
     for j in range(ITERS):
         diagonal, below = matrix[j][j], matrix[j + 1][j]
         radius = jnp.sqrt(diagonal * diagonal + below * below)
-        cosine, sine = diagonal / radius, below / radius
-        matrix[j][j] = radius
+        inverses[j] = 1.0 / radius
+        cosine, sine = diagonal * inverses[j], below * inverses[j]
         for k in range(j + 1, ITERS):
             upper, lower = matrix[j][k], matrix[j + 1][k]
             matrix[j][k] = cosine * upper + sine * lower
@@ -245,7 +251,7 @@
         partial = target[j]
         for k in range(j + 1, ITERS):
             partial = partial - matrix[j][k] * coeffs[k]
-        coeffs[j] = partial / matrix[j][j]
+        coeffs[j] = partial * inverses[j]
     padded = jnp.concatenate(coeffs + [jnp.zeros((8 - ITERS, scenarios), jnp.float32)], axis=0)
     padded = jnp.concatenate([padded, jnp.zeros((8, 128 - scenarios), jnp.float32)], axis=1)
     columns = jnp.transpose(padded)[:scenarios]
@@ -364,8 +370,11 @@
     place = lax.axis_index("row").astype(jnp.int32)[None]
     gram, own = krylov_call(place, starts, pieces)
     by_row = lax.all_to_all(gram, "row", split_axis=0, concat_axis=0, tiled=True)
+    own = call(hand_on_kernel, jax.ShapeDtypeStruct(own.shape, f32), "v")(own)
+    by_row, own = lax.optimization_barrier((by_row, own))
     group = call(add_kernel, jax.ShapeDtypeStruct((tiles,) + gram.shape[1:], f32), "v")(by_row)
     by_tile = lax.all_to_all(group, "tile", split_axis=0, concat_axis=0, tiled=True)
+    own = call(hand_on_kernel, jax.ShapeDtypeStruct(own.shape, f32), "v")(own)
     result, safe = call(
         solve_kernel,
         (field_shape, jax.ShapeDtypeStruct((1,), f32)),

time: 101 us -> 103 us (1.020)
  blocking collectives: 52.4 us -> 23.2 us
  waiting for transfers between devices: 9.4 us -> 27 us
  starting transfers between devices: 28.6 us -> 40.6 us
  Pallas kernels: 7.76 us -> 9.1 us
    all_to_all x2 -> x0, blocking collectives: 29.3 us -> none  [the longest x1 16.6 us: per_device(): lax.all_to_all(group, 'tile', split_axis=0, concat_axis=0, tiled=True)]
    all_to_all x0 -> x2, waiting for transfers between devices: none -> 17.6 us  [the longest x1 9.3 us: per_device(): lax.all_to_all(group, 'tile', split_axis=0, concat_axis=0, tiled=True)]
    all_to_all x0 -> x2, starting transfers between devices: none -> 12 us  [the longest x1 7.5 us: per_device(): lax.all_to_all(group, 'tile', split_axis=0, concat_axis=0, tiled=True)]
    pallas_call x5 -> x7, Pallas kernels: 7.76 us -> 9.1 us  [placed(): run(*(pltpu.with_memory_space_constraint(x, pltpu.HBM) if c == 'h' else x...]
  transfers between devices with their start and end apart: 4 -> 6, of which waited for: 2 -> 4; matrix products, arithmetic and copies ran while one was open for 1% -> 1% of each run, Pallas kernels for 0% -> 0%
where the time goes in v8:
time: 103 us; the launch traced here: 102 us
  starting transfers between devices  40.6 us (39%)
  waiting for transfers between devices  27 us (26%)
  blocking collectives  23.2 us (23%)
  Pallas kernels  9.1 us (9%)
    all_gather x1, blocking collectives, per_device(): starts = lax.all_gather(initial, 'row')  20.5 us
    all_to_all x1, starting transfers between devices, per_device(): lax.all_to_all(bucket, 'tile', split_axis=0, concat_axis=0, tiled=True)  13.7 us
    ppermute x2, starting transfers between devices, gather_blocks(): piece = lax.ppermute(piece, 'row', ring)  10.4 us
    ppermute x2, waiting for transfers between devices, gather_blocks(): piece = lax.ppermute(piece, 'row', ring)  9.4 us
    all_to_all x1, waiting for transfers between devices, per_device(): lax.all_to_all(group, 'tile', split_axis=0, concat_axis=0, tiled=True)  9.3 us
    pallas_call x7, Pallas kernels, placed(): run(*(pltpu.with_memory_space_constraint(x, pltpu.HBM) if c == 'h' else x...  9.1 us
    all_to_all x1, waiting for transfers between devices, per_device(): lax.all_to_all(gram, 'row', split_axis=0, concat_axis=0, tiled=True)  8.3 us
    all_to_all x1, starting transfers between devices, per_device(): lax.all_to_all(group, 'tile', split_axis=0, concat_axis=0, tiled=True)  7.5 us
  transfers between devices with their start and end apart: 6, of which 4 were waited for; matrix products, arithmetic and copies ran while one was open for 1% of the time, Pallas kernels for 0%

profile of v8, /device:TPU:1, one launch (start us, length us, event | category | flops | bytes accessed | tf_op | source)
XLA Modules:
  0.0 101.8 jit_solution(2208194602155518480)
XLA Ops:
  0.0 3.5 %shard_map.82 = (f32[32,64,128]{2,1,0:T(8,128)}, f32[3,128,128]{2,1,0:T(8,128)S(1)}, bf16[128,128]{1,0:T(8,128)(2,1)S(1)}, f32[2,128]{1,0:T(2,128)S(1)}) custom-call(s32[1]{0:T(128)} %bitcast.35.tile_ref, s32[32]{0:T(128)} %bitcast.252, s32[32]{0:T(128)} %bitcast.253, s32[2]{0:T(128)} %bitcast.254, bf16[3,128,128]{2,1,0:T(8,128)(2,1)} %bitcast.232, ...), custom_call_target="tpu_custom_call" | custom-call | tf_op jit(solution)/shard_map/pallas_call | solution.py:30
  3.5 13.7 %all-to-all-start = ((f32[32,64,128]{2,1,0:T(8,128)}), f32[32,64,128]{2,1,0:T(8,128)S(1)}, u32[]{:S(2)}, u32[]{:S(2)}) async-start(f32[32,64,128]{2,1,0:T(8,128)} %get-tuple-element.45), calls=%async_computation | async-start | bytes 2097152 | tf_op jit(solution)/shard_map/all_to_all | solution.py:366
  17.2 2.7 %all-gather.1 = f32[6,128,128]{2,1,0:T(8,128)S(1)} all-gather(f32[3,128,128]{2,1,0:T(8,128)S(1)} %get-tuple-element.47), channel_id=3, replica_groups={{0,1},{2,3},{4,5},{6,7},{8,9},{10,11},{12,13},{14,15},{16,17},{18,19},{..., dimensions={0}, use_global_device_ids=true | all-gather | bytes 589824 | tf_op jit(solution)/shard_map/all_gather | solution.py:270
  19.9 5.1 %collective-permute-start.10 = (f32[2,3,128,128]{3,2,1,0:T(8,128)S(1)}, f32[2,3,128,128]{3,2,1,0:T(8,128)S(1)}, u32[]{:S(2)}, u32[]{:S(2)}) collective-permute-start(f32[2,3,128,128]{3,2,1,0:T(8,128)S(1)} %bitcast.228), channel_id=1, source_target_pairs={{0,2},{1,15},{2,4},{3,1},{4,6},{5,3},{6,8},{7,5},{8,10},{9,7},{10,... | collective-permute-start | bytes 1179656 | tf_op jit(solution)/shard_map/ppermute | solution.py:273
  25.0 4.7 %collective-permute-done.10.refs_1_ = f32[2,3,128,128]{3,2,1,0:T(8,128)S(1)} collective-permute-done((f32[2,3,128,128]{3,2,1,0:T(8,128)S(1)}, f32[2,3,128,128]{3,2,1,0:T(8,128)S(1)}, u32[]{:S(2)}, u32[]{:S(2)}) %collective-permute-start.10) | collective-permute-done | bytes 393248 | tf_op jit(solution)/shard_map/ppermute | solution.py:273
  29.7 5.3 %collective-permute-start.11 = (f32[2,3,128,128]{3,2,1,0:T(8,128)S(1)}, f32[2,3,128,128]{3,2,1,0:T(8,128)S(1)}, u32[]{:S(2)}, u32[]{:S(2)}) collective-permute-start(f32[2,3,128,128]{3,2,1,0:T(8,128)S(1)} %collective-permute-done.10.refs_1_), channel_id=1, source_target_pairs={{0,2},{1,15},{2,4},{3,1},{4,6},{5,3},{6,8},{7,5},{8,10},{9,7},{10,... | collective-permute-start | bytes 1179656 | tf_op jit(solution)/shard_map/ppermute | solution.py:273
  35.0 4.7 %collective-permute-done.11.refs_2_ = f32[2,3,128,128]{3,2,1,0:T(8,128)S(1)} collective-permute-done((f32[2,3,128,128]{3,2,1,0:T(8,128)S(1)}, f32[2,3,128,128]{3,2,1,0:T(8,128)S(1)}, u32[]{:S(2)}, u32[]{:S(2)}) %collective-permute-start.11) | collective-permute-done | bytes 393248 | tf_op jit(solution)/shard_map/ppermute | solution.py:273
  39.7 1.0 pad_maximum_fusion.3
  40.7 4.4 %collective-permute-start.12 = (f32[2,2,3,128,128]{4,3,2,1,0:T(8,128)}, f32[2,2,3,128,128]{4,3,2,1,0:T(8,128)S(1)}, u32[]{:S(2)}, u32[]{:S(2)}) collective-permute-start(f32[2,2,3,128,128]{4,3,2,1,0:T(8,128)} %pad_maximum_fusion.3), channel_id=1, source_target_pairs={{0,1},{1,0},{2,3},{3,2},{4,5},{5,4},{6,7},{7,6},{8,9},{9,8},{10,11... | collective-permute-start | bytes 2359304 | tf_op jit(solution)/shard_map/ppermute | solution.py:275
  45.1 0.0 all-to-all-done.received_ref
  45.1 0.2 shard_map.83
  45.3 20.5 %all-gather = f32[1024,128]{1,0:T(8,128)S(1)} all-gather(f32[64,128]{1,0:T(8,128)S(1)} %shard_map.83), channel_id=2, replica_groups=mesh['tile'=32,'row'=16] {'row'}, dimensions={0}, use_global_device_ids=true | all-gather | bytes 557056 | tf_op jit(solution)/shard_map/all_gather | solution.py:369
  65.9 0.0 collective-permute-done.12.refs_3_
  65.9 3.1 %shard_map.84 = (f32[16,1,1408]{2,1,0:T(1,128)}, f32[5,64,128]{2,1,0:T(8,128)S(1)}) custom-call(s32[1]{0:T(128)} %bitcast.34.place_ref, f32[16,64,128]{2,1,0:T(8,128)S(1)} %bitcast.227, f32[2,3,128,128]{3,2,1,0:T(8,128)S(1)} %bitcast.229, f32[2,3,128,128]{3,2,1,0:T(8,128)S(1)} %collective-permute-done.10.refs_1_, ...), custom_call_target="tpu_custom_call" | custom-call | tf_op jit(solution)/shard_map/pallas_call | solution.py:30
  68.9 4.5 %all-to-all-start.1 = ((f32[16,1,1408]{2,1,0:T(1,128)}), f32[16,1,1408]{2,1,0:T(1,128)S(1)}, u32[]{:S(2)}, u32[]{:S(2)}) async-start(f32[16,1,1408]{2,1,0:T(1,128)} %get-tuple-element.48), calls=%async_computation.1 | async-start | bytes 180224 | tf_op jit(solution)/shard_map/all_to_all | solution.py:372
  73.4 8.3 %all-to-all-done.1.received_ref = f32[16,1,1408]{2,1,0:T(1,128)S(1)} async-done(((f32[16,1,1408]{2,1,0:T(1,128)}), f32[16,1,1408]{2,1,0:T(1,128)S(1)}, u32[]{:S(2)}, u32[]{:S(2)}) %all-to-all-start.1) | async-done | bytes 90144 | tf_op jit(solution)/shard_map/all_to_all | solution.py:372
  81.7 0.7 shard_map.86
  82.5 7.5 %all-to-all-start.2 = ((f32[32,1,1408]{2,1,0:T(1,128)}), f32[32,1,1408]{2,1,0:T(1,128)S(1)}, u32[]{:S(2)}, u32[]{:S(2)}) async-start(f32[32,1,1408]{2,1,0:T(1,128)} %shard_map.86), calls=%async_computation.2 | async-start | bytes 360448 | tf_op jit(solution)/shard_map/all_to_all | solution.py:376
  90.0 0.0 copy-start
  90.0 9.3 %all-to-all-done.2.received_ref = f32[32,1,1408]{2,1,0:T(1,128)S(1)} async-done(((f32[32,1,1408]{2,1,0:T(1,128)}), f32[32,1,1408]{2,1,0:T(1,128)S(1)}, u32[]{:S(2)}, u32[]{:S(2)}) %all-to-all-start.2) | async-done | bytes 180256 | tf_op jit(solution)/shard_map/all_to_all | solution.py:376
  99.3 1.6 %shard_map.88 = (f32[64,128]{1,0:T(8,128)}, f32[1]{0:T(128)}) custom-call(f32[32,1,1408]{2,1,0:T(1,128)S(1)} %all-to-all-done.2.received_ref, f32[5,64,128]{2,1,0:T(8,128)S(1)} %shard_map.87.fields_ref), custom_call_target="tpu_custom_call" | custom-call | tf_op jit(solution)/shard_map/pallas_call | solution.py:30
  100.9 0.0 copy-done
  100.9 0.7 while.9
  (2 shorter events, 0.0 us)
Async XLA Ops:
  3.5 41.6 %all-to-all-start = ((f32[32,64,128]{2,1,0:T(8,128)}), f32[32,64,128]{2,1,0:T(8,128)S(1)}, u32[]{:S(2)}, u32[]{:S(2)}) async-start(f32[32,64,128]{2,1,0:T(8,128)} %get-tuple-element.45), calls=%async_computation | async-start | bytes 2097152 | tf_op jit(solution)/shard_map/all_to_all | solution.py:366
  19.9 9.8 %collective-permute-start.10 = (f32[2,3,128,128]{3,2,1,0:T(8,128)S(1)}, f32[2,3,128,128]{3,2,1,0:T(8,128)S(1)}, u32[]{:S(2)}, u32[]{:S(2)}) collective-permute-start(f32[2,3,128,128]{3,2,1,0:T(8,128)S(1)} %bitcast.228), channel_id=1, source_target_pairs={{0,2},{1,15},{2,4},{3,1},{4,6},{5,3},{6,8},{7,5},{8,10},{9,7},{10,... | collective-permute-start | bytes 1179656 | tf_op jit(solution)/shard_map/ppermute | solution.py:273
  29.7 10.0 %collective-permute-start.11 = (f32[2,3,128,128]{3,2,1,0:T(8,128)S(1)}, f32[2,3,128,128]{3,2,1,0:T(8,128)S(1)}, u32[]{:S(2)}, u32[]{:S(2)}) collective-permute-start(f32[2,3,128,128]{3,2,1,0:T(8,128)S(1)} %collective-permute-done.10.refs_1_), channel_id=1, source_target_pairs={{0,2},{1,15},{2,4},{3,1},{4,6},{5,3},{6,8},{7,5},{8,10},{9,7},{10,... | collective-permute-start | bytes 1179656 | tf_op jit(solution)/shard_map/ppermute | solution.py:273
  40.7 25.2 %collective-permute-start.12 = (f32[2,2,3,128,128]{4,3,2,1,0:T(8,128)}, f32[2,2,3,128,128]{4,3,2,1,0:T(8,128)S(1)}, u32[]{:S(2)}, u32[]{:S(2)}) collective-permute-start(f32[2,2,3,128,128]{4,3,2,1,0:T(8,128)} %pad_maximum_fusion.3), channel_id=1, source_target_pairs={{0,1},{1,0},{2,3},{3,2},{4,5},{5,4},{6,7},{7,6},{8,9},{9,8},{10,11... | collective-permute-start | bytes 2359304 | tf_op jit(solution)/shard_map/ppermute | solution.py:275
  68.9 12.8 %all-to-all-start.1 = ((f32[16,1,1408]{2,1,0:T(1,128)}), f32[16,1,1408]{2,1,0:T(1,128)S(1)}, u32[]{:S(2)}, u32[]{:S(2)}) async-start(f32[16,1,1408]{2,1,0:T(1,128)} %get-tuple-element.48), calls=%async_computation.1 | async-start | bytes 180224 | tf_op jit(solution)/shard_map/all_to_all | solution.py:372
  82.5 16.8 %all-to-all-start.2 = ((f32[32,1,1408]{2,1,0:T(1,128)}), f32[32,1,1408]{2,1,0:T(1,128)S(1)}, u32[]{:S(2)}, u32[]{:S(2)}) async-start(f32[32,1,1408]{2,1,0:T(1,128)} %shard_map.86), calls=%async_computation.2 | async-start | bytes 360448 | tf_op jit(solution)/shard_map/all_to_all | solution.py:376
  90.0 10.9 %copy-start = (bf16[1,1,3,128,128]{4,3,2,1,0:T(8,128)(2,1)S(1)}, bf16[1,1,3,128,128]{4,3,2,1,0:T(8,128)(2,1)}, u32[]{:S(2)}) copy-start(bf16[1,1,3,128,128]{4,3,2,1,0:T(8,128)(2,1)} %param.15) | copy-start | bytes 294916

commit v9 on v7

--- a/solution.py
+++ b/solution.py
@@ -109,7 +109,7 @@
         ),
         "s" + "h" * len(inputs),
         scratch_shapes=[space(x.shape, x.dtype) for space, x in zip(spaces, inputs)]
-        + [pltpu.SemaphoreType.DMA((len(inputs) - 1,)), pltpu.SemaphoreType.DMA((4,))],
+        + [pltpu.SemaphoreType.DMA((len(inputs) - 1,)), pltpu.SemaphoreType.DMA((1,))],
     )(tile, *inputs)
 
 

time: 101 us -> 100 us (0.990)
  no operation moved by 1% of the time
where the time goes in v9:
time: 100 us; the launch traced here: 99.6 us
  blocking collectives  52.4 us (52%)
  starting transfers between devices  28.6 us (29%)
  waiting for transfers between devices  9.4 us (9%)
  Pallas kernels  7.24 us (7%)
    all_gather x1, blocking collectives, per_device(): starts = lax.all_gather(initial, 'row')  20.5 us
    all_to_all x1, blocking collectives, per_device(): lax.all_to_all(group, 'tile', split_axis=0, concat_axis=0, tiled=True)  16.6 us
    all_to_all x1, starting transfers between devices, per_device(): lax.all_to_all(bucket, 'tile', split_axis=0, concat_axis=0, tiled=True)  13.7 us
    all_to_all x1, blocking collectives, per_device(): lax.all_to_all(gram, 'row', split_axis=0, concat_axis=0, tiled=True)  12.6 us
    ppermute x2, starting transfers between devices, gather_blocks(): piece = lax.ppermute(piece, 'row', ring)  10.4 us
    ppermute x2, waiting for transfers between devices, gather_blocks(): piece = lax.ppermute(piece, 'row', ring)  9.4 us
    pallas_call x5, Pallas kernels, placed(): run(*(pltpu.with_memory_space_constraint(x, pltpu.HBM) if c == 'h' else x...  7.24 us
    ppermute x1, starting transfers between devices, gather_blocks(): return pieces + [lax.ppermute(jnp.stack(pieces[1:]), 'row', swap)]  4.44 us
  transfers between devices with their start and end apart: 4, of which 2 were waited for; matrix products, arithmetic and copies ran while one was open for 1% of the time, Pallas kernels for 0%

profile of v9, /device:TPU:1, one launch (start us, length us, event | category | flops | bytes accessed | tf_op | source)
XLA Modules:
  0.0 99.6 jit_solution(322650286274988551)
XLA Ops:
  0.0 3.0 %shard_map.82 = (f32[32,64,128]{2,1,0:T(8,128)}, f32[3,128,128]{2,1,0:T(8,128)S(1)}, bf16[128,128]{1,0:T(8,128)(2,1)S(1)}, f32[2,128]{1,0:T(2,128)S(1)}) custom-call(s32[1]{0:T(128)} %bitcast.35.tile_ref, s32[32]{0:T(128)} %bitcast.252, s32[32]{0:T(128)} %bitcast.253, s32[2]{0:T(128)} %bitcast.254, bf16[3,128,128]{2,1,0:T(8,128)(2,1)} %bitcast.232, ...), custom_call_target="tpu_custom_call" | custom-call | tf_op jit(solution)/shard_map/pallas_call | solution.py:30
  3.0 13.7 %all-to-all-start = ((f32[32,64,128]{2,1,0:T(8,128)}), f32[32,64,128]{2,1,0:T(8,128)S(1)}, u32[]{:S(2)}, u32[]{:S(2)}) async-start(f32[32,64,128]{2,1,0:T(8,128)} %get-tuple-element.43), calls=%async_computation | async-start | bytes 2097152 | tf_op jit(solution)/shard_map/all_to_all | solution.py:360
  16.7 2.7 %all-gather.1 = f32[6,128,128]{2,1,0:T(8,128)S(1)} all-gather(f32[3,128,128]{2,1,0:T(8,128)S(1)} %get-tuple-element.45), channel_id=3, replica_groups={{0,1},{2,3},{4,5},{6,7},{8,9},{10,11},{12,13},{14,15},{16,17},{18,19},{..., dimensions={0}, use_global_device_ids=true | all-gather | bytes 589824 | tf_op jit(solution)/shard_map/all_gather | solution.py:264
  19.4 5.1 %collective-permute-start.10 = (f32[2,3,128,128]{3,2,1,0:T(8,128)S(1)}, f32[2,3,128,128]{3,2,1,0:T(8,128)S(1)}, u32[]{:S(2)}, u32[]{:S(2)}) collective-permute-start(f32[2,3,128,128]{3,2,1,0:T(8,128)S(1)} %bitcast.228), channel_id=1, source_target_pairs={{0,2},{1,15},{2,4},{3,1},{4,6},{5,3},{6,8},{7,5},{8,10},{9,7},{10,... | collective-permute-start | bytes 1179656 | tf_op jit(solution)/shard_map/ppermute | solution.py:267
  24.5 4.7 %collective-permute-done.10.refs_1_ = f32[2,3,128,128]{3,2,1,0:T(8,128)S(1)} collective-permute-done((f32[2,3,128,128]{3,2,1,0:T(8,128)S(1)}, f32[2,3,128,128]{3,2,1,0:T(8,128)S(1)}, u32[]{:S(2)}, u32[]{:S(2)}) %collective-permute-start.10) | collective-permute-done | bytes 393248 | tf_op jit(solution)/shard_map/ppermute | solution.py:267
  29.2 5.3 %collective-permute-start.11 = (f32[2,3,128,128]{3,2,1,0:T(8,128)S(1)}, f32[2,3,128,128]{3,2,1,0:T(8,128)S(1)}, u32[]{:S(2)}, u32[]{:S(2)}) collective-permute-start(f32[2,3,128,128]{3,2,1,0:T(8,128)S(1)} %collective-permute-done.10.refs_1_), channel_id=1, source_target_pairs={{0,2},{1,15},{2,4},{3,1},{4,6},{5,3},{6,8},{7,5},{8,10},{9,7},{10,... | collective-permute-start | bytes 1179656 | tf_op jit(solution)/shard_map/ppermute | solution.py:267
  34.5 4.7 %collective-permute-done.11.refs_2_ = f32[2,3,128,128]{3,2,1,0:T(8,128)S(1)} collective-permute-done((f32[2,3,128,128]{3,2,1,0:T(8,128)S(1)}, f32[2,3,128,128]{3,2,1,0:T(8,128)S(1)}, u32[]{:S(2)}, u32[]{:S(2)}) %collective-permute-start.11) | collective-permute-done | bytes 393248 | tf_op jit(solution)/shard_map/ppermute | solution.py:267
  39.2 1.0 pad_maximum_fusion.3
  40.2 4.4 %collective-permute-start.12 = (f32[2,2,3,128,128]{4,3,2,1,0:T(8,128)}, f32[2,2,3,128,128]{4,3,2,1,0:T(8,128)S(1)}, u32[]{:S(2)}, u32[]{:S(2)}) collective-permute-start(f32[2,2,3,128,128]{4,3,2,1,0:T(8,128)} %pad_maximum_fusion.3), channel_id=1, source_target_pairs={{0,1},{1,0},{2,3},{3,2},{4,5},{5,4},{6,7},{7,6},{8,9},{9,8},{10,11... | collective-permute-start | bytes 2359304 | tf_op jit(solution)/shard_map/ppermute | solution.py:269
  44.6 0.0 all-to-all-done.received_ref
  44.6 0.2 shard_map.83
  44.8 20.5 %all-gather = f32[1024,128]{1,0:T(8,128)S(1)} all-gather(f32[64,128]{1,0:T(8,128)S(1)} %shard_map.83), channel_id=2, replica_groups=mesh['tile'=32,'row'=16] {'row'}, dimensions={0}, use_global_device_ids=true | all-gather | bytes 557056 | tf_op jit(solution)/shard_map/all_gather | solution.py:363
  65.3 0.0 collective-permute-done.12.refs_3_
  65.3 2.4 %shard_map.84 = (f32[16,1,1408]{2,1,0:T(1,128)S(1)}, f32[5,64,128]{2,1,0:T(8,128)S(1)}) custom-call(s32[1]{0:T(128)} %bitcast.34.place_ref, f32[16,64,128]{2,1,0:T(8,128)S(1)} %bitcast.227, f32[2,3,128,128]{3,2,1,0:T(8,128)S(1)} %bitcast.229, f32[2,3,128,128]{3,2,1,0:T(8,128)S(1)} %collective-permute-done.10.refs_1_, ...), custom_call_target="tpu_custom_call" | custom-call | tf_op jit(solution)/shard_map/pallas_call | solution.py:30
  67.7 12.6 %all_to_all.15.received_ref = f32[16,1,1408]{2,1,0:T(1,128)S(1)} all-to-all(f32[16,1,1408]{2,1,0:T(1,128)S(1)} %get-tuple-element.46), channel_id=1, replica_groups=mesh['tile'=32,'row'=16] {'row'}, dimensions={0} | all-to-all | bytes 180224 | tf_op jit(solution)/shard_map/all_to_all | solution.py:366
  80.3 0.1 shard_map.85
  80.4 16.6 %all_to_all.16.received_ref = f32[32,1,1408]{2,1,0:T(1,128)S(1)} all-to-all(f32[32,1,1408]{2,1,0:T(1,128)S(1)} %shard_map.85), channel_id=1, replica_groups=mesh['tile'=32,'row'=16] {'tile'}, dimensions={0} | all-to-all | bytes 360448 | tf_op jit(solution)/shard_map/all_to_all | solution.py:368
  97.0 0.0 copy-start
  97.0 1.6 %shard_map.86 = (f32[64,128]{1,0:T(8,128)}, f32[1]{0:T(128)}) custom-call(f32[32,1,1408]{2,1,0:T(1,128)S(1)} %all_to_all.16.received_ref, f32[5,64,128]{2,1,0:T(8,128)S(1)} %get-tuple-element.47.fields_ref), custom_call_target="tpu_custom_call" | custom-call | tf_op jit(solution)/shard_map/pallas_call | solution.py:30
  98.7 0.0 copy-done
  98.7 0.7 while.9
Async XLA Ops:
  3.0 41.6 %all-to-all-start = ((f32[32,64,128]{2,1,0:T(8,128)}), f32[32,64,128]{2,1,0:T(8,128)S(1)}, u32[]{:S(2)}, u32[]{:S(2)}) async-start(f32[32,64,128]{2,1,0:T(8,128)} %get-tuple-element.43), calls=%async_computation | async-start | bytes 2097152 | tf_op jit(solution)/shard_map/all_to_all | solution.py:360
  19.4 9.8 %collective-permute-start.10 = (f32[2,3,128,128]{3,2,1,0:T(8,128)S(1)}, f32[2,3,128,128]{3,2,1,0:T(8,128)S(1)}, u32[]{:S(2)}, u32[]{:S(2)}) collective-permute-start(f32[2,3,128,128]{3,2,1,0:T(8,128)S(1)} %bitcast.228), channel_id=1, source_target_pairs={{0,2},{1,15},{2,4},{3,1},{4,6},{5,3},{6,8},{7,5},{8,10},{9,7},{10,... | collective-permute-start | bytes 1179656 | tf_op jit(solution)/shard_map/ppermute | solution.py:267
  29.2 10.0 %collective-permute-start.11 = (f32[2,3,128,128]{3,2,1,0:T(8,128)S(1)}, f32[2,3,128,128]{3,2,1,0:T(8,128)S(1)}, u32[]{:S(2)}, u32[]{:S(2)}) collective-permute-start(f32[2,3,128,128]{3,2,1,0:T(8,128)S(1)} %collective-permute-done.10.refs_1_), channel_id=1, source_target_pairs={{0,2},{1,15},{2,4},{3,1},{4,6},{5,3},{6,8},{7,5},{8,10},{9,7},{10,... | collective-permute-start | bytes 1179656 | tf_op jit(solution)/shard_map/ppermute | solution.py:267
  40.2 25.2 %collective-permute-start.12 = (f32[2,2,3,128,128]{4,3,2,1,0:T(8,128)}, f32[2,2,3,128,128]{4,3,2,1,0:T(8,128)S(1)}, u32[]{:S(2)}, u32[]{:S(2)}) collective-permute-start(f32[2,2,3,128,128]{4,3,2,1,0:T(8,128)} %pad_maximum_fusion.3), channel_id=1, source_target_pairs={{0,1},{1,0},{2,3},{3,2},{4,5},{5,4},{6,7},{7,6},{8,9},{9,8},{10,11... | collective-permute-start | bytes 2359304 | tf_op jit(solution)/shard_map/ppermute | solution.py:269
  97.0 1.6 %copy-start = (bf16[1,1,3,128,128]{4,3,2,1,0:T(8,128)(2,1)S(1)}, bf16[1,1,3,128,128]{4,3,2,1,0:T(8,128)(2,1)}, u32[]{:S(2)}) copy-start(bf16[1,1,3,128,128]{4,3,2,1,0:T(8,128)(2,1)} %param.15) | copy-start | bytes 294916

commit v10 on v9

--- a/solution.py
+++ b/solution.py
@@ -177,7 +177,7 @@
         own_ref[j] = fields[j]
 
 
-def krylov_call(place, starts, pieces):
+def krylov_call(place, starts, pieces, tiles=32):
     rows, scenarios, segments = starts.shape
     f32, bf16 = jnp.float32, jnp.bfloat16
     padded_pairs = -(-len(PAIRS) * scenarios // 128) * 128 // scenarios
@@ -185,7 +185,7 @@
     return call(
         krylov_kernel,
         (
-            jax.ShapeDtypeStruct((rows, 1, padded_pairs * scenarios), f32),
+            jax.ShapeDtypeStruct((tiles, 1, padded_pairs * scenarios), f32),
             jax.ShapeDtypeStruct((ITERS, scenarios, segments), f32),
         ),
         "sv" + "v" * len(pieces),
@@ -362,16 +362,16 @@
     initial = call(start_kernel, field_shape, "vv")(received, jacobi_kept)
     starts = lax.all_gather(initial, "row")
     place = lax.axis_index("row").astype(jnp.int32)[None]
-    gram, own = krylov_call(place, starts, pieces)
-    by_row = lax.all_to_all(gram, "row", split_axis=0, concat_axis=0, tiled=True)
-    group = call(add_kernel, jax.ShapeDtypeStruct((tiles,) + gram.shape[1:], f32), "v")(by_row)
-    by_tile = lax.all_to_all(group, "tile", split_axis=0, concat_axis=0, tiled=True)
+    gram, own = krylov_call(place, starts, pieces, tiles)
+    by_tile = lax.all_to_all(gram, "tile", split_axis=0, concat_axis=0, tiled=True)
+    group = call(add_kernel, jax.ShapeDtypeStruct((rows,) + gram.shape[1:], f32), "v")(by_tile)
+    by_row = lax.all_to_all(group, "row", split_axis=0, concat_axis=0, tiled=True)
     result, safe = call(
         solve_kernel,
         (field_shape, jax.ShapeDtypeStruct((1,), f32)),
         "vv",
         out_specs=(pl.BlockSpec(memory_space=pltpu.VMEM), pl.BlockSpec(memory_space=pltpu.SMEM)),
-    )(by_tile, own)
+    )(by_row, own)
     safe, result = lax.while_loop(
         lambda state: state[0][0] < 0.5,
         lambda state: (jnp.ones_like(state[0]), stepwise_solve(initial, near, jacobi_kept, gates)),

time: 100 us -> 103 us (1.030)
  blocking collectives: 52.4 us -> 55 us
    all_to_all x2, blocking collectives: 29.2 us -> 31.8 us  [the longest x1 16.7 us: per_device(): lax.all_to_all(group, 'row', split_axis=0, concat_axis=0, tiled=True)]
where the time goes in v10:
time: 103 us; the launch traced here: 102 us
  blocking collectives  55 us (53%)
  starting transfers between devices  28.6 us (28%)
  waiting for transfers between devices  9.4 us (9%)
  Pallas kernels  7.29 us (7%)
    all_gather x1, blocking collectives, per_device(): starts = lax.all_gather(initial, 'row')  20.5 us
    all_to_all x1, blocking collectives, per_device(): lax.all_to_all(group, 'row', split_axis=0, concat_axis=0, tiled=True)  16.7 us
    all_to_all x1, blocking collectives, per_device(): lax.all_to_all(gram, 'tile', split_axis=0, concat_axis=0, tiled=True)  15.1 us
    all_to_all x1, starting transfers between devices, per_device(): lax.all_to_all(bucket, 'tile', split_axis=0, concat_axis=0, tiled=True)  13.7 us
    ppermute x2, starting transfers between devices, gather_blocks(): piece = lax.ppermute(piece, 'row', ring)  10.4 us
    ppermute x2, waiting for transfers between devices, gather_blocks(): piece = lax.ppermute(piece, 'row', ring)  9.4 us
    pallas_call x5, Pallas kernels, placed(): run(*(pltpu.with_memory_space_constraint(x, pltpu.HBM) if c == 'h' else x...  7.29 us
    ppermute x1, starting transfers between devices, gather_blocks(): return pieces + [lax.ppermute(jnp.stack(pieces[1:]), 'row', swap)]  4.44 us
  transfers between devices with their start and end apart: 4, of which 2 were waited for; matrix products, arithmetic and copies ran while one was open for 1% of the time, Pallas kernels for 0%

profile of v10, /device:TPU:1, one launch (start us, length us, event | category | flops | bytes accessed | tf_op | source)
XLA Modules:
  0.0 102.3 jit_solution(4425053914311416010)
XLA Ops:
  0.0 3.0 %shard_map.82 = (f32[32,64,128]{2,1,0:T(8,128)}, f32[3,128,128]{2,1,0:T(8,128)S(1)}, bf16[128,128]{1,0:T(8,128)(2,1)S(1)}, f32[2,128]{1,0:T(2,128)S(1)}) custom-call(s32[1]{0:T(128)} %bitcast.35.tile_ref, s32[32]{0:T(128)} %bitcast.252, s32[32]{0:T(128)} %bitcast.253, s32[2]{0:T(128)} %bitcast.254, bf16[3,128,128]{2,1,0:T(8,128)(2,1)} %bitcast.232, ...), custom_call_target="tpu_custom_call" | custom-call | tf_op jit(solution)/shard_map/pallas_call | solution.py:30
  3.0 13.7 %all-to-all-start = ((f32[32,64,128]{2,1,0:T(8,128)}), f32[32,64,128]{2,1,0:T(8,128)S(1)}, u32[]{:S(2)}, u32[]{:S(2)}) async-start(f32[32,64,128]{2,1,0:T(8,128)} %get-tuple-element.43), calls=%async_computation | async-start | bytes 2097152 | tf_op jit(solution)/shard_map/all_to_all | solution.py:360
  16.7 2.7 %all-gather.1 = f32[6,128,128]{2,1,0:T(8,128)S(1)} all-gather(f32[3,128,128]{2,1,0:T(8,128)S(1)} %get-tuple-element.45), channel_id=3, replica_groups={{0,1},{2,3},{4,5},{6,7},{8,9},{10,11},{12,13},{14,15},{16,17},{18,19},{..., dimensions={0}, use_global_device_ids=true | all-gather | bytes 589824 | tf_op jit(solution)/shard_map/all_gather | solution.py:264
  19.4 5.1 %collective-permute-start.10 = (f32[2,3,128,128]{3,2,1,0:T(8,128)S(1)}, f32[2,3,128,128]{3,2,1,0:T(8,128)S(1)}, u32[]{:S(2)}, u32[]{:S(2)}) collective-permute-start(f32[2,3,128,128]{3,2,1,0:T(8,128)S(1)} %bitcast.228), channel_id=1, source_target_pairs={{0,2},{1,15},{2,4},{3,1},{4,6},{5,3},{6,8},{7,5},{8,10},{9,7},{10,... | collective-permute-start | bytes 1179656 | tf_op jit(solution)/shard_map/ppermute | solution.py:267
  24.5 4.7 %collective-permute-done.10.refs_1_ = f32[2,3,128,128]{3,2,1,0:T(8,128)S(1)} collective-permute-done((f32[2,3,128,128]{3,2,1,0:T(8,128)S(1)}, f32[2,3,128,128]{3,2,1,0:T(8,128)S(1)}, u32[]{:S(2)}, u32[]{:S(2)}) %collective-permute-start.10) | collective-permute-done | bytes 393248 | tf_op jit(solution)/shard_map/ppermute | solution.py:267
  29.2 5.3 %collective-permute-start.11 = (f32[2,3,128,128]{3,2,1,0:T(8,128)S(1)}, f32[2,3,128,128]{3,2,1,0:T(8,128)S(1)}, u32[]{:S(2)}, u32[]{:S(2)}) collective-permute-start(f32[2,3,128,128]{3,2,1,0:T(8,128)S(1)} %collective-permute-done.10.refs_1_), channel_id=1, source_target_pairs={{0,2},{1,15},{2,4},{3,1},{4,6},{5,3},{6,8},{7,5},{8,10},{9,7},{10,... | collective-permute-start | bytes 1179656 | tf_op jit(solution)/shard_map/ppermute | solution.py:267
  34.5 4.7 %collective-permute-done.11.refs_2_ = f32[2,3,128,128]{3,2,1,0:T(8,128)S(1)} collective-permute-done((f32[2,3,128,128]{3,2,1,0:T(8,128)S(1)}, f32[2,3,128,128]{3,2,1,0:T(8,128)S(1)}, u32[]{:S(2)}, u32[]{:S(2)}) %collective-permute-start.11) | collective-permute-done | bytes 393248 | tf_op jit(solution)/shard_map/ppermute | solution.py:267
  39.2 1.0 pad_maximum_fusion.3
  40.2 4.4 %collective-permute-start.12 = (f32[2,2,3,128,128]{4,3,2,1,0:T(8,128)}, f32[2,2,3,128,128]{4,3,2,1,0:T(8,128)S(1)}, u32[]{:S(2)}, u32[]{:S(2)}) collective-permute-start(f32[2,2,3,128,128]{4,3,2,1,0:T(8,128)} %pad_maximum_fusion.3), channel_id=1, source_target_pairs={{0,1},{1,0},{2,3},{3,2},{4,5},{5,4},{6,7},{7,6},{8,9},{9,8},{10,11... | collective-permute-start | bytes 2359304 | tf_op jit(solution)/shard_map/ppermute | solution.py:269
  44.6 0.0 all-to-all-done.received_ref
  44.6 0.2 shard_map.83
  44.8 20.5 %all-gather = f32[1024,128]{1,0:T(8,128)S(1)} all-gather(f32[64,128]{1,0:T(8,128)S(1)} %shard_map.83), channel_id=2, replica_groups=mesh['tile'=32,'row'=16] {'row'}, dimensions={0}, use_global_device_ids=true | all-gather | bytes 557056 | tf_op jit(solution)/shard_map/all_gather | solution.py:363
  65.3 0.0 collective-permute-done.12.refs_3_
  65.3 2.4 %shard_map.84 = (f32[32,1,1408]{2,1,0:T(1,128)S(1)}, f32[5,64,128]{2,1,0:T(8,128)S(1)}) custom-call(s32[1]{0:T(128)} %bitcast.34.place_ref, f32[16,64,128]{2,1,0:T(8,128)S(1)} %bitcast.227, f32[2,3,128,128]{3,2,1,0:T(8,128)S(1)} %bitcast.229, f32[2,3,128,128]{3,2,1,0:T(8,128)S(1)} %collective-permute-done.10.refs_1_, ...), custom_call_target="tpu_custom_call" | custom-call | tf_op jit(solution)/shard_map/pallas_call | solution.py:30
  67.8 15.1 %all_to_all.15.received_ref = f32[32,1,1408]{2,1,0:T(1,128)S(1)} all-to-all(f32[32,1,1408]{2,1,0:T(1,128)S(1)} %get-tuple-element.46), channel_id=1, replica_groups=mesh['tile'=32,'row'=16] {'tile'}, dimensions={0} | all-to-all | bytes 360448 | tf_op jit(solution)/shard_map/all_to_all | solution.py:366
  82.9 0.1 shard_map.85
  83.0 16.7 %all_to_all.16.received_ref = f32[16,1,1408]{2,1,0:T(1,128)S(1)} all-to-all(f32[16,1,1408]{2,1,0:T(1,128)S(1)} %shard_map.85), channel_id=1, replica_groups=mesh['tile'=32,'row'=16] {'row'}, dimensions={0} | all-to-all | bytes 180224 | tf_op jit(solution)/shard_map/all_to_all | solution.py:368
  99.7 0.0 copy-start
  99.7 1.6 %shard_map.86 = (f32[64,128]{1,0:T(8,128)}, f32[1]{0:T(128)}) custom-call(f32[16,1,1408]{2,1,0:T(1,128)S(1)} %all_to_all.16.received_ref, f32[5,64,128]{2,1,0:T(8,128)S(1)} %get-tuple-element.47.fields_ref), custom_call_target="tpu_custom_call" | custom-call | tf_op jit(solution)/shard_map/pallas_call | solution.py:30
  101.4 0.0 copy-done
  101.4 0.7 while.9
Async XLA Ops:
  3.0 41.6 %all-to-all-start = ((f32[32,64,128]{2,1,0:T(8,128)}), f32[32,64,128]{2,1,0:T(8,128)S(1)}, u32[]{:S(2)}, u32[]{:S(2)}) async-start(f32[32,64,128]{2,1,0:T(8,128)} %get-tuple-element.43), calls=%async_computation | async-start | bytes 2097152 | tf_op jit(solution)/shard_map/all_to_all | solution.py:360
  19.4 9.8 %collective-permute-start.10 = (f32[2,3,128,128]{3,2,1,0:T(8,128)S(1)}, f32[2,3,128,128]{3,2,1,0:T(8,128)S(1)}, u32[]{:S(2)}, u32[]{:S(2)}) collective-permute-start(f32[2,3,128,128]{3,2,1,0:T(8,128)S(1)} %bitcast.228), channel_id=1, source_target_pairs={{0,2},{1,15},{2,4},{3,1},{4,6},{5,3},{6,8},{7,5},{8,10},{9,7},{10,... | collective-permute-start | bytes 1179656 | tf_op jit(solution)/shard_map/ppermute | solution.py:267
  29.2 10.0 %collective-permute-start.11 = (f32[2,3,128,128]{3,2,1,0:T(8,128)S(1)}, f32[2,3,128,128]{3,2,1,0:T(8,128)S(1)}, u32[]{:S(2)}, u32[]{:S(2)}) collective-permute-start(f32[2,3,128,128]{3,2,1,0:T(8,128)S(1)} %collective-permute-done.10.refs_1_), channel_id=1, source_target_pairs={{0,2},{1,15},{2,4},{3,1},{4,6},{5,3},{6,8},{7,5},{8,10},{9,7},{10,... | collective-permute-start | bytes 1179656 | tf_op jit(solution)/shard_map/ppermute | solution.py:267
  40.2 25.2 %collective-permute-start.12 = (f32[2,2,3,128,128]{4,3,2,1,0:T(8,128)}, f32[2,2,3,128,128]{4,3,2,1,0:T(8,128)S(1)}, u32[]{:S(2)}, u32[]{:S(2)}) collective-permute-start(f32[2,2,3,128,128]{4,3,2,1,0:T(8,128)} %pad_maximum_fusion.3), channel_id=1, source_target_pairs={{0,1},{1,0},{2,3},{3,2},{4,5},{5,4},{6,7},{7,6},{8,9},{9,8},{10,11... | collective-permute-start | bytes 2359304 | tf_op jit(solution)/shard_map/ppermute | solution.py:269
  99.7 1.6 %copy-start = (bf16[1,1,3,128,128]{4,3,2,1,0:T(8,128)(2,1)S(1)}, bf16[1,1,3,128,128]{4,3,2,1,0:T(8,128)(2,1)}, u32[]{:S(2)}) copy-start(bf16[1,1,3,128,128]{4,3,2,1,0:T(8,128)(2,1)} %param.15) | copy-start | bytes 294916
